TPU v7x, 32 devices: a whole 2x2x4 slice. The times are simulated.
32 devices in a mesh: dp: 8 (over y, x, core), seq: 4 (over z).
Axes of the slice: x: 2, y: 2, z: 4, core: 2. Of those that a mesh axis runs over, the one named last changes fastest.
Arguments:
- embeddings: bfloat16 [2, 8, 2048, 768], P(None, 'dp', 'seq'), may hold values from -6 to 6
- lengths: int32 [2, 8], P(None, 'dp'), may hold values from 512 to 2048, as said below
- cotangent: bfloat16 [2, 8, 1024, 768], P(None, 'dp', 'seq'), may hold values from -6 to 6
- conv_weight: bfloat16 [5, 768], P(None, ('dp', 'seq')), may hold values from -2.5 to 2.5
- scorer: bfloat16 [768], P(('dp', 'seq')), may hold values from -0.4375 to 0.4375
- gain_attn: bfloat16 [768], P(('dp', 'seq')), may hold values from 0.5 to 1.5
- w_query: bfloat16 [768, 768], P(('dp', 'seq')), may hold values from -0.109375 to 0.109375
- w_key: bfloat16 [768, 768], P(('dp', 'seq')), may hold values from -0.109375 to 0.109375
- w_value: bfloat16 [768, 768], P(('dp', 'seq')), may hold values from -0.21875 to 0.21875
- w_out: bfloat16 [768, 768], P(('dp', 'seq')), may hold values from -0.875 to 0.875
- rel_bias: bfloat16 [32, 12], replicated, may hold values from -4 to 4
- gain_ffn: bfloat16 [768], P(('dp', 'seq')), may hold values from 0.5 to 1.5
- w_gate: bfloat16 [768, 2048], P(('dp', 'seq')), may hold values from -0.21875 to 0.21875
- w_up: bfloat16 [768, 2048], P(('dp', 'seq')), may hold values from -0.21875 to 0.21875
- w_down: bfloat16 [2048, 768], P(('dp', 'seq')), may hold values from -0.125 to 0.125
Outputs:
- blocks: bfloat16 [2, 8, 1024, 768], P(None, 'dp', 'seq')
- embed_grad: float32 [2, 8, 2048, 768], P(None, 'dp', 'seq')
- conv_grad: float32 [5, 768], P(None, ('dp', 'seq'))
- scorer_grad: float32 [768], P(('dp', 'seq'))
- gain_attn_grad: float32 [768], P(('dp', 'seq'))
- query_grad: float32 [768, 768], P(('dp', 'seq'))
- key_grad: float32 [768, 768], P(('dp', 'seq'))
- value_grad: float32 [768, 768], P(('dp', 'seq'))
- out_grad: float32 [768, 768], P(('dp', 'seq'))
- rel_bias_grad: float32 [32, 12], replicated
- gain_ffn_grad: float32 [768], P(('dp', 'seq'))
- gate_grad: float32 [768, 2048], P(('dp', 'seq'))
- up_grad: float32 [768, 2048], P(('dp', 'seq'))
- down_grad: float32 [2048, 768], P(('dp', 'seq'))
Inputs may be any that keep to these rules, and one draw needn't show every extreme that they name: `lengths`: each sequence's live bytes; in every draw one sequence has exactly 2048 and one exactly 512.
All inputs are finite; a program needn't handle non-finite values.
Results may differ from a plain program's by a relative error of at most 0.02.
Values may be sent and summed in bfloat16 or wider, within the bound.
No kernel may reach another device: no remote copies, remote signals or barrier semaphores. Data moves between devices by JAX's collectives and lax.ppermute only.
A program may use at most 256 MiB of HBM per device.

v0:
```python
import jax
import jax.numpy as jnp
from jax import lax
from jax.sharding import PartitionSpec as P

HEADS = 12
HEAD = 64
BUCKETS = 32
KERNEL = 5


norm_eps = 1e-06
highest = lax.Precision.HIGHEST
cut_points = (12, 16, 23, 32, 46, 64, 91)


def padded(x, sides, width):
    for axis, dim in sides:
        devices, length = (lax.axis_size(axis), x.shape[dim])
        up = [(i, (i + 1) % devices) for i in range(devices - 1)]
        down = [(j, i) for i, j in up]
        last = lax.slice_in_dim(x, length - width, length, axis=dim)
        leading = lax.slice_in_dim(x, 0, width, axis=dim)
        before = lax.ppermute(last, axis, up)
        after = lax.ppermute(leading, axis, down)
        x = jnp.concatenate([before, x, after], axis=dim)
    return x


def bucket_of(offset):
    distance = jnp.abs(offset)
    far_bucket = 8 + sum(((distance >= cut_point).astype(jnp.int32) for cut_point in cut_points))
    return jnp.where(distance < 8, distance, far_bucket) + jnp.where(offset > 0, 16, 0)


def bucket_onehot(query_pos, key_pos):
    return (
        bucket_of(key_pos[None, :] - query_pos[:, None])[..., None]
        == jnp.arange(BUCKETS, dtype=jnp.int32)
    ).astype(jnp.float32)


def bias_block(query_pos, key_pos, rel_f32):
    return jnp.einsum("tub,bh->htu", bucket_onehot(query_pos, key_pos), rel_f32, precision=highest)


def rms_scale(values, gain_vec):
    return (
        values * lax.rsqrt(jnp.mean(values * values, axis=-1, keepdims=True) + norm_eps) * gain_vec
    )


def gelu_gate(gate_in, up_in):
    return jax.nn.gelu(gate_in, approximate=True) * up_in


def block_mean(center, block_size):
    shape_now = center.shape
    grouped = center.reshape(
        shape_now[:-2] + (shape_now[-2] // block_size, block_size, shape_now[-1])
    )
    averaged = jnp.mean(grouped, axis=-2, keepdims=True)
    return jnp.broadcast_to(averaged, grouped.shape).reshape(shape_now)


def triple_mean(conv_wide, positions):
    num_cells = positions.shape[0]
    window = [conv_wide[..., offset_cell : offset_cell + num_cells, :] for offset_cell in range(5)]
    leading = window[2] + window[3] + window[4]
    central = window[1] + window[2] + window[3]
    trailing = window[0] + window[1] + window[2]
    remainder = (positions % 3)[:, None]
    return jnp.where(remainder == 0, leading, jnp.where(remainder == 1, central, trailing)) / 3.0


def gbst_forward(wide_bytes, conv_weight, scorer, positions_wide, lengths):
    half_kernel = KERNEL // 2
    rim_width = half_kernel + 2
    num_cells = wide_bytes.shape[-2] - 2 * rim_width
    conv_len = num_cells + 4
    byte_live = ((positions_wide >= 0) & (positions_wide < lengths[..., None])).astype(jnp.float32)[
        ..., None
    ]
    masked = wide_bytes * byte_live
    conv_wide = sum(
        (
            conv_weight[tap_index] * masked[..., tap_index : tap_index + conv_len, :]
            for tap_index in range(KERNEL)
        )
    )
    conv_wide = conv_wide * byte_live[..., half_kernel : half_kernel + conv_len, :]
    center = conv_wide[..., 2 : 2 + num_cells, :]
    center_pos = positions_wide[rim_width : rim_width + num_cells]
    stacked = jnp.stack(
        [center, block_mean(center, 2), triple_mean(conv_wide, center_pos), block_mean(center, 4)],
        axis=0,
    )
    size_logits = jnp.einsum("s...d,d->s...", stacked, scorer, precision=highest)
    size_weights = jax.nn.softmax(size_logits, axis=0)
    mixture = jnp.sum(size_weights[..., None] * stacked, axis=0)
    shape_now = mixture.shape
    return jnp.mean(
        mixture.reshape(shape_now[:-2] + (shape_now[-2] // 2, 2, shape_now[-1])), axis=-2
    )


def score_rows(query_heads, keys_all, pair_bias, key_live):
    raw_scores = (
        jnp.einsum("sthd,suhd->shtu", query_heads, keys_all, preferred_element_type=jnp.float32)
        + pair_bias[None]
    )
    return jnp.where(key_live[:, None, None, :], raw_scores, -1000000000.0)


def return_rims(grad_wide, rim_width):
    inner = grad_wide[:, rim_width:-rim_width]
    rim_terms = jnp.concatenate([grad_wide[:, :rim_width], grad_wide[:, -rim_width:]], axis=1)
    rim_back = padded(rim_terms.astype(jnp.bfloat16), (("seq", 1),), rim_width).astype(
        rim_terms.dtype
    )
    inner = inner.at[:, :rim_width].add(rim_back[:, :rim_width])
    return inner.at[:, -rim_width:].add(rim_back[:, -rim_width:])


def shards(
    embeddings,
    lengths,
    cotangent,
    conv_weight,
    scorer,
    gain_attn,
    w_query,
    w_key,
    w_value,
    w_out,
    rel_bias,
    gain_ffn,
    w_gate,
    w_up,
    w_down,
):
    num_micro, num_seqs, local_bytes, model_width = embeddings.shape
    local_tokens = local_bytes // 2
    seq_count = lax.axis_size("seq")
    seq_index = lax.axis_index("seq")
    rim_width = KERNEL // 2 + 2
    key_count = local_tokens * seq_count
    rel_f32 = rel_bias.astype(jnp.float32)
    token_start = seq_index * local_tokens
    positions_wide = (
        2 * token_start - rim_width + jnp.arange(2 * local_tokens + 2 * rim_width, dtype=jnp.int32)
    )
    query_pos = token_start + jnp.arange(local_tokens, dtype=jnp.int32)
    key_pos = jnp.arange(key_count, dtype=jnp.int32)
    row_block = min(512, local_tokens)
    row_starts = list(range(0, local_tokens, row_block))
    pair_blocks = [bias_block(query_pos, key_pos, rel_f32) for row_first in row_starts]
    score_grads = [
        jnp.zeros((HEADS, row_block, key_count), jnp.float32) for row_first in row_starts
    ]
    blocks_list = []
    embed_list = []
    running = None
    for step_number in range(num_micro):
        forward_weights = (
            lax.all_gather(conv_weight, ("dp", "seq"), axis=1, tiled=True),
            lax.all_gather(scorer, ("dp", "seq"), axis=0, tiled=True),
            lax.all_gather(gain_attn, ("dp", "seq"), axis=0, tiled=True),
            lax.all_gather(w_query, ("dp", "seq"), axis=0, tiled=True),
            lax.all_gather(w_key, ("dp", "seq"), axis=0, tiled=True),
            lax.all_gather(w_value, ("dp", "seq"), axis=0, tiled=True),
            lax.all_gather(w_out, ("dp", "seq"), axis=0, tiled=True),
            lax.all_gather(gain_ffn, ("dp", "seq"), axis=0, tiled=True),
            lax.all_gather(w_gate, ("dp", "seq"), axis=0, tiled=True),
            lax.all_gather(w_up, ("dp", "seq"), axis=0, tiled=True),
            lax.all_gather(w_down, ("dp", "seq"), axis=0, tiled=True),
        )
        (
            conv_full,
            scorer_full,
            gain_one,
            query_full,
            key_full,
            value_full,
            out_full,
            gain_two,
            gate_full,
            up_full,
            down_full,
        ) = forward_weights
        seq_lengths = lengths[step_number]
        wide_bytes = padded(embeddings[step_number], (("seq", 1),), rim_width)

        def pool_local(wide_now, conv_now, scorer_now):
            return gbst_forward(wide_now, conv_now, scorer_now, positions_wide, seq_lengths)

        hidden_in, gbst_pull = jax.vjp(
            pool_local,
            wide_bytes.astype(jnp.float32),
            conv_full.astype(jnp.float32),
            scorer_full.astype(jnp.float32),
        )
        normed, norm_pull = jax.vjp(rms_scale, hidden_in, gain_one.astype(jnp.float32))
        normed_low = normed.astype(jnp.bfloat16)
        queries = jnp.dot(normed_low, query_full, preferred_element_type=jnp.float32).astype(
            jnp.bfloat16
        )
        keys_local = jnp.dot(normed_low, key_full, preferred_element_type=jnp.float32).astype(
            jnp.bfloat16
        )
        values_local = jnp.dot(normed_low, value_full, preferred_element_type=jnp.float32).astype(
            jnp.bfloat16
        )
        pair_all = lax.all_gather(
            jnp.concatenate([keys_local, values_local], axis=-1), "seq", axis=1, tiled=True
        )
        keys_all = pair_all[..., :model_width].reshape(num_seqs, key_count, HEADS, HEAD)
        values_all = pair_all[..., model_width:].reshape(num_seqs, key_count, HEADS, HEAD)
        query_heads = queries.reshape(num_seqs, local_tokens, HEADS, HEAD)
        key_live = 2 * key_pos[None, :] < seq_lengths[:, None]
        maxima = []
        totals = []
        attended_parts = []
        for block_number, row_first in enumerate(row_starts):
            query_block = query_heads
            scores = score_rows(query_block, keys_all, pair_blocks[block_number], key_live)
            row_max = jnp.max(scores, axis=-1, keepdims=True)
            exp_scores = jnp.exp(scores - row_max)
            row_total = jnp.sum(exp_scores, axis=-1, keepdims=True)
            probs_low = (exp_scores / row_total).astype(jnp.bfloat16)
            attended_parts.append(
                jnp.einsum(
                    "shtu,suhd->sthd", probs_low, values_all, preferred_element_type=jnp.float32
                ).astype(jnp.bfloat16)
            )
            maxima.append(row_max)
            totals.append(row_total)
        attended = attended_parts[0].reshape(num_seqs, local_tokens, model_width)
        after_attn = hidden_in + jnp.dot(attended, out_full, preferred_element_type=jnp.float32)
        normed_ffn, ffn_pull = jax.vjp(rms_scale, after_attn, gain_two.astype(jnp.float32))
        normed_ffn_low = normed_ffn.astype(jnp.bfloat16)
        gate_value = jnp.dot(normed_ffn_low, gate_full, preferred_element_type=jnp.float32)
        up_value = jnp.dot(normed_ffn_low, up_full, preferred_element_type=jnp.float32)
        inner_act, gelu_pull = jax.vjp(gelu_gate, gate_value, up_value)
        inner_low = inner_act.astype(jnp.bfloat16)
        block_out = after_attn + jnp.dot(inner_low, down_full, preferred_element_type=jnp.float32)
        blocks_list.append(block_out)
        back_weights = (
            lax.all_gather(w_query, ("dp", "seq"), axis=0, tiled=True),
            lax.all_gather(w_key, ("dp", "seq"), axis=0, tiled=True),
            lax.all_gather(w_value, ("dp", "seq"), axis=0, tiled=True),
            lax.all_gather(w_out, ("dp", "seq"), axis=0, tiled=True),
            lax.all_gather(w_gate, ("dp", "seq"), axis=0, tiled=True),
            lax.all_gather(w_up, ("dp", "seq"), axis=0, tiled=True),
            lax.all_gather(w_down, ("dp", "seq"), axis=0, tiled=True),
        )
        query_back, key_back, value_back, out_back, gate_back, up_back, down_back = back_weights
        seed_low = cotangent[step_number]
        seed_grad = seed_low.astype(jnp.float32)
        down_grad = jnp.einsum(
            "stf,std->fd", inner_low, seed_low, preferred_element_type=jnp.float32
        )
        grad_inner = jnp.einsum(
            "std,fd->stf", seed_low, down_back, preferred_element_type=jnp.float32
        )
        grad_gate, grad_up = gelu_pull(grad_inner)
        grad_gate_low = grad_gate.astype(jnp.bfloat16)
        grad_up_low = grad_up.astype(jnp.bfloat16)
        gate_grad = jnp.einsum(
            "std,stf->df", normed_ffn_low, grad_gate_low, preferred_element_type=jnp.float32
        )
        up_grad = jnp.einsum(
            "std,stf->df", normed_ffn_low, grad_up_low, preferred_element_type=jnp.float32
        )
        grad_normed_ffn = jnp.einsum(
            "stf,df->std", grad_gate_low, gate_back, preferred_element_type=jnp.float32
        ) + jnp.einsum("stf,df->std", grad_up_low, up_back, preferred_element_type=jnp.float32)
        grad_after, gain_ffn_grad = ffn_pull(grad_normed_ffn)
        grad_after = seed_grad + grad_after
        grad_after_low = grad_after.astype(jnp.bfloat16)
        out_grad = jnp.einsum(
            "std,ste->de", attended, grad_after_low, preferred_element_type=jnp.float32
        )
        grad_attended = (
            jnp.einsum("ste,de->std", grad_after_low, out_back, preferred_element_type=jnp.float32)
            .astype(jnp.bfloat16)
            .reshape(num_seqs, local_tokens, HEADS, HEAD)
        )
        key_terms = jnp.zeros((num_seqs, key_count, HEADS, HEAD), jnp.float32)
        value_terms = jnp.zeros((num_seqs, key_count, HEADS, HEAD), jnp.float32)
        query_parts = []
        row_dots = []
        for block_number, row_first in enumerate(row_starts):
            query_block = query_heads
            scores = score_rows(query_block, keys_all, pair_blocks[block_number], key_live)
            attn_full = jnp.exp(scores - maxima[block_number]) / totals[block_number]
            probs_low = attn_full.astype(jnp.bfloat16)
            grad_probs = jnp.einsum(
                "sthd,suhd->shtu", grad_attended, values_all, preferred_element_type=jnp.float32
            )
            weighted = attn_full * grad_probs
            row_dot = jnp.sum(weighted, axis=-1, keepdims=True)
            grad_scores_low = (weighted - attn_full * row_dot).astype(jnp.bfloat16)
            score_grads[block_number] = score_grads[block_number] + jnp.sum(
                grad_scores_low.astype(jnp.float32), axis=0
            )
            query_parts.append(
                jnp.einsum(
                    "shtu,suhd->sthd", grad_scores_low, keys_all, preferred_element_type=jnp.float32
                ).astype(jnp.bfloat16)
            )
            row_dots.append(row_dot)
            key_terms = jnp.einsum(
                "shtu,sthd->suhd", grad_scores_low, query_block, preferred_element_type=jnp.float32
            )
            value_terms = jnp.einsum(
                "shtu,sthd->suhd", probs_low, grad_attended, preferred_element_type=jnp.float32
            )
        grad_queries = query_parts[0].reshape(num_seqs, local_tokens, model_width)
        pair_terms = jnp.concatenate(
            [
                key_terms.reshape(num_seqs, key_count, model_width),
                value_terms.reshape(num_seqs, key_count, model_width),
            ],
            axis=-1,
        )
        pair_grads = lax.psum_scatter(
            pair_terms.astype(jnp.bfloat16), "seq", scatter_dimension=1, tiled=True
        )
        grad_keys_low = pair_grads[..., :model_width]
        grad_values_low = pair_grads[..., model_width:]
        query_grad = jnp.einsum(
            "std,ste->de", normed_low, grad_queries, preferred_element_type=jnp.float32
        )
        key_grad = jnp.einsum(
            "std,ste->de", normed_low, grad_keys_low, preferred_element_type=jnp.float32
        )
        value_grad = jnp.einsum(
            "std,ste->de", normed_low, grad_values_low, preferred_element_type=jnp.float32
        )
        grad_normed = jnp.einsum(
            "ste,de->std", grad_queries, query_back, preferred_element_type=jnp.float32
        )
        grad_normed = grad_normed + jnp.einsum(
            "ste,de->std", grad_keys_low, key_back, preferred_element_type=jnp.float32
        )
        grad_normed = grad_normed + jnp.einsum(
            "ste,de->std", grad_values_low, value_back, preferred_element_type=jnp.float32
        )
        grad_hidden, gain_attn_grad = norm_pull(grad_normed)
        grad_hidden = grad_after + grad_hidden
        grad_wide, conv_grad, scorer_grad = gbst_pull(grad_hidden)
        embed_list.append(return_rims(grad_wide, rim_width))
        owned_now = (
            lax.psum_scatter(conv_grad, ("dp", "seq"), scatter_dimension=1, tiled=True),
            lax.psum_scatter(scorer_grad, ("dp", "seq"), scatter_dimension=0, tiled=True),
            lax.psum_scatter(gain_attn_grad, ("dp", "seq"), scatter_dimension=0, tiled=True),
            lax.psum_scatter(query_grad, ("dp", "seq"), scatter_dimension=0, tiled=True),
            lax.psum_scatter(key_grad, ("dp", "seq"), scatter_dimension=0, tiled=True),
            lax.psum_scatter(value_grad, ("dp", "seq"), scatter_dimension=0, tiled=True),
            lax.psum_scatter(out_grad, ("dp", "seq"), scatter_dimension=0, tiled=True),
            lax.psum_scatter(gain_ffn_grad, ("dp", "seq"), scatter_dimension=0, tiled=True),
            lax.psum_scatter(gate_grad, ("dp", "seq"), scatter_dimension=0, tiled=True),
            lax.psum_scatter(up_grad, ("dp", "seq"), scatter_dimension=0, tiled=True),
            lax.psum_scatter(down_grad, ("dp", "seq"), scatter_dimension=0, tiled=True),
        )
        running = owned_now if running is None else jax.tree.map(jnp.add, running, owned_now)
    bias_terms = sum(
        (
            jnp.einsum(
                "htu,tub->bh",
                score_grads[block_number],
                bucket_onehot(query_pos, key_pos),
                precision=highest,
            )
            for block_number, row_first in enumerate(row_starts)
        )
    )
    bias_total = lax.psum(bias_terms, ("dp", "seq"))
    blocks_out = jnp.stack(blocks_list).astype(jnp.bfloat16)
    embed_out = jnp.stack(embed_list)
    return (
        blocks_out,
        embed_out,
        running[0],
        running[1],
        running[2],
        running[3],
        running[4],
        running[5],
        running[6],
        bias_total,
        running[7],
        running[8],
        running[9],
        running[10],
    )


def solution(mesh):
    return jax.shard_map(
        shards,
        mesh=mesh,
        in_specs=(
            P(None, "dp", "seq", None),
            P(None, "dp"),
            P(None, "dp", "seq", None),
            P(None, ("dp", "seq")),
            P(("dp", "seq")),
            P(("dp", "seq")),
            P(("dp", "seq"), None),
            P(("dp", "seq"), None),
            P(("dp", "seq"), None),
            P(("dp", "seq"), None),
            P(),
            P(("dp", "seq")),
            P(("dp", "seq"), None),
            P(("dp", "seq"), None),
            P(("dp", "seq"), None),
        ),
        out_specs=(
            P(None, "dp", "seq", None),
            P(None, "dp", "seq", None),
            P(None, ("dp", "seq")),
            P(("dp", "seq")),
            P(("dp", "seq")),
            P(("dp", "seq"), None),
            P(("dp", "seq"), None),
            P(("dp", "seq"), None),
            P(("dp", "seq"), None),
            P(),
            P(("dp", "seq")),
            P(("dp", "seq"), None),
            P(("dp", "seq"), None),
            P(("dp", "seq"), None),
        ),
        check_vma=False,
    )
```

profile of v0, /device:TPU:0, one launch (start us, length us, event | category | flops | bytes accessed | tf_op | source)
XLA Modules:
  0.0 1580.8 jit_solution(1401699054016114566)
XLA Ops:
  23.9 69.0 %all-gather = bf16[32,24,5]{1,2,0:T(8,128)(2,1)S(1)} all-gather(bf16[1,24,5]{1,2,0:T(8,128)(2,1)S(1)} %bitcast.321), channel_id=1, replica_groups=mesh['dp'=8,'seq'=4] {'dp','seq'}, dimensions={0}, use_global_device_ids=true | all-gather | bytes 7920 | tf_op jit(solution)/shard_map/all_gather | solution.py:166
  96.1 37.3 %all-reduce.40 = (bf16[768]{0:T(1024)(128)(2,1)S(1)}, bf16[768]{0:T(1024)(128)(2,1)S(1)}, bf16[768]{0:T(1024)(128)(2,1)}) all-reduce(bf16[768]{0:T(1024)(128)(2,1)S(1)} %dynamic-update-slice.14, bf16[768]{0:T(1024)(128)(2,1)S(1)} %dynamic-update-slice.15, ...), channel_id=1, replica_groups=mesh['dp'=8,'seq'=4] {'dp','seq'}, use_global_device_ids=true, to_apply=%add.32 | all-reduce | flops 2304 | bytes 9216
  187.1 13.0 reshape.2229
  242.8 39.9 %all-gather.15.cloned.1.call-done = bf16[1,1024,1536]{2,1,0:T(8,128)(2,1)} async-done(((bf16[1,256,1536]{2,1,0:T(8,128)(2,1)}), bf16[1,1024,1536]{2,1,0:T(8,128)(2,1)}) %all-gather.15.cloned.1.call-update) | async-done | bytes 3145744 | tf_op jit(solution)/shard_map/all_gather | solution.py:214
  288.2 58.7 %all-gather.27.cloned.1.call-done = bf16[1,1024,1536]{2,1,0:T(8,128)(2,1)} async-done(((bf16[1,256,1536]{2,1,0:T(8,128)(2,1)}), bf16[1,1024,1536]{2,1,0:T(8,128)(2,1)}) %all-gather.27.cloned.1.call-update) | async-done | bytes 3145744 | tf_op jit(solution)/shard_map/all_gather | solution.py:214
  359.0 19.0 %fusion.7 = f32[12,256,1024]{2,1,0:T(8,128)} fusion(f32[256,1024,12]{1,2,0:T(8,128)} %fusion.3, pred[1024]{0:T(1024)(128)(4,1)S(1)} %fusion.132, bf16[256,12,64]{0,2,1:T(8,128)(2,1)S(1)} %bitcast.290, bf16[1024,12,64]{0,2,1:T(8,128)(2,1)S(1)} %bitcast.284), kind=kOutput, calls=%fused_computation.10 | convolution fusion | flops 408944640 | bytes 27132928 | tf_op jit(solution)/shard_map/sthd,suhd->shtu/dot_general | solution.py:109
  378.0 15.3 fusion.160
  393.9 15.1 fusion.61
  412.1 18.9 %fusion.8 = f32[12,256,1024]{2,1,0:T(8,128)} fusion(f32[256,1024,12]{1,2,0:T(8,128)} %fusion.3, pred[1024]{0:T(1024)(128)(4,1)S(1)} %fusion.131, bf16[256,12,64]{0,2,1:T(8,128)(2,1)S(1)} %bitcast.292, bf16[1024,12,64]{0,2,1:T(8,128)(2,1)S(1)} %bitcast.286), kind=kOutput, calls=%fused_computation.11 | convolution fusion | flops 408944640 | bytes 27132928 | tf_op jit(solution)/shard_map/sthd,suhd->shtu/dot_general | solution.py:109
  431.0 15.3 fusion.159
  467.5 56.5 %all-gather.21.cloned.1.call-done = bf16[768,2048]{1,0:T(8,128)(2,1)} async-done(((bf16[24,2048]{1,0:T(8,128)(2,1)}), bf16[768,2048]{1,0:T(8,128)(2,1)}) %all-gather.21.cloned.1.call-update) | async-done | bytes 3145744 | tf_op jit(solution)/shard_map/all_gather | solution.py:174
  528.3 56.6 %all-gather.25.cloned.1.call-done = bf16[2048,768]{1,0:T(8,128)(2,1)} async-done(((bf16[64,768]{1,0:T(8,128)(2,1)}), bf16[2048,768]{1,0:T(8,128)(2,1)}) %all-gather.25.cloned.1.call-update) | async-done | bytes 3145744 | tf_op jit(solution)/shard_map/all_gather | solution.py:176
  610.4 15.2 fusion.42
  645.3 24.0 %convert_add_fusion = (f32[12,256,1024]{2,1,0:T(8,128)}, bf16[12,256,1024]{2,1,0:T(8,128)(2,1)}, bf16[12,256,1024]{2,1,0:T(8,128)(2,1)S(1)}) fusion(f32[12,256,1024]{2,1,0:T(8,128)} %get-tuple-element.189, f32[12,256]{1,0:T(8,128)S(1)} %get-tuple-element.188, f32[12,256,1024]{2,1,0:T(8,128)} %get-tuple-element.181, f32[12,256]{1,0:T(8,128)S(1)} %copy-done.125, ...), kind=kLoop, calls=%fused_computation.12 | loop fusion | flops 34603008 | bytes 75546624 | tf_op jit(solution)/shard_map/add | solution.py:304
  674.1 15.0 fusion.39
  745.2 25.6 %fusion.75 = f32[32,12]{0,1:T(8,128)} fusion(f32[12,256,1024]{2,1,0:T(8,128)} %get-tuple-element.95, s32[256,1024]{1,0:T(8,128)S(1)} %copy-done.50), kind=kOutput, calls=%fused_computation.164 | convolution fusion | flops 1216348160 | bytes 13633024 | tf_op jit(solution)/shard_map/htu,tub->bh/dot_general | solution.py:370
  774.3 21.6 %reduce-scatter.11.cloned.1.call-done = bf16[1,256,1536]{1,2,0:T(8,128)(2,1)} async-done(((bf16[1,1024,1536]{1,2,0:T(8,128)(2,1)}), bf16[1,256,1536]{1,2,0:T(8,128)(2,1)}) %reduce-scatter.11.cloned.1.call-update) | async-done | bytes 786448 | tf_op jit(solution)/shard_map/reduce_scatter | solution.py:327
  924.5 43.8 %all-reduce.39 = (f32[5,768]{1,0:T(8,128)S(1)}, f32[768]{0:T(1024)S(1)}, f32[768]{0:T(1024)S(1)}, f32[32,12]{0,1:T(8,128)}, f32[768]{0:T(1024)S(1)}) all-reduce(f32[5,768]{1,0:T(8,128)S(1)} %add_add_fusion.4, f32[768]{0:T(1024)S(1)} %add.546, f32[768]{0:T(1024)S(1)} %add.547, ...), channel_id=15, replica_groups=mesh['dp'=8,'seq'=4] {'dp','seq'}, use_global_device_ids=true, to_apply=%region_41.42.clone | all-reduce | flops 6528 | bytes 52224
  973.1 32.3 %reduce-scatter.15.cloned.1.call-done = f32[24,768]{1,0:T(8,128)} async-done(((f32[768,768]{1,0:T(8,128)}), f32[24,768]{1,0:T(8,128)}) %reduce-scatter.15.cloned.1.call-update) | async-done | bytes 73744 | tf_op jit(solution)/shard_map/reduce_scatter | solution.py:358
  1005.4 119.7 %reduce-scatter.27.cloned.1.call-done = f32[64,768]{1,0:T(8,128)} async-done(((f32[2048,768]{1,0:T(8,128)}), f32[64,768]{1,0:T(8,128)}) %reduce-scatter.27.cloned.1.call-update) | async-done | bytes 196624 | tf_op jit(solution)/shard_map/reduce_scatter | solution.py:365
  1125.1 120.5 %reduce-scatter.23.cloned.1.call-done = f32[24,2048]{1,0:T(8,128)} async-done(((f32[768,2048]{1,0:T(8,128)}), f32[24,2048]{1,0:T(8,128)}) %reduce-scatter.23.cloned.1.call-update) | async-done | bytes 196624 | tf_op jit(solution)/shard_map/reduce_scatter | solution.py:363
  1245.6 119.6 %reduce-scatter.25.cloned.1.call-done = f32[24,2048]{1,0:T(8,128)} async-done(((f32[768,2048]{1,0:T(8,128)}), f32[24,2048]{1,0:T(8,128)}) %reduce-scatter.25.cloned.1.call-update) | async-done | bytes 196624 | tf_op jit(solution)/shard_map/reduce_scatter | solution.py:364
  1365.2 104.9 %reduce-scatter.19.cloned.1.call-done = f32[24,768]{1,0:T(8,128)} async-done(((f32[768,768]{1,0:T(8,128)}), f32[24,768]{1,0:T(8,128)}) %reduce-scatter.19.cloned.1.call-update) | async-done | bytes 73744 | tf_op jit(solution)/shard_map/reduce_scatter | solution.py:360
  1470.1 103.7 %reduce-scatter.17.cloned.1.call-done = f32[24,768]{1,0:T(8,128)} async-done(((f32[768,768]{1,0:T(8,128)}), f32[24,768]{1,0:T(8,128)}) %reduce-scatter.17.cloned.1.call-update) | async-done | bytes 73744 | tf_op jit(solution)/shard_map/reduce_scatter | solution.py:359
  (670 shorter events, 403.0 us)
Async XLA Ops:
  7.2 206.7 %all-gather.13.cloned.1.call-start = ((), (), s32[]{:S(2)}) async-start(), calls=%async_computation.10 | async-start | bytes 1216512 | tf_op jit(solution)/shard_map/all_gather | solution.py:171
  7.9 208.1 %all-gather.11.cloned.1.call-start = ((), (), s32[]{:S(2)}) async-start(), calls=%async_computation.9 | async-start | bytes 1216512 | tf_op jit(solution)/shard_map/all_gather | solution.py:170
  8.7 228.1 %all-gather.17.cloned.1.call-start = ((), (), s32[]{:S(2)}) async-start(), calls=%async_computation.12 | async-start | bytes 1216512 | tf_op jit(solution)/shard_map/all_gather | solution.py:169
  10.3 123.5 %collective-permute-start.2 = (bf16[1,4,768]{2,1,0:T(4,128)(2,1)S(1)}, bf16[1,4,768]{2,1,0:T(4,128)(2,1)S(1)}, u32[]{:S(2)}, u32[]{:S(2)}) collective-permute-start(bf16[1,4,768]{2,1,0:T(4,128)(2,1)S(1)} %get-tuple-element.150), channel_id=1, source_target_pairs={{0,1},{1,2},{2,3},{4,5},{5,6},{6,7},{8,9},{9,10},{10,11},{12,13},{... | collective-permute-start | bytes 18440 | tf_op jit(solution)/shard_map/ppermute | solution.py:24
  15.2 118.5 %collective-permute-start.3 = (bf16[1,4,768]{2,1,0:T(4,128)(2,1)S(1)}, bf16[1,4,768]{2,1,0:T(4,128)(2,1)S(1)}, u32[]{:S(2)}, u32[]{:S(2)}) collective-permute-start(bf16[1,4,768]{2,1,0:T(4,128)(2,1)S(1)} %get-tuple-element.151), channel_id=1, source_target_pairs={{1,0},{2,1},{3,2},{5,4},{6,5},{7,6},{9,8},{10,9},{11,10},{13,12},{... | collective-permute-start | bytes 18440 | tf_op jit(solution)/shard_map/ppermute | solution.py:25
  16.5 116.9 %collective-permute-start = (bf16[1,4,768]{2,1,0:T(4,128)(2,1)S(1)}, bf16[1,4,768]{2,1,0:T(4,128)(2,1)S(1)}, u32[]{:S(2)}, u32[]{:S(2)}) collective-permute-start(bf16[1,4,768]{2,1,0:T(4,128)(2,1)S(1)} %get-tuple-element.148), channel_id=1, source_target_pairs={{0,1},{1,2},{2,3},{4,5},{5,6},{6,7},{8,9},{9,10},{10,11},{12,13},{... | collective-permute-start | bytes 18440 | tf_op jit(solution)/shard_map/ppermute | solution.py:24
  21.1 112.4 %collective-permute-start.1 = (bf16[1,4,768]{2,1,0:T(4,128)(2,1)S(1)}, bf16[1,4,768]{2,1,0:T(4,128)(2,1)S(1)}, u32[]{:S(2)}, u32[]{:S(2)}) collective-permute-start(bf16[1,4,768]{2,1,0:T(4,128)(2,1)S(1)} %get-tuple-element.149), channel_id=1, source_target_pairs={{1,0},{2,1},{3,2},{5,4},{6,5},{7,6},{9,8},{10,9},{11,10},{13,12},{... | collective-permute-start | bytes 18440 | tf_op jit(solution)/shard_map/ppermute | solution.py:25
  22.4 260.4 %all-gather.15.cloned.1.call-start = ((), (), s32[]{:S(2)}) async-start(), calls=%async_computation.11 | async-start | bytes 3932160 | tf_op jit(solution)/shard_map/all_gather | solution.py:214
  218.8 128.2 %all-gather.27.cloned.1.call-start = ((), (), s32[]{:S(2)}) async-start(), calls=%async_computation.17 | async-start | bytes 3932160 | tf_op jit(solution)/shard_map/all_gather | solution.py:214
  222.1 187.0 %all-gather.19.cloned.1.call-start = ((), (), s32[]{:S(2)}) async-start(), calls=%async_computation.13 | async-start | bytes 1216512 | tf_op jit(solution)/shard_map/all_gather | solution.py:172
  222.7 240.6 %all-gather.23.cloned.1.call-start = ((), (), s32[]{:S(2)}) async-start(), calls=%async_computation.15 | async-start | bytes 3244032 | tf_op jit(solution)/shard_map/all_gather | solution.py:175
  223.4 300.6 %all-gather.21.cloned.1.call-start = ((), (), s32[]{:S(2)}) async-start(), calls=%async_computation.14 | async-start | bytes 3244032 | tf_op jit(solution)/shard_map/all_gather | solution.py:174
  224.2 360.7 %all-gather.25.cloned.1.call-start = ((), (), s32[]{:S(2)}) async-start(), calls=%async_computation.16 | async-start | bytes 3244032 | tf_op jit(solution)/shard_map/all_gather | solution.py:176
  224.9 545.9 %reduce-scatter.13.cloned.1.call-start = ((), (), s32[]{:S(2)}) async-start(), calls=%async_computation.19 | async-start | bytes 3932160 | tf_op jit(solution)/shard_map/reduce_scatter | solution.py:327
  674.0 121.8 %reduce-scatter.11.cloned.1.call-start = ((), (), s32[]{:S(2)}) async-start(), calls=%async_computation.18 | async-start | bytes 3932160 | tf_op jit(solution)/shard_map/reduce_scatter | solution.py:327
  695.3 277.8 %reduce-scatter.21.cloned.1.call-start = ((), (), s32[]{:S(2)}) async-start(), calls=%async_computation.23 | async-start | bytes 2433024 | tf_op jit(solution)/shard_map/reduce_scatter | solution.py:361
  699.5 305.9 %reduce-scatter.15.cloned.1.call-start = ((), (), s32[]{:S(2)}) async-start(), calls=%async_computation.20 | async-start | bytes 2433024 | tf_op jit(solution)/shard_map/reduce_scatter | solution.py:358
  714.6 410.4 %reduce-scatter.27.cloned.1.call-start = ((), (), s32[]{:S(2)}) async-start(), calls=%async_computation.26 | async-start | bytes 6488064 | tf_op jit(solution)/shard_map/reduce_scatter | solution.py:365
  721.0 524.6 %reduce-scatter.23.cloned.1.call-start = ((), (), s32[]{:S(2)}) async-start(), calls=%async_computation.24 | async-start | bytes 6488064 | tf_op jit(solution)/shard_map/reduce_scatter | solution.py:363
  727.1 638.0 %reduce-scatter.25.cloned.1.call-start = ((), (), s32[]{:S(2)}) async-start(), calls=%async_computation.25 | async-start | bytes 6488064 | tf_op jit(solution)/shard_map/reduce_scatter | solution.py:364
  733.2 736.9 %reduce-scatter.19.cloned.1.call-start = ((), (), s32[]{:S(2)}) async-start(), calls=%async_computation.22 | async-start | bytes 2433024 | tf_op jit(solution)/shard_map/reduce_scatter | solution.py:360
  822.7 751.1 %reduce-scatter.17.cloned.1.call-start = ((), (), s32[]{:S(2)}) async-start(), calls=%async_computation.21 | async-start | bytes 2433024 | tf_op jit(solution)/shard_map/reduce_scatter | solution.py:359
  906.7 64.2 %collective-permute-start.6 = (bf16[1,4,768]{2,1,0:T(4,128)(2,1)S(1)}, bf16[1,4,768]{2,1,0:T(4,128)(2,1)S(1)}, u32[]{:S(2)}, u32[]{:S(2)}) collective-permute-start(bf16[1,4,768]{2,1,0:T(4,128)(2,1)S(1)} %get-tuple-element.131), channel_id=1, source_target_pairs={{0,1},{1,2},{2,3},{4,5},{5,6},{6,7},{8,9},{9,10},{10,11},{12,13},{... | collective-permute-start | bytes 18440 | tf_op jit(solution)/shard_map/ppermute | solution.py:24
  909.7 61.2 %collective-permute-start.7 = (bf16[1,4,768]{2,1,0:T(4,128)(2,1)S(1)}, bf16[1,4,768]{2,1,0:T(4,128)(2,1)S(1)}, u32[]{:S(2)}, u32[]{:S(2)}) collective-permute-start(bf16[1,4,768]{2,1,0:T(4,128)(2,1)S(1)} %get-tuple-element.132), channel_id=1, source_target_pairs={{1,0},{2,1},{3,2},{5,4},{6,5},{7,6},{9,8},{10,9},{11,10},{13,12},{... | collective-permute-start | bytes 18440 | tf_op jit(solution)/shard_map/ppermute | solution.py:25
  (196 other events, 3490.2 us)
Sparse Core Ops, SparseCore 0:
  10.8 56.7 all-gather.12
  70.5 53.2 all-gather.10
  126.6 52.9 all-gather.16
  218.9 63.8 all-gather.14
  284.7 62.1 all-gather.26
  349.6 52.7 all-gather.18
  405.2 57.9 all-gather.22
  466.2 57.8 all-gather.20
  527.0 57.8 all-gather.24
  674.1 59.0 reduce-scatter.12
  735.5 60.2 reduce-scatter.10
  801.6 99.0 reduce-scatter.20
  907.3 98.0 reduce-scatter.14
  1011.5 113.5 reduce-scatter.26
  1132.0 113.4 reduce-scatter.22
  1251.6 113.4 reduce-scatter.24
  1371.7 98.2 reduce-scatter.18
  1475.8 97.9 reduce-scatter.16
where the time goes:
time: 1590 us; the launch traced here: 1580 us
  waiting for transfers between devices  840 us (53%)
  matrix products  260 us (16%)
  other arithmetic  155 us (10%)
  blocking collectives  150 us (9%)
  local copies, waits for them, and re-layouts  135 us (8%)
  starting transfers between devices  23.4 us (1%)
  between operations  17.3 us (1%)
    reduce_scatter x1, waiting for transfers between devices, shards(): lax.psum_scatter(gate_grad, ('dp', 'seq'), scatter_dimension=0, tiled=True)  121 us
    reduce_scatter x1, waiting for transfers between devices, shards(): lax.psum_scatter(down_grad, ('dp', 'seq'), scatter_dimension=0, tiled=True)  120 us
    reduce_scatter x1, waiting for transfers between devices, shards(): lax.psum_scatter(up_grad, ('dp', 'seq'), scatter_dimension=0, tiled=True)  120 us
    reduce_scatter x1, waiting for transfers between devices, shards(): lax.psum_scatter(value_grad, ('dp', 'seq'), scatter_dimension=0, tiled=True)  105 us
    reduce_scatter x1, waiting for transfers between devices, shards(): lax.psum_scatter(key_grad, ('dp', 'seq'), scatter_dimension=0, tiled=True)  104 us
    all_gather x2, waiting for transfers between devices, shards(): lax.all_gather(jnp.concatenate([keys_local, values_local], axis=-1), 'seq...  98.7 us
    unnamed x2, blocking collectives  81.2 us
    all_gather x1, blocking collectives, shards(): lax.all_gather(conv_weight, ('dp', 'seq'), axis=1, tiled=True)  69 us
  transfers between devices with their start and end apart: 26, of which 12 were waited for; matrix products, arithmetic and copies ran while one was open for 28% of the time, Pallas kernels for 0%

commit v1 on v0

v1 whole, which is shorter than its diff:
```python
import jax
import jax.numpy as jnp
from jax import lax
from jax.experimental import pallas as pl
from jax.experimental.pallas import tpu as pltpu
from jax.sharding import PartitionSpec as P

HEADS = 12
HEAD = 64
BUCKETS = 32
KERNEL = 5


norm_eps = 1e-06
highest = lax.Precision.HIGHEST
cut_points = (12, 16, 23, 32, 46, 64, 91)


def neighbour_edges(x, width):
    devices, length = (lax.axis_size("seq"), x.shape[1])
    up = [(i, i + 1) for i in range(devices - 1)]
    down = [(j, i) for i, j in up]
    before = lax.ppermute(x[:, length - width :], "seq", up)
    after = lax.ppermute(x[:, :width], "seq", down)
    return before, after


def bucket_of(offset):
    distance = jnp.abs(offset)
    far_bucket = 8 + sum(((distance >= cut_point).astype(jnp.int32) for cut_point in cut_points))
    return jnp.where(distance < 8, distance, far_bucket) + jnp.where(offset > 0, 16, 0)


def rms_scale(values, gain_vec):
    return (
        values * lax.rsqrt(jnp.mean(values * values, axis=-1, keepdims=True) + norm_eps) * gain_vec
    )


def gelu_gate(gate_in, up_in):
    return jax.nn.gelu(gate_in, approximate=True) * up_in


EDGE = 8
LANES = 128


def shifted(x, step):
    return pltpu.roll(x, (-step) % x.shape[0], 0)


def byte_facts(token_start, length, rows):
    token = token_start - EDGE + lax.broadcasted_iota(jnp.int32, (rows, LANES), 0)
    first = 2 * token
    even_live = jnp.where((first >= 0) & (first < length), 1.0, 0.0)
    odd_live = jnp.where((first + 1 >= 0) & (first + 1 < length), 1.0, 0.0)
    remainder = lax.rem(first + 6 * EDGE, 3)
    odd_token = lax.rem(token + 2 * EDGE, 2) == 1
    return even_live, odd_live, remainder, odd_token


def pooled_scalars(six, remainder, odd_token):
    even_b, odd_b, even, odd, even_a, odd_a = six
    pair = even + odd
    quad = pair + jnp.where(odd_token, even_b + odd_b, even_a + odd_a)
    shared = pair + jnp.where(remainder == 0, even_a, odd_b)
    split = remainder == 2
    triple_even = jnp.where(split, even_b + odd_b + even, shared)
    triple_odd = jnp.where(split, odd + even_a + odd_a, shared)
    third = 1.0 / 3.0
    return (
        (even, 0.5 * pair, third * triple_even, 0.25 * quad),
        (odd, 0.5 * pair, third * triple_odd, 0.25 * quad),
    )


def spread_scalars(even, odd, remainder, odd_token):
    third = 1.0 / 3.0
    pair = 0.5 * (even[1] + odd[1])
    quad = 0.25 * (even[3] + odd[3])
    both = third * (even[2] + odd[2])
    only_even = third * even[2]
    only_odd = third * odd[2]
    split = remainder == 2
    zero = jnp.zeros_like(pair)
    quad_b = jnp.where(odd_token, quad, zero)
    quad_a = jnp.where(odd_token, zero, quad)
    even_here = even[0] + pair + quad + jnp.where(split, only_even, both)
    odd_here = odd[0] + pair + quad + jnp.where(split, only_odd, both)
    even_b = quad_b + jnp.where(split, only_even, zero)
    odd_b = quad_b + jnp.where(split, only_even, jnp.where(remainder == 1, both, zero))
    even_a = quad_a + jnp.where(split, only_odd, jnp.where(remainder == 0, both, zero))
    odd_a = quad_a + jnp.where(split, only_odd, zero)
    return even_b, odd_b, even_here, odd_here, even_a, odd_a


def softmax_of(logits):
    top = jnp.maximum(jnp.maximum(logits[0], logits[1]), jnp.maximum(logits[2], logits[3]))
    parts = [jnp.exp(logit - top) for logit in logits]
    total = (parts[0] + parts[1]) + (parts[2] + parts[3])
    return [part / total for part in parts]


def lane_sum(x):
    return jnp.broadcast_to(jnp.sum(x, axis=1, keepdims=True), x.shape)


def byte_windows(ref, rows, lanes):
    return [ref[EDGE + step : EDGE + step + rows, lanes] for step in (-1, 0, 1)]


def load_bytes(before_ref, body_ref, after_ref, wide_ref):
    edge = 2 * EDGE
    size = body_ref.shape[1]
    for number in range(body_ref.shape[2] // LANES):
        lanes = slice(number * LANES, (number + 1) * LANES)
        wide_ref[number, :edge] = before_ref[0, :, lanes].astype(jnp.float32)
        wide_ref[number, edge : edge + size] = body_ref[0, :, lanes].astype(jnp.float32)
        wide_ref[number, edge + size :] = after_ref[0, :, lanes].astype(jnp.float32)


def conv_chunk(wide_ref, xe_ref, xo_ref, ce_ref, co_ref, vec_ref, facts, number):
    lanes = chunk_lanes(number)
    rows = facts[0].shape[0]
    main = slice(EDGE, EDGE + rows)
    xe_ref[main, lanes] = wide_ref[number, pl.ds(0, rows, stride=2)] * facts[0]
    xo_ref[main, lanes] = wide_ref[number, pl.ds(1, rows, stride=2)] * facts[1]
    even_b, even, even_a = byte_windows(xe_ref, rows, lanes)
    odd_b, odd, odd_a = byte_windows(xo_ref, rows, lanes)
    taps = [vec_ref[j : j + 1, lanes] for j in range(KERNEL)]
    conv_even = (
        taps[0] * even_b + taps[1] * odd_b + taps[2] * even + taps[3] * odd + taps[4] * even_a
    )
    conv_odd = (
        taps[0] * odd_b + taps[1] * even + taps[2] * odd + taps[3] * even_a + taps[4] * odd_a
    )
    ce_ref[main, lanes] = conv_even * facts[0]
    co_ref[main, lanes] = conv_odd * facts[1]


def clear_edges(refs, rows):
    for ref in refs:
        zeros = jnp.zeros((EDGE, ref.shape[1]), jnp.float32)
        ref[:EDGE] = zeros
        ref[EDGE + rows :] = zeros


def chunk_lanes(number):
    return pl.ds(pl.multiple_of(number * LANES, LANES), LANES)


def size_weights(logit_ref, remainder, odd_token):
    even = lane_sum(logit_ref[0])
    odd = lane_sum(logit_ref[1])
    six = (shifted(even, -1), shifted(odd, -1), even, odd, shifted(even, 1), shifted(odd, 1))
    logits_even, logits_odd = pooled_scalars(six, remainder, odd_token)
    return softmax_of(logits_even), softmax_of(logits_odd)


def pool_forward_kernel(
    info_ref,
    before_ref,
    body_ref,
    after_ref,
    vec_ref,
    out_ref,
    wide_ref,
    xe_ref,
    xo_ref,
    ce_ref,
    co_ref,
    logit_ref,
    coef_ref,
    square_ref,
):
    piece = pl.program_id(0)
    width = body_ref.shape[2]
    tokens = body_ref.shape[1] // 2
    rows = tokens + 2 * EDGE
    chunks = width // LANES
    facts = byte_facts(info_ref[0], info_ref[1 + piece], rows)
    load_bytes(before_ref, body_ref, after_ref, wide_ref)
    clear_edges((xe_ref, xo_ref, ce_ref, co_ref), rows)
    logit_ref[...] = jnp.zeros_like(logit_ref)
    main = slice(EDGE, EDGE + rows)

    def first_pass(number, carry):
        lanes = chunk_lanes(number)
        conv_chunk(wide_ref, xe_ref, xo_ref, ce_ref, co_ref, vec_ref, facts, number)
        scorer = vec_ref[KERNEL : KERNEL + 1, lanes]
        logit_ref[0] = logit_ref[0] + ce_ref[main, lanes] * scorer
        logit_ref[1] = logit_ref[1] + co_ref[main, lanes] * scorer
        return carry

    lax.fori_loop(0, chunks, first_pass, 0)
    remainder, odd_token = facts[2:]
    even, odd = size_weights(logit_ref, remainder, odd_token)
    spread = spread_scalars(even, odd, remainder, odd_token)
    for k in range(6):
        coef_ref[k] = 0.5 * spread[k][EDGE : EDGE + tokens]
    square_ref[...] = jnp.zeros_like(square_ref)

    def second_pass(number, carry):
        lanes = chunk_lanes(number)
        total = None
        for step in range(3):
            start = 2 * EDGE + step - 1
            for parity, ref in ((0, ce_ref), (1, co_ref)):
                term = coef_ref[2 * step + parity] * ref[start : start + tokens, lanes]
                total = term if total is None else total + term
        xe_ref[:tokens, lanes] = total
        square_ref[...] = square_ref[...] + total * total
        return carry

    lax.fori_loop(0, chunks, second_pass, 0)
    scale = lax.rsqrt(lane_sum(square_ref[...]) * (1.0 / width) + norm_eps)
    square_ref[...] = scale

    def third_pass(number, carry):
        lanes = chunk_lanes(number)
        gain = vec_ref[KERNEL + 1 : KERNEL + 2, lanes]
        out_ref[0, :tokens, lanes] = (
            xe_ref[:tokens, lanes] * square_ref[...] * gain
        ).astype(jnp.bfloat16)
        return carry

    lax.fori_loop(0, chunks, third_pass, 0)
    row = jnp.transpose(scale)[: 2 * EDGE]
    top = row.astype(jnp.bfloat16).astype(jnp.float32)
    line = lax.broadcasted_iota(jnp.int32, row.shape, 0)
    tail = jnp.where(line == 0, top, jnp.where(line == 1, row - top, 0.0)).astype(jnp.bfloat16)
    rest = jnp.zeros((2 * EDGE, width - tokens), jnp.bfloat16)
    out_ref[0, tokens:] = jnp.concatenate([tail, rest], axis=1)


def pool_forward(info, before, body, after, vectors):
    count, size, width = body.shape
    tokens = size // 2
    rows = tokens + 2 * EDGE
    assert tokens % LANES == 0 and tokens < width
    wide = pltpu.VMEM((width // LANES, size + 4 * EDGE, LANES), jnp.float32)
    tall = pltpu.VMEM((rows + 2 * EDGE, width), jnp.float32)
    edge = pl.BlockSpec((1, 2 * EDGE, width), lambda p, _: (p, 0, 0))
    return pl.pallas_call(
        pool_forward_kernel,
        name="pool_forward",
        grid_spec=pltpu.PrefetchScalarGridSpec(
            num_scalar_prefetch=1,
            grid=(count,),
            in_specs=[
                edge,
                pl.BlockSpec((1, size, width), lambda p, _: (p, 0, 0)),
                edge,
                pl.BlockSpec((8, width), lambda p, _: (0, 0)),
            ],
            out_specs=pl.BlockSpec((1, tokens + 2 * EDGE, width), lambda p, _: (p, 0, 0)),
            scratch_shapes=[
                wide,
                tall,
                tall,
                tall,
                tall,
                pltpu.VMEM((2, rows, LANES), jnp.float32),
                pltpu.VMEM((6, tokens, LANES), jnp.float32),
                pltpu.VMEM((tokens, LANES), jnp.float32),
            ],
        ),
        out_shape=jax.ShapeDtypeStruct((count, tokens + 2 * EDGE, width), jnp.bfloat16),
        compiler_params=pltpu.CompilerParams(vmem_limit_bytes=48 << 20),
    )(info, before, body, after, vectors)


def pool_backward_kernel(
    info_ref,
    before_ref,
    body_ref,
    after_ref,
    grad_before_ref,
    grad_ref,
    grad_after_ref,
    vec_ref,
    embed_ref,
    small_ref,
    wide_ref,
    xe_ref,
    xo_ref,
    ce_ref,
    co_ref,
    dh_ref,
    de_ref,
    do_ref,
    logit_ref,
    dots_ref,
    coef_ref,
    pair_ref,
):
    piece = pl.program_id(0)
    width = body_ref.shape[2]
    tokens = body_ref.shape[1] // 2
    rows = tokens + 2 * EDGE
    chunks = width // LANES
    f32 = jnp.float32
    facts = byte_facts(info_ref[0], info_ref[1 + piece], rows)
    load_bytes(before_ref, body_ref, after_ref, wide_ref)
    clear_edges((xe_ref, xo_ref, ce_ref, co_ref, dh_ref, de_ref, do_ref), rows)
    dh_ref[EDGE : 2 * EDGE] = grad_before_ref[0].astype(f32)
    dh_ref[2 * EDGE : 2 * EDGE + tokens] = grad_ref[0].astype(f32)
    dh_ref[2 * EDGE + tokens : 3 * EDGE + tokens] = grad_after_ref[0].astype(f32)
    logit_ref[...] = jnp.zeros_like(logit_ref)
    dots_ref[...] = jnp.zeros_like(dots_ref)
    main = slice(EDGE, EDGE + rows)

    def first_pass(number, carry):
        lanes = chunk_lanes(number)
        conv_chunk(wide_ref, xe_ref, xo_ref, ce_ref, co_ref, vec_ref, facts, number)
        scorer = vec_ref[KERNEL : KERNEL + 1, lanes]
        logit_ref[0] = logit_ref[0] + ce_ref[main, lanes] * scorer
        logit_ref[1] = logit_ref[1] + co_ref[main, lanes] * scorer
        grad = dh_ref[main, lanes]
        for step in range(3):
            start = EDGE + step - 1
            for parity, ref in ((0, ce_ref), (1, co_ref)):
                k = 2 * step + parity
                dots_ref[k] = dots_ref[k] + grad * ref[start : start + rows, lanes]
        return carry

    lax.fori_loop(0, chunks, first_pass, 0)
    remainder, odd_token = facts[2:]
    even, odd = size_weights(logit_ref, remainder, odd_token)
    six = [0.5 * lane_sum(dots_ref[k]) for k in range(6)]
    grads_even, grads_odd = pooled_scalars(six, remainder, odd_token)

    def logit_grads(weights, grads):
        mean = (weights[0] * grads[0] + weights[1] * grads[1]) + (
            weights[2] * grads[2] + weights[3] * grads[3]
        )
        return [weight * (grad - mean) for weight, grad in zip(weights, grads)]

    spread = spread_scalars(even, odd, remainder, odd_token)
    steer = spread_scalars(
        logit_grads(even, grads_even), logit_grads(odd, grads_odd), remainder, odd_token
    )
    for k in range(6):
        step = k // 2 - 1
        coef_ref[k] = 0.5 * shifted(spread[k], -step)
    coef_ref[6] = steer[2] + shifted(steer[4], -1) + shifted(steer[0], 1)
    coef_ref[7] = steer[3] + shifted(steer[5], -1) + shifted(steer[1], 1)

    def second_pass(number, carry):
        lanes = chunk_lanes(number)
        scorer = vec_ref[KERNEL : KERNEL + 1, lanes]
        grad_b, grad, grad_a = byte_windows(dh_ref, rows, lanes)
        for parity, live, ref in ((0, facts[0], de_ref), (1, facts[1], do_ref)):
            total = (
                coef_ref[parity] * grad_a
                + coef_ref[2 + parity] * grad
                + coef_ref[4 + parity] * grad_b
                + coef_ref[6 + parity] * scorer
            )
            ref[main, lanes] = total * live
        own = slice(2 * EDGE, 2 * EDGE + tokens)
        before = slice(2 * EDGE - 1, 2 * EDGE - 1 + tokens)
        after = slice(2 * EDGE + 1, 2 * EDGE + 1 + tokens)
        taps = [vec_ref[j : j + 1, lanes] for j in range(KERNEL)]
        even_b, even, even_a = [de_ref[part, lanes] for part in (before, own, after)]
        odd_b, odd, odd_a = [do_ref[part, lanes] for part in (before, own, after)]
        inner = slice(EDGE, EDGE + tokens)
        pair_ref[pl.ds(0, tokens, stride=2)] = facts[0][inner] * (
            taps[0] * even_a + taps[1] * odd + taps[2] * even + taps[3] * odd_b + taps[4] * even_b
        )
        pair_ref[pl.ds(1, tokens, stride=2)] = facts[1][inner] * (
            taps[0] * odd_a + taps[1] * even_a + taps[2] * odd + taps[3] * even + taps[4] * odd_b
        )
        embed_ref[0, :, lanes] = pair_ref[...]
        x_even = [xe_ref[part, lanes] for part in (before, own, after)]
        x_odd = [xo_ref[part, lanes] for part in (before, own, after)]
        terms = [
            even * x_even[0] + odd * x_odd[0],
            even * x_odd[0] + odd * x_even[1],
            even * x_even[1] + odd * x_odd[1],
            even * x_odd[1] + odd * x_even[2],
            even * x_even[2] + odd * x_odd[2],
            coef_ref[6, inner] * ce_ref[own, lanes] + coef_ref[7, inner] * co_ref[own, lanes],
        ]
        sums = [jnp.sum(term, axis=0, keepdims=True) for term in terms]
        sums = sums + [jnp.zeros_like(sums[0])] * (8 - len(sums))
        small_ref[0, :, lanes] = jnp.concatenate(sums, axis=0)
        return carry

    lax.fori_loop(0, chunks, second_pass, 0)


def pool_backward(info, before, body, after, grad_before, grad, grad_after, vectors):
    count, size, width = body.shape
    tokens = size // 2
    rows = tokens + 2 * EDGE
    wide = pltpu.VMEM((width // LANES, size + 4 * EDGE, LANES), jnp.float32)
    tall = pltpu.VMEM((rows + 2 * EDGE, width), jnp.float32)
    edge = pl.BlockSpec((1, 2 * EDGE, width), lambda p, _: (p, 0, 0))
    grad_edge = pl.BlockSpec((1, EDGE, width), lambda p, _: (p, 0, 0))
    return pl.pallas_call(
        pool_backward_kernel,
        name="pool_backward",
        grid_spec=pltpu.PrefetchScalarGridSpec(
            num_scalar_prefetch=1,
            grid=(count,),
            in_specs=[
                edge,
                pl.BlockSpec((1, size, width), lambda p, _: (p, 0, 0)),
                edge,
                grad_edge,
                pl.BlockSpec((1, tokens, width), lambda p, _: (p, 0, 0)),
                grad_edge,
                pl.BlockSpec((8, width), lambda p, _: (0, 0)),
            ],
            out_specs=[
                pl.BlockSpec((1, size, width), lambda p, _: (p, 0, 0)),
                pl.BlockSpec((1, 8, width), lambda p, _: (p, 0, 0)),
            ],
            scratch_shapes=[wide]
            + [tall] * 7
            + [
                pltpu.VMEM((2, rows, LANES), jnp.float32),
                pltpu.VMEM((6, rows, LANES), jnp.float32),
                pltpu.VMEM((8, rows, LANES), jnp.float32),
                pltpu.VMEM((size, LANES), jnp.float32),
            ],
        ),
        out_shape=[
            jax.ShapeDtypeStruct((count, size, width), jnp.float32),
            jax.ShapeDtypeStruct((count, 8, width), jnp.float32),
        ],
        compiler_params=pltpu.CompilerParams(vmem_limit_bytes=56 << 20),
    )(info, before, body, after, grad_before, grad, grad_after, vectors)


def bits_of(axis):
    size = lax.axis_size(axis)
    count = size.bit_length() - 1
    assert 1 << count == size
    return count


def stage_orders():
    dp_bits, seq_bits = (bits_of("dp"), bits_of("seq"))
    along_seq = [("seq", bit) for bit in reversed(range(seq_bits))]
    across = [("dp", bit) for bit in range(1, dp_bits)]
    cores = [("dp", 0)]
    return (along_seq + across[::-1] + cores, along_seq + across + cores)


def place_of(axis, bit):
    dp_bits, seq_bits = (bits_of("dp"), bits_of("seq"))
    return dp_bits - 1 - bit if axis == "dp" else dp_bits + seq_bits - 1 - bit


def swap_bit(x, axis, bit):
    size = lax.axis_size(axis)
    return lax.ppermute(x, axis, [(i, i ^ (1 << bit)) for i in range(size)])


def own_bit(axis, bit):
    return (lax.axis_index(axis) >> bit) & 1


def gather_all(x, order):
    held = []
    whole = x
    for axis, bit in order:
        place = place_of(axis, bit)
        dim = sum(other < place for other in held)
        arrived = swap_bit(whole, axis, bit)
        upper = own_bit(axis, bit) == 1
        whole = jnp.stack(
            [jnp.where(upper, arrived, whole), jnp.where(upper, whole, arrived)], axis=dim
        )
        held.append(place)
    return whole.reshape((1 << len(order),) + x.shape)


def scatter_sum(blocks, order):
    shape = blocks.shape[1:]
    part = blocks.reshape((2,) * len(order) + shape)
    held = list(range(len(order)))
    for number, (axis, bit) in enumerate(order[::-1]):
        place = place_of(axis, bit)
        dim = held.index(place)
        held.remove(place)
        mine = own_bit(axis, bit)
        leaving = lax.dynamic_index_in_dim(part, 1 - mine, dim, keepdims=False)
        staying = lax.dynamic_index_in_dim(part, mine, dim, keepdims=False)
        arrived = swap_bit(leaving.astype(jnp.bfloat16), axis, bit)
        part = staying.astype(jnp.float32) + arrived.astype(jnp.float32)
        if number < len(order) - 1:
            part = part.astype(jnp.bfloat16)
    return part


def sum_all(x, order):
    for axis, bit in order[::-1]:
        x = x + swap_bit(x, axis, bit)
    return x


def to_chips(pieces):
    count = pieces.shape[0]
    dp_size, seq_size = (lax.axis_size("dp"), lax.axis_size("seq"))
    seq_index = lax.axis_index("seq")
    arrived = []
    for phase in range(count):
        pairs = chip_pairs(dp_size, seq_size, count, phase)
        leaving = lax.dynamic_index_in_dim(pieces, (seq_index + phase) % count, 0, keepdims=False)
        arrived.append(lax.ppermute(leaving, ("dp", "seq"), pairs))
    stacked = jnp.stack(arrived)
    number = seq_index % count
    return jnp.concatenate(
        [
            lax.dynamic_index_in_dim(stacked, (number - r) % count, 0, keepdims=False)
            for r in range(count)
        ],
        axis=0,
    )


def from_chips(tokens, count):
    dp_size, seq_size = (lax.axis_size("dp"), lax.axis_size("seq"))
    seq_index = lax.axis_index("seq")
    number = seq_index % count
    split = tokens.reshape((count, tokens.shape[0] // count) + tokens.shape[1:])
    arrived = []
    for phase in range(count):
        pairs = [(j, i) for i, j in chip_pairs(dp_size, seq_size, count, phase)]
        leaving = lax.dynamic_index_in_dim(split, (number - phase) % count, 0, keepdims=False)
        arrived.append(lax.ppermute(leaving, ("dp", "seq"), pairs))
    stacked = jnp.stack(arrived)
    return jnp.stack(
        [
            lax.dynamic_index_in_dim(stacked, (j - seq_index) % count, 0, keepdims=False)
            for j in range(count)
        ]
    )


def chip_pairs(dp_size, seq_size, count, phase):
    pairs = []
    for dp in range(dp_size):
        for seq in range(seq_size):
            core_to = seq // count
            seq_to = dp % 2 * count + (seq + phase) % count
            pairs.append((dp * seq_size + seq, (dp // 2 * 2 + core_to) * seq_size + seq_to))
    return pairs


TILE = 128
AUG = 16


def mm(a, b):
    return jnp.dot(a, b, preferred_element_type=jnp.float32)


def mm_nt(a, b):
    return lax.dot_general(a, b, (((1,), (1,)), ((), ())), preferred_element_type=jnp.float32)


def mm_tn(a, b):
    return lax.dot_general(a, b, (((0,), (0,)), ((), ())), preferred_element_type=jnp.float32)


def one_head(pair_rows, a):
    zeros = jnp.zeros((HEAD, pair_rows.shape[1]), pair_rows.dtype)
    half = pair_rows[a * HEAD : (a + 1) * HEAD]
    return jnp.concatenate([half, zeros] if a == 0 else [zeros, half], axis=0)


def near_rows(first_tile, i, d):
    return pl.ds(pl.multiple_of((first_tile + (i + d)) * TILE, TILE), TILE)


def split_rows(base, row):
    low, f32 = (jnp.bfloat16, jnp.float32)
    top = row.astype(low).astype(f32)
    middle = (row - top).astype(low).astype(f32)
    bottom = row - top - middle
    line = lax.broadcasted_iota(jnp.int32, base.shape, 0)
    return jnp.where(
        line == 9, -top, jnp.where(line == 10, -middle, jnp.where(line == 11, -bottom, base))
    ).astype(low)


def attn_forward_kernel(
    first_ref, q_ref, k_ref, ka_ref, v_ref, far_ref, bias_ref, out_ref, lse_ref, s_ref
):
    keys = k_ref.shape[0]
    tokens = q_ref.shape[1]
    lhs = jnp.concatenate([k_ref[...], ka_ref[...]], axis=1)
    pad = jnp.zeros((TILE - AUG, tokens), jnp.bfloat16)
    first = first_ref[0]
    for a in range(2):
        rhs = jnp.concatenate([one_head(q_ref[...], a), far_ref[a], pad], axis=0)
        s_ref[TILE : TILE + keys] = mm(lhs, rhs)
        for i in range(tokens // TILE):
            for d in range(3):
                rows = near_rows(first, i, d)
                lanes = slice(i * TILE, (i + 1) * TILE)
                s_ref[rows, lanes] = s_ref[rows, lanes] + bias_ref[a, d]
        s = s_ref[TILE : TILE + keys]
        row_max = jnp.max(s, axis=0, keepdims=True)
        probs = jnp.exp(s - row_max).astype(jnp.bfloat16)
        v_rows = jnp.concatenate(
            [v_ref[a * HEAD : (a + 1) * HEAD], jnp.ones((AUG, keys), jnp.bfloat16)], axis=0
        )
        both = mm(v_rows, probs)
        total = both[HEAD : HEAD + 1]
        out_ref[a * HEAD : (a + 1) * HEAD] = (both[:HEAD] / total).astype(jnp.bfloat16)
        lse_ref[0, a : a + 1] = row_max + jnp.log(total)


def attn_forward(first, q_t, keys, key_aug, v_t, far, bias):
    width, tokens = q_t.shape
    key_count = keys.shape[0]
    pairs = width // TILE
    return pl.pallas_call(
        attn_forward_kernel,
        name="attn_forward",
        grid_spec=pltpu.PrefetchScalarGridSpec(
            num_scalar_prefetch=1,
            grid=(pairs,),
            in_specs=[
                pl.BlockSpec((TILE, tokens), lambda h, _: (h, 0)),
                pl.BlockSpec((key_count, TILE), lambda h, _: (0, h)),
                pl.BlockSpec((key_count, TILE), lambda h, _: (0, 0)),
                pl.BlockSpec((TILE, key_count), lambda h, _: (h, 0)),
                pl.BlockSpec((2, AUG, tokens), lambda h, _: (h, 0, 0)),
                pl.BlockSpec((2, 3, TILE, TILE), lambda h, _: (h, 0, 0, 0)),
            ],
            out_specs=[
                pl.BlockSpec((TILE, tokens), lambda h, _: (h, 0)),
                pl.BlockSpec((1, 2, tokens), lambda h, _: (h, 0, 0)),
            ],
            scratch_shapes=[pltpu.VMEM((key_count + 2 * TILE, tokens), jnp.float32)],
        ),
        out_shape=[
            jax.ShapeDtypeStruct((width, tokens), jnp.bfloat16),
            jax.ShapeDtypeStruct((pairs, 2, tokens), jnp.float32),
        ],
        compiler_params=pltpu.CompilerParams(vmem_limit_bytes=48 << 20),
    )(first, q_t, keys, key_aug, v_t, far, bias)


def attn_backward_kernel(
    first_ref,
    q_ref,
    do_ref,
    out_ref,
    lse_ref,
    k_ref,
    v_ref,
    kt_ref,
    ka_ref,
    block_ref,
    far_ref,
    bias_ref,
    dq_ref,
    dk_ref,
    dv_ref,
    near_ref,
    sums_ref,
    s_ref,
    ds_ref,
    p_ref,
):
    keys = k_ref.shape[0]
    tokens = q_ref.shape[1]
    f32, low = (jnp.float32, jnp.bfloat16)
    first = first_ref[0]
    main = slice(TILE, TILE + keys)
    k_lhs = jnp.concatenate([k_ref[...], ka_ref[...]], axis=1)
    v_lhs = jnp.concatenate([v_ref[...], ka_ref[...]], axis=1)
    pad = jnp.zeros((TILE - AUG, tokens), low)
    edge = jnp.zeros((TILE, tokens), low)
    q_heads = [one_head(q_ref[...], a) for a in range(2)]
    do_heads = [one_head(do_ref[...], a) for a in range(2)]
    for a in range(2):
        head = slice(a * HEAD, (a + 1) * HEAD)
        aug = split_rows(far_ref[a].astype(f32), lse_ref[0, a : a + 1])
        s_ref[main] = mm(k_lhs, jnp.concatenate([q_heads[a], aug, pad], axis=0))
        for i in range(tokens // TILE):
            for d in range(3):
                rows = near_rows(first, i, d)
                lanes = slice(i * TILE, (i + 1) * TILE)
                s_ref[rows, lanes] = s_ref[rows, lanes] + bias_ref[a, d]
        probs = jnp.exp(s_ref[main])
        p_ref[a] = probs.astype(low)
        row_dot = jnp.sum(
            do_ref[head].astype(f32) * out_ref[head].astype(f32), axis=0, keepdims=True
        )
        aug = split_rows(jnp.zeros((AUG, tokens), f32), row_dot)
        grad_probs = mm(v_lhs, jnp.concatenate([do_heads[a], aug, pad], axis=0))
        ds_ref[a, main] = (probs * grad_probs).astype(low)
        ds_ref[a, :TILE] = edge
        ds_ref[a, TILE + keys :] = edge
        left = jnp.concatenate([kt_ref[head], block_ref[...]], axis=0)
        both = mm(left, ds_ref[a, main])
        dq_ref[head] = both[:HEAD].astype(low)
        sums_ref[0, a] = both[HEAD:]
        for d in range(3):
            total = None
            for i in range(tokens // TILE):
                rows = near_rows(first, i, d)
                term = ds_ref[a, rows, i * TILE : (i + 1) * TILE].astype(f32)
                total = term if total is None else total + term
            near_ref[a, d] = total
    dk_ref[...] = mm_nt(
        jnp.concatenate([ds_ref[0, main], ds_ref[1, main]], axis=1),
        jnp.concatenate(q_heads, axis=1),
    ).astype(low)
    dv_ref[...] = mm_nt(
        jnp.concatenate([p_ref[0], p_ref[1]], axis=1), jnp.concatenate(do_heads, axis=1)
    ).astype(low)


def attn_backward(first, q_t, do_t, out_t, lse, keys, values, k_t, key_aug, block_rows, far, bias):
    width, tokens = q_t.shape
    key_count = keys.shape[0]
    pairs = width // TILE
    across = pl.BlockSpec((TILE, tokens), lambda h, _: (h, 0))
    along = pl.BlockSpec((key_count, TILE), lambda h, _: (0, h))
    return pl.pallas_call(
        attn_backward_kernel,
        name="attn_backward",
        grid_spec=pltpu.PrefetchScalarGridSpec(
            num_scalar_prefetch=1,
            grid=(pairs,),
            in_specs=[
                across,
                across,
                across,
                pl.BlockSpec((1, 2, tokens), lambda h, _: (h, 0, 0)),
                along,
                along,
                pl.BlockSpec((TILE, key_count), lambda h, _: (h, 0)),
                pl.BlockSpec((key_count, TILE), lambda h, _: (0, 0)),
                pl.BlockSpec((AUG, key_count), lambda h, _: (0, 0)),
                pl.BlockSpec((2, AUG, tokens), lambda h, _: (h, 0, 0)),
                pl.BlockSpec((2, 3, TILE, TILE), lambda h, _: (h, 0, 0, 0)),
            ],
            out_specs=[
                across,
                along,
                along,
                pl.BlockSpec((2, 3, TILE, TILE), lambda h, _: (h, 0, 0, 0)),
                pl.BlockSpec((1, 2, AUG, tokens), lambda h, _: (h, 0, 0, 0)),
            ],
            scratch_shapes=[
                pltpu.VMEM((key_count + 2 * TILE, tokens), jnp.float32),
                pltpu.VMEM((2, key_count + 2 * TILE, tokens), jnp.bfloat16),
                pltpu.VMEM((2, key_count, tokens), jnp.bfloat16),
            ],
        ),
        out_shape=[
            jax.ShapeDtypeStruct((width, tokens), jnp.bfloat16),
            jax.ShapeDtypeStruct((key_count, width), jnp.bfloat16),
            jax.ShapeDtypeStruct((key_count, width), jnp.bfloat16),
            jax.ShapeDtypeStruct((2 * pairs, 3, TILE, TILE), jnp.float32),
            jax.ShapeDtypeStruct((pairs, 2, AUG, tokens), jnp.float32),
        ],
        compiler_params=pltpu.CompilerParams(vmem_limit_bytes=56 << 20),
    )(first, q_t, do_t, out_t, lse, keys, values, k_t, key_aug, block_rows, far, bias)


def attn_tables(first, tokens, key_count, length, rel_bias):
    low, f32 = (jnp.bfloat16, jnp.float32)
    blocks = key_count // TILE
    assert blocks <= 8
    key_pos = jnp.arange(key_count, dtype=jnp.int32)
    column = jnp.arange(TILE, dtype=jnp.int32)[None, :]
    key_aug = jnp.where(column == (key_pos // TILE)[:, None], 1.0, 0.0)
    dead = jnp.where(2 * key_pos < length, 0.0, -1000000000.0)[:, None]
    key_aug = jnp.where(column == 8, dead, key_aug)
    key_aug = jnp.where((column >= 9) & (column < 12), 1.0, key_aug).astype(low)
    line = jnp.arange(AUG, dtype=jnp.int32)
    block_rows = jnp.where(line[:, None] == (key_pos // TILE)[None, :], 1.0, 0.0).astype(low)
    tile = first + jnp.arange(tokens, dtype=jnp.int32) // TILE
    apart = (line[:, None] - tile[None, :])[None]
    rel_t = rel_bias.astype(f32).T
    before = rel_t[:, BUCKETS // 2 - 1][:, None, None]
    after = rel_t[:, BUCKETS - 1][:, None, None]
    far = jnp.where(apart <= -2, before, jnp.where(apart >= 2, after, 0.0))
    in_use = (line < blocks)[None, :, None]
    far = jnp.where(in_use, far, jnp.where((line == 8)[None, :, None], 1.0, 0.0)).astype(low)
    bias = jnp.einsum("djib,bh->hdji", near_onehot(), rel_bias.astype(f32), precision=highest)
    return key_aug, block_rows, far, bias


def near_onehot():
    step = jnp.arange(TILE, dtype=jnp.int32)
    offset = (
        TILE * (jnp.arange(3, dtype=jnp.int32) - 1)[:, None, None]
        + step[None, :, None]
        - step[None, None, :]
    )
    return (bucket_of(offset)[..., None] == jnp.arange(BUCKETS, dtype=jnp.int32)).astype(
        jnp.float32
    )


def bias_gradient(first, near, sums):
    pairs, _, _, tokens = sums.shape
    close = jnp.einsum("hdji,djib->bh", near, near_onehot(), precision=highest)
    line = jnp.arange(AUG, dtype=jnp.int32)[:, None]
    tile = first + jnp.arange(tokens, dtype=jnp.int32)[None, :] // TILE
    apart = line - tile
    sums = sums.reshape(2 * pairs, AUG, tokens)
    before = jnp.sum(jnp.where(apart <= -2, sums, 0.0), axis=(1, 2))
    after = jnp.sum(jnp.where(apart >= 2, sums, 0.0), axis=(1, 2))
    bucket = jnp.arange(BUCKETS, dtype=jnp.int32)[:, None]
    return (
        close
        + jnp.where(bucket == BUCKETS // 2 - 1, before[None, :], 0.0)
        + jnp.where(bucket == BUCKETS - 1, after[None, :], 0.0)
    )


def shards(
    embeddings,
    lengths,
    cotangent,
    conv_weight,
    scorer,
    gain_attn,
    w_query,
    w_key,
    w_value,
    w_out,
    rel_bias,
    gain_ffn,
    w_gate,
    w_up,
    w_down,
):
    num_micro, num_seqs, local_bytes, model_width = embeddings.shape
    piece_tokens = local_bytes // 2
    count = num_micro * num_seqs
    seq_count = lax.axis_size("seq")
    assert seq_count == 2 * count
    seq_index = lax.axis_index("seq")
    core = lax.axis_index("dp") % 2
    device = lax.axis_index("dp") * seq_count + seq_index
    local_tokens = count * piece_tokens
    key_count = 2 * local_tokens
    low, f32 = (jnp.bfloat16, jnp.float32)
    order_a, order_b = stage_orders()
    rows = w_query.shape[0]
    vec_rows = KERNEL + 3

    vectors = jnp.concatenate(
        [conv_weight, scorer[None], gain_attn[None], gain_ffn[None]], axis=0
    )
    vectors = gather_all(vectors, order_a)
    vectors = jnp.swapaxes(vectors, 0, 1).reshape(vec_rows, model_width).astype(f32)
    gain_one, gain_two = (vectors[KERNEL + 1], vectors[KERNEL + 2])

    pieces = embeddings.reshape(count, local_bytes, model_width)
    piece_lengths = lengths.reshape(count)
    bytes_before, bytes_after = neighbour_edges(pieces, 2 * EDGE)
    token_start = seq_index * piece_tokens
    info = jnp.concatenate([token_start.reshape(1).astype(jnp.int32), piece_lengths])
    both_lengths = swap_bit(piece_lengths, "dp", 0)
    both_lengths = jnp.where(
        core == seq_index // count, piece_lengths, both_lengths
    )
    seq_length = lax.dynamic_index_in_dim(both_lengths, seq_index % count, 0, keepdims=False)

    sent = pool_forward(info, bytes_before, pieces, bytes_after, vectors)
    arrived = to_chips(sent).reshape(count, piece_tokens + 2 * EDGE, model_width)
    normed_low = arrived[:, :piece_tokens].reshape(local_tokens, model_width)
    scale = arrived[:, piece_tokens : piece_tokens + 2, :piece_tokens].astype(f32)
    scale = jnp.sum(scale, axis=1).reshape(local_tokens, 1)
    unit = normed_low.astype(f32) / gain_one
    hidden_in = unit / scale
    seed_low = to_chips(cotangent.reshape(count, piece_tokens, model_width))
    seed_grad = seed_low.astype(f32)

    first = gather_all(jnp.concatenate([w_query, w_key], axis=1), order_a)
    second = gather_all(jnp.concatenate([w_value, w_out], axis=1), order_b)
    gate_full = gather_all(w_gate, order_a).reshape(model_width, -1)
    up_full = gather_all(w_up, order_b).reshape(model_width, -1)
    down_full = gather_all(w_down, order_a).reshape(-1, model_width)
    first = first.reshape(model_width, 2 * model_width)
    second = second.reshape(model_width, 2 * model_width)
    query_full, key_full = (first[:, :model_width], first[:, model_width:])
    value_full, out_full = (second[:, :model_width], second[:, model_width:])

    normed_other = swap_bit(normed_low, "dp", 0)
    normed_all = jnp.concatenate(
        [
            jnp.where(core == 0, normed_low, normed_other),
            jnp.where(core == 0, normed_other, normed_low),
        ],
        axis=0,
    )

    first_tile = core * (local_tokens // TILE)
    key_aug, block_rows, far, bias = attn_tables(
        first_tile, local_tokens, key_count, seq_length, rel_bias
    )
    first_ref = first_tile.astype(jnp.int32).reshape(1)

    def project_t(weight, tokens):
        return lax.dot_general(
            weight, tokens, (((0,), (1,)), ((), ())), preferred_element_type=f32
        ).astype(low)

    q_t = project_t(query_full, normed_low)
    k_t = project_t(key_full, normed_all)
    v_t = project_t(value_full, normed_all)
    keys_all = mm(normed_all, key_full).astype(low)
    values_all = mm(normed_all, value_full).astype(low)
    attended_t, lse = attn_forward(first_ref, q_t, keys_all, key_aug, v_t, far, bias)
    after_attn = hidden_in + mm_tn(attended_t, out_full)
    normed_ffn, ffn_pull = jax.vjp(rms_scale, after_attn, gain_two)
    normed_ffn_low = normed_ffn.astype(low)
    gate_value = mm(normed_ffn_low, gate_full)
    up_value = mm(normed_ffn_low, up_full)
    inner_act, gelu_pull = jax.vjp(gelu_gate, gate_value, up_value)
    inner_low = inner_act.astype(low)
    block_out = (after_attn + mm(inner_low, down_full)).astype(low)
    blocks_out = from_chips(block_out, count).reshape(
        num_micro, num_seqs, piece_tokens, model_width
    )

    down_grad = mm_tn(inner_low, seed_low).astype(low)
    down_grad = scatter_sum(down_grad.reshape(-1, w_down.shape[0], model_width), order_b)
    grad_inner = mm_nt(seed_low, down_full)
    grad_gate, grad_up = gelu_pull(grad_inner)
    grad_gate_low = grad_gate.astype(low)
    grad_up_low = grad_up.astype(low)
    gate_grad = mm_tn(normed_ffn_low, grad_gate_low).astype(low)
    gate_grad = scatter_sum(gate_grad.reshape(-1, rows, w_gate.shape[1]), order_a)
    up_grad = mm_tn(normed_ffn_low, grad_up_low).astype(low)
    up_grad = scatter_sum(up_grad.reshape(-1, rows, w_up.shape[1]), order_b)
    grad_normed_ffn = mm_nt(grad_gate_low, gate_full) + mm_nt(grad_up_low, up_full)
    grad_after, gain_ffn_grad = ffn_pull(grad_normed_ffn)
    grad_after = seed_grad + grad_after
    grad_after_low = grad_after.astype(low)
    out_grad = mm(attended_t, grad_after_low).astype(low)
    out_grad = scatter_sum(out_grad.reshape(-1, rows, model_width), order_a)
    grad_attended_t = mm_nt(out_full, grad_after_low).astype(low)
    grad_queries_t, key_terms, value_terms, near, sums = attn_backward(
        first_ref,
        q_t,
        grad_attended_t,
        attended_t,
        lse,
        keys_all,
        values_all,
        k_t,
        key_aug,
        block_rows,
        far,
        bias,
    )
    shared = mm_nt(key_terms, key_full) + mm_nt(value_terms, value_full)
    shared = shared.reshape(2, local_tokens, model_width)
    leaving = lax.dynamic_index_in_dim(shared, 1 - core, 0, keepdims=False).astype(low)
    staying = lax.dynamic_index_in_dim(shared, core, 0, keepdims=False)
    grad_normed = lax.dot_general(
        grad_queries_t, query_full, (((0,), (1,)), ((), ())), preferred_element_type=f32
    ) + staying + swap_bit(leaving, "dp", 0).astype(f32)
    query_grad = lax.dot_general(
        normed_low, grad_queries_t, (((0,), (1,)), ((), ())), preferred_element_type=f32
    ).astype(low)
    query_grad = scatter_sum(query_grad.reshape(-1, rows, model_width), order_b)
    key_grad = mm_tn(normed_all, key_terms).astype(low)
    key_grad = scatter_sum(key_grad.reshape(-1, rows, model_width), order_a)
    value_grad = mm_tn(normed_all, value_terms).astype(low)
    value_grad = scatter_sum(value_grad.reshape(-1, rows, model_width), order_b)
    gained = grad_normed * gain_one
    gain_attn_grad = jnp.sum(grad_normed * unit, axis=0)
    grad_hidden = grad_after + scale * (
        gained - unit * jnp.mean(gained * unit, axis=-1, keepdims=True)
    )
    grad_pieces = from_chips(grad_hidden.astype(low), count)
    grad_before, grad_after_edge = neighbour_edges(grad_pieces, EDGE)
    embed_grad, pool_small = pool_backward(
        info, bytes_before, pieces, bytes_after, grad_before, grad_pieces, grad_after_edge, vectors
    )
    embed_out = embed_grad.reshape(num_micro, num_seqs, local_bytes, model_width)
    pool_small = jnp.sum(pool_small, axis=0)[: KERNEL + 1]
    bias_terms = bias_gradient(first_tile, near, sums)
    bias_row = jnp.pad(bias_terms.reshape(-1), (0, model_width - bias_terms.size))
    small = jnp.concatenate(
        [pool_small, gain_attn_grad[None], gain_ffn_grad[None], bias_row[None]],
        axis=0,
    )
    small = sum_all(small, order_a)
    bias_total = small[vec_rows, : bias_terms.size].reshape(bias_terms.shape)
    own = lax.dynamic_slice_in_dim(small[:vec_rows], device * rows, rows, axis=1)
    return (
        blocks_out,
        embed_out,
        own[:KERNEL],
        own[KERNEL],
        own[KERNEL + 1],
        query_grad,
        key_grad,
        value_grad,
        out_grad,
        bias_total,
        own[KERNEL + 2],
        gate_grad,
        up_grad,
        down_grad,
    )


def solution(mesh):
    return jax.shard_map(
        shards,
        mesh=mesh,
        in_specs=(
            P(None, "dp", "seq", None),
            P(None, "dp"),
            P(None, "dp", "seq", None),
            P(None, ("dp", "seq")),
            P(("dp", "seq")),
            P(("dp", "seq")),
            P(("dp", "seq"), None),
            P(("dp", "seq"), None),
            P(("dp", "seq"), None),
            P(("dp", "seq"), None),
            P(),
            P(("dp", "seq")),
            P(("dp", "seq"), None),
            P(("dp", "seq"), None),
            P(("dp", "seq"), None),
        ),
        out_specs=(
            P(None, "dp", "seq", None),
            P(None, "dp", "seq", None),
            P(None, ("dp", "seq")),
            P(("dp", "seq")),
            P(("dp", "seq")),
            P(("dp", "seq"), None),
            P(("dp", "seq"), None),
            P(("dp", "seq"), None),
            P(("dp", "seq"), None),
            P(),
            P(("dp", "seq")),
            P(("dp", "seq"), None),
            P(("dp", "seq"), None),
            P(("dp", "seq"), None),
        ),
        check_vma=False,
    )
```

time: 1590 us -> 517 us (0.33)
  waiting for transfers between devices: 840 us -> 188 us
  matrix products: 260 us -> 63.1 us
  blocking collectives: 150 us -> 0 us
  other arithmetic: 155 us -> 47.6 us
  local copies, waits for them, and re-layouts: 135 us -> 44 us
  starting transfers between devices: 23.4 us -> 99.3 us
  Pallas kernels: 0 us -> 65.1 us
    reduce_scatter x9 -> x0, waiting for transfers between devices: 622 us -> none  [the longest x1 121 us: shards(): lax.psum_scatter(gate_grad, ('dp', 'seq'), scatter_dimension=0, tiled=True)]
    all_gather x9 -> x0, waiting for transfers between devices: 214 us -> none  [the longest x2 98.7 us: shards(): lax.all_gather(jnp.concatenate([keys_local, values_local], axis=-1), 'seq...]
    dot_general x60 -> x25, matrix products: 260 us -> 63.1 us  [the longest x6 16.7 us: mm_tn(): lax.dot_general(a, b, (((0,), (0,)), ((), ())), preferred_element_type=jn...]
    ppermute x8 -> x85, waiting for transfers between devices: 0.02 us -> 188 us  [the longest x73 188 us: swap_bit(): return lax.ppermute(x, axis, [(i, i ^ 1 << bit) for i in range(size)])]
    unnamed x2 -> x0, blocking collectives: 81.2 us -> none
    ppermute x8 -> x85, starting transfers between devices: 22.5 us -> 99.3 us  [the longest x73 78.1 us: swap_bit(): return lax.ppermute(x, axis, [(i, i ^ 1 << bit) for i in range(size)])]
    all_gather x1 -> x0, blocking collectives: 69 us -> none  [shards(): lax.all_gather(conv_weight, ('dp', 'seq'), axis=1, tiled=True)]
    pallas_call x0 -> x4, Pallas kernels: none -> 65.1 us  [the longest x1 22.5 us: attn_backward(): pl.pallas_call(attn_backward_kernel, name='attn_backward', grid_spec=pltp...]
  transfers between devices with their start and end apart: 26 -> 85, of which waited for: 12 -> 45; matrix products, arithmetic and copies ran while one was open for 28% -> 20% of each run, Pallas kernels for 0% -> 8%
where the time goes in v1:
time: 517 us; the launch traced here: 511 us
  waiting for transfers between devices  188 us (36%)
  starting transfers between devices  99.3 us (19%)
  Pallas kernels  65.1 us (13%)
  matrix products  63.1 us (12%)
  other arithmetic  47.6 us (9%)
  local copies, waits for them, and re-layouts  44 us (9%)
    ppermute x73, waiting for transfers between devices, swap_bit(): return lax.ppermute(x, axis, [(i, i ^ 1 << bit) for i in range(size)])  188 us
    ppermute x73, starting transfers between devices, swap_bit(): return lax.ppermute(x, axis, [(i, i ^ 1 << bit) for i in range(size)])  78.1 us
    pallas_call x1, Pallas kernels, attn_backward(): pl.pallas_call(attn_backward_kernel, name='attn_backward', grid_spec=pltp...  22.5 us
    pallas_call x1, Pallas kernels, pool_backward(): pl.pallas_call(pool_backward_kernel, name='pool_backward', grid_spec=pltp...  19.9 us
    dot_general x6, matrix products, mm_tn(): lax.dot_general(a, b, (((0,), (0,)), ((), ())), preferred_element_type=jn...  16.7 us
    dot_general x6, matrix products, mm(): return jnp.dot(a, b, preferred_element_type=jnp.float32)  15 us
    pallas_call x1, Pallas kernels, attn_forward(): pl.pallas_call(attn_forward_kernel, name='attn_forward', grid_spec=pltpu....  14.8 us
    another operation x59, other arithmetic, gather_all(): jnp.stack([jnp.where(upper, arrived, whole), jnp.where(upper, whole, arri...  13.6 us
  transfers between devices with their start and end apart: 85, of which 45 were waited for; matrix products, arithmetic and copies ran while one was open for 20% of the time, Pallas kernels for 8%

profile of v1, /device:TPU:0, one launch (start us, length us, event | category | flops | bytes accessed | tf_op | source)
XLA Modules:
  0.0 510.7 jit_solution(4444888352509490824)
XLA Ops:
  2.1 4.9 collective-permute-start
  46.6 7.9 %pool_forward.1 = bf16[2,272,768]{2,1,0:T(8,128)(2,1)S(1)} custom-call(s32[3]{0:T(128)S(1)} %pad_add_fusion.info_ref, bf16[2,16,768]{2,1,0:T(8,128)(2,1)S(1)} %collective-permute-done.before_ref, bf16[2,512,768]{2,1,0:T(8,128)(2,1)S(1)} %bitcast.466, bf16[2,16,768]{2,1,0:T(8,128)(2,1)S(1)} %collective-permute-done.1.after_ref, ...), custom_call_target="tpu_custom_call" | custom-call | tf_op jit(solution)/shard_map/pool_forward/pallas_call | solution.py:244
  54.6 5.1 collective-permute-start.26
  62.3 22.0 %collective-permute-done.26 = bf16[24,2048]{1,0:T(8,128)(2,1)S(1)} collective-permute-done((bf16[24,2048]{1,0:T(8,128)(2,1)S(1)}, bf16[24,2048]{1,0:T(8,128)(2,1)S(1)}, u32[]{:S(2)}, u32[]{:S(2)}) %collective-permute-start.26) | collective-permute-done | bytes 98336 | tf_op jit(solution)/shard_map/ppermute | solution.py:459
  86.5 12.5 %collective-permute-done.10 = bf16[2,24,1536]{2,1,0:T(8,128)(2,1)S(1)} collective-permute-done((bf16[2,24,1536]{2,1,0:T(8,128)(2,1)S(1)}, bf16[2,24,1536]{2,1,0:T(8,128)(2,1)S(1)}, u32[]{:S(2)}, u32[]{:S(2)}) %collective-permute-start.10) | collective-permute-done | bytes 147488 | tf_op jit(solution)/shard_map/ppermute | solution.py:459
  99.1 6.1 %collective-permute-done.17 = bf16[2,24,1536]{2,1,0:T(8,128)(2,1)S(1)} collective-permute-done((bf16[2,24,1536]{2,1,0:T(8,128)(2,1)S(1)}, bf16[2,24,1536]{2,1,0:T(8,128)(2,1)S(1)}, u32[]{:S(2)}, u32[]{:S(2)}) %collective-permute-start.17) | collective-permute-done | bytes 147488 | tf_op jit(solution)/shard_map/ppermute | solution.py:459
  105.6 6.0 %collective-permute-done.27 = bf16[2,24,2048]{2,1,0:T(8,128)(2,1)S(1)} collective-permute-done((bf16[2,24,2048]{2,1,0:T(8,128)(2,1)S(1)}, bf16[2,24,2048]{2,1,0:T(8,128)(2,1)S(1)}, u32[]{:S(2)}, u32[]{:S(2)}) %collective-permute-start.27) | collective-permute-done | bytes 196640 | tf_op jit(solution)/shard_map/ppermute | solution.py:459
  112.2 5.0 collective-permute-done.32
  118.0 4.9 collective-permute-done.22
  150.2 6.7 %collective-permute-done.19 = bf16[2,2,2,24,1536]{4,3,1,2,0:T(8,128)(2,1)S(1)} collective-permute-done((bf16[2,2,2,24,1536]{4,3,1,2,0:T(8,128)(2,1)S(1)}, bf16[2,2,2,24,1536]{4,3,1,2,0:T(8,128)(2,1)S(1)}, u32[]{:S(2)}, u32[]{:S(2)}) %collective-permute-start.19) | collective-permute-done | bytes 589856 | tf_op jit(solution)/shard_map/ppermute | solution.py:459
  157.8 7.5 %collective-permute-done.34 = bf16[2,2,2,64,768]{4,3,2,1,0:T(8,128)(2,1)S(1)} collective-permute-done((bf16[2,2,2,64,768]{4,3,2,1,0:T(8,128)(2,1)S(1)}, bf16[2,2,2,64,768]{4,3,2,1,0:T(8,128)(2,1)S(1)}, u32[]{:S(2)}, u32[]{:S(2)}) %collective-permute-start.34) | collective-permute-done | bytes 786464 | tf_op jit(solution)/shard_map/ppermute | solution.py:459
  171.4 10.6 %collective-permute-done.24 = bf16[2,2,2,24,2048]{4,3,2,1,0:T(8,128)(2,1)S(1)} collective-permute-done((bf16[2,2,2,24,2048]{4,3,2,1,0:T(8,128)(2,1)S(1)}, bf16[2,2,2,24,2048]{4,3,2,1,0:T(8,128)(2,1)S(1)}, u32[]{:S(2)}, u32[]{:S(2)}) %collective-permute-start.24) | collective-permute-done | bytes 786464 | tf_op jit(solution)/shard_map/ppermute | solution.py:459
  188.2 14.8 %attn_forward.1 = (bf16[768,512]{1,0:T(8,128)(2,1)S(1)}, f32[6,2,512]{2,1,0:T(2,128)S(1)}) custom-call(s32[1]{0:T(128)} %bitcast.27.first_ref, bf16[768,512]{1,0:T(8,128)(2,1)S(1)} %convolution_convert_fusion.12.q_ref, bf16[1024,768]{1,0:T(8,128)(2,1)S(1)} %convolution_convert_fusion.6.k_ref, bf16[1024,128]{1,0:T(8,128)(2,1)S(1)} %select_convert_fusion.ka_ref, ...), custom_call_target="tpu_custom_call" | custom-call | tf_op jit(solution)/shard_map/attn_forward/pallas_call | solution.py:623
  221.5 6.6 %fusion.8 = (bf16[512,2048]{1,0:T(8,128)(2,1)S(1)}, bf16[512,2048]{1,0:T(8,128)(2,1)S(1)}, bf16[512,2048]{1,0:T(8,128)(2,1)}) fusion(f32[512,2048]{1,0:T(8,128)S(1)} %fusion.67, f32[512,2048]{1,0:T(8,128)S(1)} %fusion.100, bf16[512,768]{1,0:T(8,128)(2,1)S(1)} %multiply_convert_fusion.2, bf16[768,2048]{1,0:T(8,128)(2,1)S(1)} %bitcast.487), kind=kOutput, calls=%fused_computation.11 | convolution fusion | flops 1637875712 | bytes 18612224 | tf_op jit(solution)/shard_map/dot_general | solution.py:559
  236.2 22.5 %attn_backward.1 = (bf16[768,512]{1,0:T(8,128)(2,1)}, bf16[1024,768]{1,0:T(8,128)(2,1)}, bf16[1024,768]{1,0:T(8,128)(2,1)}, f32[12,3,128,128]{3,2,1,0:T(8,128)}, f32[6,2,16,512]{3,2,1,0:T(8,128)}) custom-call(s32[1]{0:T(128)} %bitcast.27.first_ref, bf16[768,512]{1,0:T(8,128)(2,1)} %copy-done.4, bf16[768,512]{1,0:T(8,128)(2,1)} %convolution_convert_fusion.11.do_ref, ...), custom_call_target="tpu_custom_call" | custom-call | tf_op jit(solution)/shard_map/attn_backward/pallas_call | solution.py:729
  286.8 4.5 collective-permute-start.36
  305.7 5.9 %fusion.26 = f32[32,12]{0,1:T(8,128)} fusion(f32[12,3,128,128]{2,0,3,1:T(8,128)} %copy.68, s32[3,128,128]{1,2,0:T(8,128)} %copy-done.35, f32[12]{0:T(128)S(1)} %broadcast_in_dim.246, f32[12]{0:T(128)S(1)} %broadcast_in_dim.241, pred[32]{0:T(512)(128)(4,1)} %get-tuple-element.180, pred[32]{0:T(512)(128)(4,1)} %get-tuple-element.181), kind=kOutput, calls=%fused_computation.97 | convolution fusion | flops 228066816 | bytes 2557600 | tf_op jit(solution)/shard_map/hdji,djib->bh/dot_general | solution.py:810
  344.4 4.8 collective-permute-done.52
  349.8 5.0 collective-permute-done.57
  360.3 4.8 collective-permute-done.67
  396.0 19.9 %pool_backward.1 = (f32[2,512,768]{2,1,0:T(8,128)}, f32[2,8,768]{2,1,0:T(8,128)}) custom-call(s32[3]{0:T(128)} %copy-done.11, bf16[2,16,768]{2,1,0:T(8,128)(2,1)} %copy-done.8, bf16[2,512,768]{2,1,0:T(8,128)(2,1)} %bitcast.465, bf16[2,16,768]{2,1,0:T(8,128)(2,1)} %copy-done.9, bf16[2,8,768]{2,1,0:T(8,128)(2,1)} %copy-done.62, ...), custom_call_target="tpu_custom_call" | custom-call | tf_op jit(solution)/shard_map/pool_backward/pallas_call | solution.py:401
  450.9 8.8 %collective-permute-done.71 = bf16[2,2,2,24,2048]{4,3,1,2,0:T(8,128)(2,1)S(1)} collective-permute-done((bf16[2,2,2,24,2048]{4,3,1,2,0:T(8,128)(2,1)S(1)}, bf16[2,2,2,24,2048]{4,3,1,2,0:T(8,128)(2,1)S(1)}, u32[]{:S(2)}, u32[]{:S(2)}) %collective-permute-start.71) | collective-permute-done | bytes 786464 | tf_op jit(solution)/shard_map/ppermute | solution.py:459
  460.4 8.3 %collective-permute-done.76 = bf16[2,2,2,24,2048]{4,3,1,2,0:T(8,128)(2,1)S(1)} collective-permute-done((bf16[2,2,2,24,2048]{4,3,1,2,0:T(8,128)(2,1)S(1)}, bf16[2,2,2,24,2048]{4,3,1,2,0:T(8,128)(2,1)S(1)}, u32[]{:S(2)}, u32[]{:S(2)}) %collective-permute-start.76) | collective-permute-done | bytes 786464 | tf_op jit(solution)/shard_map/ppermute | solution.py:459
  470.3 13.8 %collective-permute-done.81 = bf16[2,2,2,64,768]{4,3,1,2,0:T(8,128)(2,1)S(1)} collective-permute-done((bf16[2,2,2,64,768]{4,3,1,2,0:T(8,128)(2,1)S(1)}, bf16[2,2,2,64,768]{4,3,1,2,0:T(8,128)(2,1)S(1)}, u32[]{:S(2)}, u32[]{:S(2)}) %collective-permute-start.81) | collective-permute-done | bytes 786464 | tf_op jit(solution)/shard_map/ppermute | solution.py:459
  (551 shorter events, 288.6 us)
Async XLA Ops:
  2.1 41.8 %collective-permute-start = (bf16[2,16,768]{2,1,0:T(8,128)(2,1)}, bf16[2,16,768]{2,1,0:T(8,128)(2,1)S(1)}, u32[]{:S(2)}, u32[]{:S(2)}) collective-permute-start(bf16[2,16,768]{2,1,0:T(8,128)(2,1)} %get-tuple-element.98), channel_id=1, source_target_pairs={{0,1},{1,2},{2,3},{4,5},{5,6},{6,7},{8,9},{9,10},{10,11},{12,13},{... | collective-permute-start | bytes 147464 | tf_op jit(solution)/shard_map/ppermute | solution.py:23
  7.0 37.6 %collective-permute-start.1 = (bf16[2,16,768]{2,1,0:T(8,128)(2,1)}, bf16[2,16,768]{2,1,0:T(8,128)(2,1)S(1)}, u32[]{:S(2)}, u32[]{:S(2)}) collective-permute-start(bf16[2,16,768]{2,1,0:T(8,128)(2,1)} %get-tuple-element.97), channel_id=1, source_target_pairs={{1,0},{2,1},{3,2},{5,4},{6,5},{7,6},{9,8},{10,9},{11,10},{13,12},{... | collective-permute-start | bytes 147464 | tf_op jit(solution)/shard_map/ppermute | solution.py:24
  14.3 40.3 %collective-permute-start.9 = (bf16[24,1536]{1,0:T(8,128)(2,1)S(1)}, bf16[24,1536]{1,0:T(8,128)(2,1)S(1)}, u32[]{:S(2)}, u32[]{:S(2)}) collective-permute-start(bf16[24,1536]{1,0:T(8,128)(2,1)S(1)} %constant_dynamic-update-slice_fusion), channel_id=1, source_target_pairs={{0,2},{1,3},{2,0},{3,1},{4,6},{5,7},{6,4},{7,5},{8,10},{9,11},{10,... | collective-permute-start | bytes 221192 | tf_op jit(solution)/shard_map/ppermute | solution.py:459
  31.0 28.7 %collective-permute-start.16 = (bf16[24,1536]{1,0:T(8,128)(2,1)S(1)}, bf16[24,1536]{1,0:T(8,128)(2,1)}, u32[]{:S(2)}, u32[]{:S(2)}) collective-permute-start(bf16[24,1536]{1,0:T(8,128)(2,1)S(1)} %constant_dynamic-update-slice_fusion.2), channel_id=1, source_target_pairs={{0,2},{1,3},{2,0},{3,1},{4,6},{5,7},{6,4},{7,5},{8,10},{9,11},{10,... | collective-permute-start | bytes 221192 | tf_op jit(solution)/shard_map/ppermute | solution.py:459
  44.0 80.6 %collective-permute-start.38 = (bf16[256,768]{1,0:T(8,128)(2,1)S(1)}, bf16[256,768]{1,0:T(8,128)(2,1)S(1)}, u32[]{:S(2)}, u32[]{:S(2)}) collective-permute-start(bf16[256,768]{1,0:T(8,128)(2,1)S(1)} %copy-done.53), channel_id=1, source_target_pairs={{0,0},{1,1},{2,4},{3,5},{4,2},{5,3},{6,6},{7,7},{8,8},{9,9},{10,12... | collective-permute-start | bytes 1179656 | tf_op jit(solution)/shard_map/ppermute | solution.py:513
  44.7 81.5 %collective-permute-start.39 = (bf16[256,768]{1,0:T(8,128)(2,1)S(1)}, bf16[256,768]{1,0:T(8,128)(2,1)S(1)}, u32[]{:S(2)}, u32[]{:S(2)}) collective-permute-start(bf16[256,768]{1,0:T(8,128)(2,1)S(1)} %get-tuple-element.123), channel_id=1, source_target_pairs={{0,1},{1,0},{2,5},{3,4},{4,3},{5,2},{6,7},{7,6},{8,9},{9,8},{10,13... | collective-permute-start | bytes 1179656 | tf_op jit(solution)/shard_map/ppermute | solution.py:513
  54.6 29.7 %collective-permute-start.26 = (bf16[24,2048]{1,0:T(8,128)(2,1)S(1)}, bf16[24,2048]{1,0:T(8,128)(2,1)S(1)}, u32[]{:S(2)}, u32[]{:S(2)}) collective-permute-start(bf16[24,2048]{1,0:T(8,128)(2,1)S(1)} %copy-done.59), channel_id=1, source_target_pairs={{0,2},{1,3},{2,0},{3,1},{4,6},{5,7},{6,4},{7,5},{8,10},{9,11},{10,... | collective-permute-start | bytes 294920 | tf_op jit(solution)/shard_map/ppermute | solution.py:459
  61.3 65.7 %collective-permute-start.7 = (bf16[272,768]{1,0:T(8,128)(2,1)S(1)}, bf16[272,768]{1,0:T(8,128)(2,1)S(1)}, u32[]{:S(2)}, u32[]{:S(2)}) collective-permute-start(bf16[272,768]{1,0:T(8,128)(2,1)S(1)} %get-tuple-element.114), channel_id=1, source_target_pairs={{0,0},{1,1},{2,4},{3,5},{4,2},{5,3},{6,6},{7,7},{8,8},{9,9},{10,12... | collective-permute-start | bytes 1253384 | tf_op jit(solution)/shard_map/ppermute | solution.py:513
  84.3 43.3 %collective-permute-start.8 = (bf16[272,768]{1,0:T(8,128)(2,1)S(1)}, bf16[272,768]{1,0:T(8,128)(2,1)S(1)}, u32[]{:S(2)}, u32[]{:S(2)}) collective-permute-start(bf16[272,768]{1,0:T(8,128)(2,1)S(1)} %get-tuple-element.113), channel_id=1, source_target_pairs={{0,1},{1,0},{2,5},{3,4},{4,3},{5,2},{6,7},{7,6},{8,9},{9,8},{10,13... | collective-permute-start | bytes 1253384 | tf_op jit(solution)/shard_map/ppermute | solution.py:513
  148.5 33.5 %collective-permute-start.24 = (bf16[2,2,2,24,2048]{4,3,2,1,0:T(8,128)(2,1)S(1)}, bf16[2,2,2,24,2048]{4,3,2,1,0:T(8,128)(2,1)S(1)}, u32[]{:S(2)}, u32[]{:S(2)}) collective-permute-start(bf16[2,2,2,24,2048]{4,3,2,1,0:T(8,128)(2,1)S(1)} %pad_maximum_fusion.13), channel_id=1, source_target_pairs={{0,8},{4,12},{8,0},{12,4},{16,24},{20,28},{24,16},{28,20},{1,9},{5... | collective-permute-start | bytes 2359304 | tf_op jit(solution)/shard_map/ppermute | solution.py:459
  157.0 27.6 %collective-permute-start.20 = (bf16[2,2,2,2,24,1536]{5,4,2,3,1,0:T(8,128)(2,1)S(1)}, bf16[2,2,2,2,24,1536]{5,4,2,3,1,0:T(8,128)(2,1)S(1)}, u32[]{:S(2)}, u32[]{:S(2)}) collective-permute-start(bf16[2,2,2,2,24,1536]{5,4,2,3,1,0:T(8,128)(2,1)S(1)} %pad_maximum_fusion.10), channel_id=1, source_target_pairs={{0,4},{4,0},{8,12},{12,8},{16,20},{20,16},{24,28},{28,24},{1,5},{5... | collective-permute-start | bytes 3538952 | tf_op jit(solution)/shard_map/ppermute | solution.py:459
  166.7 47.0 %collective-permute-start.35 = (bf16[2,2,2,2,64,768]{5,4,3,2,1,0:T(8,128)(2,1)}, bf16[2,2,2,2,64,768]{5,4,3,2,1,0:T(8,128)(2,1)}, u32[]{:S(2)}, u32[]{:S(2)}) collective-permute-start(bf16[2,2,2,2,64,768]{5,4,3,2,1,0:T(8,128)(2,1)} %pad_maximum_fusion.8), channel_id=1, source_target_pairs={{0,4},{4,0},{8,12},{12,8},{16,20},{20,16},{24,28},{28,24},{1,5},{5... | collective-permute-start | bytes 4718600 | tf_op jit(solution)/shard_map/ppermute | solution.py:459
  171.4 39.8 %collective-permute-start.30 = (bf16[2,2,2,2,24,2048]{5,4,2,3,1,0:T(8,128)(2,1)}, bf16[2,2,2,2,24,2048]{5,4,2,3,1,0:T(8,128)(2,1)}, u32[]{:S(2)}, u32[]{:S(2)}) collective-permute-start(bf16[2,2,2,2,24,2048]{5,4,2,3,1,0:T(8,128)(2,1)} %pad_maximum_fusion.7), channel_id=1, source_target_pairs={{0,4},{4,0},{8,12},{12,8},{16,20},{20,16},{24,28},{28,24},{1,5},{5... | collective-permute-start | bytes 4718600 | tf_op jit(solution)/shard_map/ppermute | solution.py:459
  183.4 34.2 %collective-permute-start.25 = (bf16[2,2,2,2,24,2048]{5,4,3,2,1,0:T(8,128)(2,1)}, bf16[2,2,2,2,24,2048]{5,4,3,2,1,0:T(8,128)(2,1)}, u32[]{:S(2)}, u32[]{:S(2)}) collective-permute-start(bf16[2,2,2,2,24,2048]{5,4,3,2,1,0:T(8,128)(2,1)} %pad_maximum_fusion.6), channel_id=1, source_target_pairs={{0,4},{4,0},{8,12},{12,8},{16,20},{20,16},{24,28},{28,24},{1,5},{5... | collective-permute-start | bytes 4718600 | tf_op jit(solution)/shard_map/ppermute | solution.py:459
  283.9 44.4 %collective-permute-start.40 = (bf16[512,768]{1,0:T(8,128)(2,1)}, bf16[512,768]{1,0:T(8,128)(2,1)}, u32[]{:S(2)}, u32[]{:S(2)}) collective-permute-start(bf16[512,768]{1,0:T(8,128)(2,1)} %fusion.38), channel_id=1, source_target_pairs={{0,4},{4,0},{8,12},{12,8},{16,20},{20,16},{24,28},{28,24},{1,5},{5... | collective-permute-start | bytes 2359304 | tf_op jit(solution)/shard_map/ppermute | solution.py:459
  285.7 97.5 %collective-permute-start.37 = (bf16[256,768]{1,0:T(8,128)(2,1)}, bf16[256,768]{1,0:T(8,128)(2,1)}, u32[]{:S(2)}, u32[]{:S(2)}) collective-permute-start(bf16[256,768]{1,0:T(8,128)(2,1)} %get-tuple-element.127), channel_id=1, source_target_pairs={{1,0},{0,1},{5,2},{4,3},{3,4},{2,5},{7,6},{6,7},{9,8},{8,9},{13,10... | collective-permute-start | bytes 1179656 | tf_op jit(solution)/shard_map/ppermute | solution.py:534
  286.8 96.9 %collective-permute-start.36 = (bf16[256,768]{1,0:T(8,128)(2,1)}, bf16[256,768]{1,0:T(8,128)(2,1)}, u32[]{:S(2)}, u32[]{:S(2)}) collective-permute-start(bf16[256,768]{1,0:T(8,128)(2,1)} %get-tuple-element.128), channel_id=1, source_target_pairs={{0,0},{1,1},{4,2},{5,3},{2,4},{3,5},{6,6},{7,7},{8,8},{9,9},{12,10... | collective-permute-start | bytes 1179656 | tf_op jit(solution)/shard_map/ppermute | solution.py:534
  336.7 47.0 %collective-permute-start.41 = (bf16[256,768]{1,0:T(8,128)(2,1)S(1)}, bf16[256,768]{1,0:T(8,128)(2,1)S(1)}, u32[]{:S(2)}, u32[]{:S(2)}) collective-permute-start(bf16[256,768]{1,0:T(8,128)(2,1)S(1)} %get-tuple-element.120), channel_id=1, source_target_pairs={{0,0},{1,1},{4,2},{5,3},{2,4},{3,5},{6,6},{7,7},{8,8},{9,9},{12,10... | collective-permute-start | bytes 1179656 | tf_op jit(solution)/shard_map/ppermute | solution.py:534
  340.8 43.0 %collective-permute-start.42 = (bf16[256,768]{1,0:T(8,128)(2,1)S(1)}, bf16[256,768]{1,0:T(8,128)(2,1)S(1)}, u32[]{:S(2)}, u32[]{:S(2)}) collective-permute-start(bf16[256,768]{1,0:T(8,128)(2,1)S(1)} %get-tuple-element.119), channel_id=1, source_target_pairs={{1,0},{0,1},{5,2},{4,3},{3,4},{2,5},{7,6},{6,7},{9,8},{8,9},{13,10... | collective-permute-start | bytes 1179656 | tf_op jit(solution)/shard_map/ppermute | solution.py:534
  382.5 59.9 %collective-permute-start.70 = (bf16[2,2,2,2,24,2048]{5,4,2,3,0,1:T(8,128)(2,1)}, bf16[2,2,2,2,24,2048]{5,4,2,3,0,1:T(8,128)(2,1)}, u32[]{:S(2)}, u32[]{:S(2)}) collective-permute-start(bf16[2,2,2,2,24,2048]{5,4,2,3,0,1:T(8,128)(2,1)} %bitcast.457), channel_id=1, source_target_pairs={{0,4},{4,0},{8,12},{12,8},{16,20},{20,16},{24,28},{28,24},{1,5},{5... | collective-permute-start | bytes 4718600 | tf_op jit(solution)/shard_map/ppermute | solution.py:459
  383.2 62.9 %collective-permute-start.75 = (bf16[2,2,2,2,24,2048]{5,4,2,3,1,0:T(8,128)(2,1)}, bf16[2,2,2,2,24,2048]{5,4,2,3,1,0:T(8,128)(2,1)}, u32[]{:S(2)}, u32[]{:S(2)}) collective-permute-start(bf16[2,2,2,2,24,2048]{5,4,2,3,1,0:T(8,128)(2,1)} %bitcast.456), channel_id=1, source_target_pairs={{0,4},{4,0},{8,12},{12,8},{16,20},{20,16},{24,28},{28,24},{1,5},{5... | collective-permute-start | bytes 4718600 | tf_op jit(solution)/shard_map/ppermute | solution.py:459
  383.7 65.1 %collective-permute-start.80 = (bf16[2,2,2,2,64,768]{5,4,2,3,1,0:T(8,128)(2,1)}, bf16[2,2,2,2,64,768]{5,4,2,3,1,0:T(8,128)(2,1)S(1)}, u32[]{:S(2)}, u32[]{:S(2)}) collective-permute-start(bf16[2,2,2,2,64,768]{5,4,2,3,1,0:T(8,128)(2,1)} %bitcast.455), channel_id=1, source_target_pairs={{0,4},{4,0},{8,12},{12,8},{16,20},{20,16},{24,28},{28,24},{1,5},{5... | collective-permute-start | bytes 4718600 | tf_op jit(solution)/shard_map/ppermute | solution.py:459
  450.0 34.1 %collective-permute-start.81 = (bf16[2,2,2,64,768]{4,3,1,2,0:T(8,128)(2,1)S(1)}, bf16[2,2,2,64,768]{4,3,1,2,0:T(8,128)(2,1)S(1)}, u32[]{:S(2)}, u32[]{:S(2)}) collective-permute-start(bf16[2,2,2,64,768]{4,3,1,2,0:T(8,128)(2,1)S(1)} %dynamic-slice_bitcast_fusion), channel_id=1, source_target_pairs={{0,16},{4,20},{8,24},{12,28},{16,0},{20,4},{24,8},{28,12},{1,17},{... | collective-permute-start | bytes 2359304 | tf_op jit(solution)/shard_map/ppermute | solution.py:459
  460.0 28.4 %collective-permute-start.72 = (bf16[2,2,24,2048]{3,2,0,1:T(8,128)(2,1)S(1)}, bf16[2,2,24,2048]{3,2,0,1:T(8,128)(2,1)S(1)}, u32[]{:S(2)}, u32[]{:S(2)}) collective-permute-start(bf16[2,2,24,2048]{3,2,0,1:T(8,128)(2,1)S(1)} %dynamic-slice_bitcast_fusion.7), channel_id=1, source_target_pairs={{0,16},{4,20},{8,24},{12,28},{16,0},{20,4},{24,8},{28,12},{1,17},{... | collective-permute-start | bytes 1179656 | tf_op jit(solution)/shard_map/ppermute | solution.py:459
  (142 other events, 1711.8 us)

commit v2 on v1

--- a/solution.py
+++ b/solution.py
@@ -1,3 +1,5 @@
+import functools
+
 import jax
 import jax.numpy as jnp
 from jax import lax
@@ -29,16 +31,6 @@
     distance = jnp.abs(offset)
     far_bucket = 8 + sum(((distance >= cut_point).astype(jnp.int32) for cut_point in cut_points))
     return jnp.where(distance < 8, distance, far_bucket) + jnp.where(offset > 0, 16, 0)
-
-
-def rms_scale(values, gain_vec):
-    return (
-        values * lax.rsqrt(jnp.mean(values * values, axis=-1, keepdims=True) + norm_eps) * gain_vec
-    )
-
-
-def gelu_gate(gate_in, up_in):
-    return jax.nn.gelu(gate_in, approximate=True) * up_in
 
 
 EDGE = 8
@@ -244,6 +236,9 @@
     return pl.pallas_call(
         pool_forward_kernel,
         name="pool_forward",
+        cost_estimate=pl.CostEstimate(
+            flops=count * (4 << 30), bytes_accessed=1 << 20, transcendentals=0
+        ),
         grid_spec=pltpu.PrefetchScalarGridSpec(
             num_scalar_prefetch=1,
             grid=(count,),
@@ -401,6 +396,9 @@
     return pl.pallas_call(
         pool_backward_kernel,
         name="pool_backward",
+        cost_estimate=pl.CostEstimate(
+            flops=count * (10 << 30), bytes_accessed=1 << 20, transcendentals=0
+        ),
         grid_spec=pltpu.PrefetchScalarGridSpec(
             num_scalar_prefetch=1,
             grid=(count,),
@@ -441,12 +439,13 @@
     return count
 
 
-def stage_orders():
+def stage_phases():
     dp_bits, seq_bits = (bits_of("dp"), bits_of("seq"))
-    along_seq = [("seq", bit) for bit in reversed(range(seq_bits))]
-    across = [("dp", bit) for bit in range(1, dp_bits)]
-    cores = [("dp", 0)]
-    return (along_seq + across[::-1] + cores, along_seq + across + cores)
+    along = [("seq", bit) for bit in reversed(range(seq_bits))]
+    low_half = [("dp", bit) for bit in range(1, 1 + (dp_bits - 1) // 2)]
+    high_half = [("dp", bit) for bit in range(1 + (dp_bits - 1) // 2, dp_bits)]
+    ends = ([along[:1], along[1:]], [[("dp", 0)]])
+    return (ends[0] + [high_half, low_half] + ends[1], ends[0] + [low_half, high_half] + ends[1])
 
 
 def place_of(axis, bit):
@@ -463,43 +462,134 @@
     return (lax.axis_index(axis) >> bit) & 1
 
 
-def gather_all(x, order):
-    held = []
-    whole = x
-    for axis, bit in order:
-        place = place_of(axis, bit)
-        dim = sum(other < place for other in held)
-        arrived = swap_bit(whole, axis, bit)
-        upper = own_bit(axis, bit) == 1
-        whole = jnp.stack(
-            [jnp.where(upper, arrived, whole), jnp.where(upper, whole, arrived)], axis=dim
-        )
-        held.append(place)
-    return whole.reshape((1 << len(order),) + x.shape)
-
-
-def scatter_sum(blocks, order):
-    shape = blocks.shape[1:]
-    part = blocks.reshape((2,) * len(order) + shape)
-    held = list(range(len(order)))
-    for number, (axis, bit) in enumerate(order[::-1]):
-        place = place_of(axis, bit)
-        dim = held.index(place)
-        held.remove(place)
-        mine = own_bit(axis, bit)
-        leaving = lax.dynamic_index_in_dim(part, 1 - mine, dim, keepdims=False)
-        staying = lax.dynamic_index_in_dim(part, mine, dim, keepdims=False)
-        arrived = swap_bit(leaving.astype(jnp.bfloat16), axis, bit)
-        part = staying.astype(jnp.float32) + arrived.astype(jnp.float32)
-        if number < len(order) - 1:
-            part = part.astype(jnp.bfloat16)
-    return part
-
-
-def sum_all(x, order):
-    for axis, bit in order[::-1]:
-        x = x + swap_bit(x, axis, bit)
-    return x
+class Chain:
+    def __init__(self):
+        self.noted = None
+
+    def after(self, *values):
+        if self.noted is not None:
+            values = lax.optimization_barrier(values + (self.noted,))[:-1]
+        return values if len(values) > 1 else values[0]
+
+    def note(self, value):
+        self.noted = value
+        return value
+
+
+class Gathering:
+    def __init__(self, chain, block, phases, held=()):
+        self.chain, self.whole, self.held = (chain, block, list(held))
+        self.phases = [list(phase) for phase in phases]
+        self.start()
+
+    def start(self):
+        if self.phases:
+            self.arrived = swap_bit(self.whole, *self.phases[0][0])
+
+    def finish(self):
+        for axis, bit in self.phases.pop(0):
+            if self.arrived is None:
+                self.arrived = swap_bit(self.whole, axis, bit)
+            place = place_of(axis, bit)
+            dim = sum(other < place for other in self.held)
+            arrived, whole = self.chain.after(self.arrived, self.whole)
+            upper = own_bit(axis, bit) == 1
+            self.whole = self.chain.note(
+                jnp.stack(
+                    [jnp.where(upper, arrived, whole), jnp.where(upper, whole, arrived)], axis=dim
+                )
+            )
+            self.held.append(place)
+            self.arrived = None
+        self.start()
+        return self.whole
+
+
+class Reduction:
+    def __init__(self, chain, leaving, staying, rows, phases):
+        self.chain = chain
+        self.steps = [step for phase in phases[::-1] for step in phase[::-1]]
+        self.counts = [len(phase) for phase in phases[::-1]]
+        self.held = list(range(len(self.steps)))
+        axis, bit = self.steps.pop(0)
+        assert (axis, bit) == ("dp", 0)
+        self.held.remove(place_of(axis, bit))
+        shape = leaving.shape[:1] + (2,) * len(self.steps) + (rows, leaving.shape[-1])
+        self.staying = staying.reshape(shape)
+        self.arriving = swap_bit(leaving, axis, bit).reshape(shape)
+
+    def halves(self, x):
+        axis, bit = self.steps[0]
+        dim = 1 + self.held.index(place_of(axis, bit))
+        own = own_bit(axis, bit)
+        return [
+            lax.dynamic_index_in_dim(x, which, dim, keepdims=False) for which in (1 - own, own)
+        ]
+
+    def finish(self):
+        f32 = jnp.float32
+        for _ in range(self.counts.pop(0)):
+            arrived, staying = self.chain.after(self.arriving, self.staying)
+            if not self.steps:
+                self.chain.note(arrived)
+                return staying.astype(f32) + arrived.astype(f32)
+            parts = zip(self.halves(staying), self.halves(arrived))
+            leaving, staying = [
+                (x.astype(f32) + y.astype(f32)).astype(jnp.bfloat16) for x, y in parts
+            ]
+            self.chain.note(leaving)
+            self.staying = staying
+            axis, bit = self.steps.pop(0)
+            self.held.remove(place_of(axis, bit))
+            self.arriving = swap_bit(leaving, axis, bit)
+
+
+def group_masks(group):
+    axis = group[0][0]
+    size = lax.axis_size(axis)
+    masks = [0]
+    for _, bit in group:
+        masks = masks + [mask | 1 << bit for mask in masks]
+    return [(axis, [(i, i ^ mask) for i in range(size)]) for mask in masks[1:]]
+
+
+def exchange(x, group):
+    return [x] + [lax.ppermute(x, axis, pairs) for axis, pairs in group_masks(group)]
+
+
+def tree_sum(values):
+    while len(values) > 1:
+        values = [a + b for a, b in zip(values[::2], values[1::2])]
+    return values[0]
+
+
+def exchange_groups():
+    groups = [[("dp", 0)]]
+    for axis, first in (("dp", 1), ("seq", 0)):
+        left = [(axis, bit) for bit in range(first, bits_of(axis))]
+        groups += [left[i : i + 2] for i in range(0, len(left), 2)]
+    return groups
+
+
+def pack_kernel(*refs):
+    ins, out_refs = (refs[:-2], refs[-2:])
+    for out_ref, part in ((out_refs[0], ins[:4]), (out_refs[1], ins[4:])):
+        place = 0
+        for ref in part:
+            width = ref.shape[1]
+            out_ref[:, place : place + width] = ref[...]
+            place += width
+
+
+def pack_weights(w_query, w_key, w_value, w_out, w_gate, w_up):
+    rows = w_query.shape[0]
+    parts = (w_query, w_key, w_value, w_out, w_gate, w_up)
+    widths = (4 * w_query.shape[1], 2 * w_gate.shape[1])
+    return pl.pallas_call(
+        pack_kernel,
+        name="pack_weights",
+        out_shape=[jax.ShapeDtypeStruct((rows, width), w_query.dtype) for width in widths],
+    )(*parts)
 
 
 def to_chips(pieces):
@@ -511,27 +601,36 @@
         pairs = chip_pairs(dp_size, seq_size, count, phase)
         leaving = lax.dynamic_index_in_dim(pieces, (seq_index + phase) % count, 0, keepdims=False)
         arrived.append(lax.ppermute(leaving, ("dp", "seq"), pairs))
+    return arrived
+
+
+def in_token_order(arrived):
+    count = len(arrived)
+    number = lax.axis_index("seq") % count
     stacked = jnp.stack(arrived)
-    number = seq_index % count
-    return jnp.concatenate(
+    return jnp.stack(
         [
             lax.dynamic_index_in_dim(stacked, (number - r) % count, 0, keepdims=False)
             for r in range(count)
-        ],
-        axis=0,
+        ]
     )
 
 
 def from_chips(tokens, count):
     dp_size, seq_size = (lax.axis_size("dp"), lax.axis_size("seq"))
-    seq_index = lax.axis_index("seq")
-    number = seq_index % count
+    number = lax.axis_index("seq") % count
     split = tokens.reshape((count, tokens.shape[0] // count) + tokens.shape[1:])
     arrived = []
     for phase in range(count):
         pairs = [(j, i) for i, j in chip_pairs(dp_size, seq_size, count, phase)]
         leaving = lax.dynamic_index_in_dim(split, (number - phase) % count, 0, keepdims=False)
         arrived.append(lax.ppermute(leaving, ("dp", "seq"), pairs))
+    return arrived
+
+
+def in_piece_order(arrived):
+    count = len(arrived)
+    seq_index = lax.axis_index("seq")
     stacked = jnp.stack(arrived)
     return jnp.stack(
         [
@@ -589,8 +688,9 @@
 
 
 def attn_forward_kernel(
-    first_ref, q_ref, k_ref, ka_ref, v_ref, far_ref, bias_ref, out_ref, lse_ref, s_ref
+    skipped, first_ref, q_ref, k_ref, ka_ref, v_ref, far_ref, bias_ref, *rest
 ):
+    out_ref, lse_ref, s_ref = rest[skipped:]
     keys = k_ref.shape[0]
     tokens = q_ref.shape[1]
     lhs = jnp.concatenate([k_ref[...], ka_ref[...]], axis=1)
@@ -616,27 +716,32 @@
         lse_ref[0, a : a + 1] = row_max + jnp.log(total)
 
 
-def attn_forward(first, q_t, keys, key_aug, v_t, far, bias):
+def attn_forward(first, q_t, keys, key_aug, v_t, far, bias, pair_range, earlier):
     width, tokens = q_t.shape
     key_count = keys.shape[0]
     pairs = width // TILE
+    base, stop = pair_range
     return pl.pallas_call(
-        attn_forward_kernel,
+        functools.partial(attn_forward_kernel, len(earlier)),
         name="attn_forward",
+        cost_estimate=pl.CostEstimate(
+            flops=(stop - base) * (5 << 29), bytes_accessed=1 << 20, transcendentals=0
+        ),
         grid_spec=pltpu.PrefetchScalarGridSpec(
             num_scalar_prefetch=1,
-            grid=(pairs,),
+            grid=(stop - base,),
             in_specs=[
-                pl.BlockSpec((TILE, tokens), lambda h, _: (h, 0)),
-                pl.BlockSpec((key_count, TILE), lambda h, _: (0, h)),
+                pl.BlockSpec((TILE, tokens), lambda h, _: (h + base, 0)),
+                pl.BlockSpec((key_count, TILE), lambda h, _: (0, h + base)),
                 pl.BlockSpec((key_count, TILE), lambda h, _: (0, 0)),
-                pl.BlockSpec((TILE, key_count), lambda h, _: (h, 0)),
-                pl.BlockSpec((2, AUG, tokens), lambda h, _: (h, 0, 0)),
-                pl.BlockSpec((2, 3, TILE, TILE), lambda h, _: (h, 0, 0, 0)),
-            ],
+                pl.BlockSpec((TILE, key_count), lambda h, _: (h + base, 0)),
+                pl.BlockSpec((2, AUG, tokens), lambda h, _: (h + base, 0, 0)),
+                pl.BlockSpec((2, 3, TILE, TILE), lambda h, _: (h + base, 0, 0, 0)),
+            ]
+            + [pl.BlockSpec(memory_space=pl.ANY)] * len(earlier),
             out_specs=[
-                pl.BlockSpec((TILE, tokens), lambda h, _: (h, 0)),
-                pl.BlockSpec((1, 2, tokens), lambda h, _: (h, 0, 0)),
+                pl.BlockSpec((TILE, tokens), lambda h, _: (h + base, 0)),
+                pl.BlockSpec((1, 2, tokens), lambda h, _: (h + base, 0, 0)),
             ],
             scratch_shapes=[pltpu.VMEM((key_count + 2 * TILE, tokens), jnp.float32)],
         ),
@@ -644,11 +749,13 @@
             jax.ShapeDtypeStruct((width, tokens), jnp.bfloat16),
             jax.ShapeDtypeStruct((pairs, 2, tokens), jnp.float32),
         ],
+        input_output_aliases={7 + i: i for i in range(len(earlier))},
         compiler_params=pltpu.CompilerParams(vmem_limit_bytes=48 << 20),
-    )(first, q_t, keys, key_aug, v_t, far, bias)
+    )(first, q_t, keys, key_aug, v_t, far, bias, *earlier)
 
 
 def attn_backward_kernel(
+    skipped,
     first_ref,
     q_ref,
     do_ref,
@@ -661,15 +768,9 @@
     block_ref,
     far_ref,
     bias_ref,
-    dq_ref,
-    dk_ref,
-    dv_ref,
-    near_ref,
-    sums_ref,
-    s_ref,
-    ds_ref,
-    p_ref,
+    *rest,
 ):
+    dq_ref, dk_ref, dv_ref, near_ref, sums_ref, s_ref, ds_ref, p_ref = rest[skipped:]
     keys = k_ref.shape[0]
     tokens = q_ref.shape[1]
     f32, low = (jnp.float32, jnp.bfloat16)
@@ -720,37 +821,57 @@
     ).astype(low)
 
 
-def attn_backward(first, q_t, do_t, out_t, lse, keys, values, k_t, key_aug, block_rows, far, bias):
+def attn_backward(
+    first,
+    q_t,
+    do_t,
+    out_t,
+    lse,
+    keys,
+    values,
+    k_t,
+    key_aug,
+    block_rows,
+    far,
+    bias,
+    pair_range,
+    earlier,
+):
     width, tokens = q_t.shape
     key_count = keys.shape[0]
     pairs = width // TILE
-    across = pl.BlockSpec((TILE, tokens), lambda h, _: (h, 0))
-    along = pl.BlockSpec((key_count, TILE), lambda h, _: (0, h))
+    base, stop = pair_range
+    across = pl.BlockSpec((TILE, tokens), lambda h, _: (h + base, 0))
+    along = pl.BlockSpec((key_count, TILE), lambda h, _: (0, h + base))
     return pl.pallas_call(
-        attn_backward_kernel,
+        functools.partial(attn_backward_kernel, len(earlier)),
         name="attn_backward",
+        cost_estimate=pl.CostEstimate(
+            flops=(stop - base) * (9 << 29), bytes_accessed=1 << 20, transcendentals=0
+        ),
         grid_spec=pltpu.PrefetchScalarGridSpec(
             num_scalar_prefetch=1,
-            grid=(pairs,),
+            grid=(stop - base,),
             in_specs=[
                 across,
                 across,
                 across,
-                pl.BlockSpec((1, 2, tokens), lambda h, _: (h, 0, 0)),
+                pl.BlockSpec((1, 2, tokens), lambda h, _: (h + base, 0, 0)),
                 along,
                 along,
-                pl.BlockSpec((TILE, key_count), lambda h, _: (h, 0)),
+                pl.BlockSpec((TILE, key_count), lambda h, _: (h + base, 0)),
                 pl.BlockSpec((key_count, TILE), lambda h, _: (0, 0)),
                 pl.BlockSpec((AUG, key_count), lambda h, _: (0, 0)),
-                pl.BlockSpec((2, AUG, tokens), lambda h, _: (h, 0, 0)),
-                pl.BlockSpec((2, 3, TILE, TILE), lambda h, _: (h, 0, 0, 0)),
-            ],
+                pl.BlockSpec((2, AUG, tokens), lambda h, _: (h + base, 0, 0)),
+                pl.BlockSpec((2, 3, TILE, TILE), lambda h, _: (h + base, 0, 0, 0)),
+            ]
+            + [pl.BlockSpec(memory_space=pl.ANY)] * len(earlier),
             out_specs=[
                 across,
                 along,
                 along,
-                pl.BlockSpec((2, 3, TILE, TILE), lambda h, _: (h, 0, 0, 0)),
-                pl.BlockSpec((1, 2, AUG, tokens), lambda h, _: (h, 0, 0, 0)),
+                pl.BlockSpec((2, 3, TILE, TILE), lambda h, _: (h + base, 0, 0, 0)),
+                pl.BlockSpec((1, 2, AUG, tokens), lambda h, _: (h + base, 0, 0, 0)),
             ],
             scratch_shapes=[
                 pltpu.VMEM((key_count + 2 * TILE, tokens), jnp.float32),
@@ -765,8 +886,23 @@
             jax.ShapeDtypeStruct((2 * pairs, 3, TILE, TILE), jnp.float32),
             jax.ShapeDtypeStruct((pairs, 2, AUG, tokens), jnp.float32),
         ],
+        input_output_aliases={12 + i: i for i in range(len(earlier))},
         compiler_params=pltpu.CompilerParams(vmem_limit_bytes=56 << 20),
-    )(first, q_t, do_t, out_t, lse, keys, values, k_t, key_aug, block_rows, far, bias)
+    )(
+        first,
+        q_t,
+        do_t,
+        out_t,
+        lse,
+        keys,
+        values,
+        k_t,
+        key_aug,
+        block_rows,
+        far,
+        bias,
+        *earlier,
+    )
 
 
 def attn_tables(first, tokens, key_count, length, rel_bias):
@@ -789,37 +925,288 @@
     far = jnp.where(apart <= -2, before, jnp.where(apart >= 2, after, 0.0))
     in_use = (line < blocks)[None, :, None]
     far = jnp.where(in_use, far, jnp.where((line == 8)[None, :, None], 1.0, 0.0)).astype(low)
-    bias = jnp.einsum("djib,bh->hdji", near_onehot(), rel_bias.astype(f32), precision=highest)
-    return key_aug, block_rows, far, bias
-
-
-def near_onehot():
-    step = jnp.arange(TILE, dtype=jnp.int32)
-    offset = (
-        TILE * (jnp.arange(3, dtype=jnp.int32) - 1)[:, None, None]
-        + step[None, :, None]
-        - step[None, None, :]
-    )
-    return (bucket_of(offset)[..., None] == jnp.arange(BUCKETS, dtype=jnp.int32)).astype(
-        jnp.float32
-    )
-
-
-def bias_gradient(first, near, sums):
-    pairs, _, _, tokens = sums.shape
-    close = jnp.einsum("hdji,djib->bh", near, near_onehot(), precision=highest)
-    line = jnp.arange(AUG, dtype=jnp.int32)[:, None]
-    tile = first + jnp.arange(tokens, dtype=jnp.int32)[None, :] // TILE
+    return key_aug, block_rows, far
+
+
+def near_bias_kernel(rel_ref, out_ref):
+    width = 4 * TILE
+    heads = rel_ref.shape[0]
+    lane = lax.broadcasted_iota(jnp.int32, (BUCKETS, width), 1)
+    bucket = bucket_of(2 * TILE - 1 - lane)
+    line = lax.broadcasted_iota(jnp.int32, (BUCKETS, width), 0)
+    table = mm(rel_ref[...], jnp.where(bucket == line, 1.0, 0.0).astype(jnp.bfloat16))
+    for h in range(heads):
+        rows = jnp.broadcast_to(table[h : h + 1], (TILE, width))
+        rows = pltpu.roll(rows, 3 * TILE + 1, 1, stride=1, stride_axis=0)
+        for d in range(3):
+            out_ref[h, d] = rows[:, (2 - d) * TILE : (3 - d) * TILE]
+
+
+def near_bias(rel_t):
+    return pl.pallas_call(
+        near_bias_kernel,
+        name="near_bias",
+        cost_estimate=pl.CostEstimate(
+            flops=3 << 30, bytes_accessed=1 << 20, transcendentals=0
+        ),
+        out_shape=jax.ShapeDtypeStruct((rel_t.shape[0], 3, TILE, TILE), jnp.float32),
+    )(rel_t)
+
+
+def bias_gradient_kernel(first_ref, near_ref, sums_ref, out_ref, line_ref):
+    width = 4 * TILE
+    heads = near_ref.shape[0]
+    tokens = sums_ref.shape[3]
+    f32 = jnp.float32
+    line = lax.broadcasted_iota(jnp.int32, (AUG, tokens), 0)
+    tile = first_ref[0] + lax.broadcasted_iota(jnp.int32, (AUG, tokens), 1) // TILE
     apart = line - tile
-    sums = sums.reshape(2 * pairs, AUG, tokens)
-    before = jnp.sum(jnp.where(apart <= -2, sums, 0.0), axis=(1, 2))
-    after = jnp.sum(jnp.where(apart >= 2, sums, 0.0), axis=(1, 2))
-    bucket = jnp.arange(BUCKETS, dtype=jnp.int32)[:, None]
-    return (
-        close
-        + jnp.where(bucket == BUCKETS // 2 - 1, before[None, :], 0.0)
-        + jnp.where(bucket == BUCKETS - 1, after[None, :], 0.0)
-    )
+    column = lax.broadcasted_iota(jnp.int32, (1, BUCKETS), 1)
+    far_rows = []
+    for h in range(heads):
+        tiles = [near_ref[h, 2 - k] for k in range(3)]
+        rows = jnp.concatenate(tiles + [jnp.zeros((TILE, TILE), f32)], axis=1)
+        eight = rows[:8]
+        for start in range(8, TILE, 8):
+            eight = eight + pltpu.roll(rows[start : start + 8], width - start, 1)
+        total = eight[:1]
+        for step in range(1, 8):
+            total = total + pltpu.roll(eight[step : step + 1], width - step, 1)
+        line_ref[h : h + 1] = total
+        sums = sums_ref[h // 2, h % 2]
+        before = jnp.sum(jnp.where(apart <= -2, sums, 0.0), axis=1, keepdims=True)
+        after = jnp.sum(jnp.where(apart >= 2, sums, 0.0), axis=1, keepdims=True)
+        before = jnp.sum(before, axis=0, keepdims=True)
+        after = jnp.sum(after, axis=0, keepdims=True)
+        far_rows.append(
+            jnp.where(column == BUCKETS // 2 - 1, before, 0.0)
+            + jnp.where(column == BUCKETS - 1, after, 0.0)
+        )
+    lane = lax.broadcasted_iota(jnp.int32, (BUCKETS, width), 1)
+    offset = jnp.where(lane < 3 * TILE, TILE - lane, 5 * TILE - lane)
+    bucket = bucket_of(offset)
+    pick = jnp.where(bucket == lax.broadcasted_iota(jnp.int32, (BUCKETS, width), 0), 1.0, 0.0)
+    close = lax.dot_general(
+        line_ref[...], pick, (((1,), (1,)), ((), ())), precision=highest, preferred_element_type=f32
+    )
+    out_ref[...] = close + jnp.concatenate(far_rows, axis=0)
+
+
+def bias_gradient(first_ref, near, sums):
+    heads = near.shape[0]
+    return pl.pallas_call(
+        bias_gradient_kernel,
+        name="bias_gradient",
+        cost_estimate=pl.CostEstimate(
+            flops=4 << 30, bytes_accessed=1 << 20, transcendentals=0
+        ),
+        in_specs=[
+            pl.BlockSpec(memory_space=pltpu.SMEM),
+            pl.BlockSpec(memory_space=pltpu.VMEM),
+            pl.BlockSpec(memory_space=pltpu.VMEM),
+        ],
+        out_shape=jax.ShapeDtypeStruct((heads, BUCKETS), jnp.float32),
+        scratch_shapes=[pltpu.VMEM((heads, 4 * TILE), jnp.float32)],
+    )(first_ref, near, sums)
+
+
+def part_rows(blocks, mine, size):
+    width = blocks.shape[-1]
+    split = blocks.reshape(blocks.shape[0] // (2 * size), 2, size, width)
+    other, own = (split[:, 0], split[:, 1])
+    first = mine == 1
+    return jnp.where(first, other, own), jnp.where(first, own, other)
+
+
+def ffn_kernel(
+    sub,
+    core_ref,
+    after_ref,
+    gain_ref,
+    seed_ref,
+    gate_ref,
+    up_ref,
+    down_ref,
+    block_ref,
+    grad_ref,
+    gain_grad_ref,
+    wide_leave_ref,
+    wide_stay_ref,
+    down_leave_ref,
+    down_stay_ref,
+    unit_ref,
+    normed_ref,
+    normed_t_ref,
+    out_ref,
+    back_ref,
+):
+    f32, low = (jnp.float32, jnp.bfloat16)
+    step = pl.program_id(0)
+    core = core_ref[0]
+
+    @pl.when(step == 0)
+    def _():
+        after = after_ref[...]
+        scale = lax.rsqrt(jnp.mean(after * after, axis=1, keepdims=True) + norm_eps)
+        normed = (after * scale * gain_ref[...]).astype(low)
+        unit_ref[...] = jnp.broadcast_to(scale, unit_ref.shape)
+        normed_ref[...] = normed
+        normed_t_ref[...] = jnp.transpose(normed)
+        out_ref[...] = after
+        back_ref[...] = jnp.zeros_like(back_ref)
+
+    normed = normed_ref[...]
+    seed = seed_ref[...]
+    gate = mm(normed, gate_ref[...])
+    up = mm(normed, up_ref[...])
+    cube = 0.044715 * gate * gate
+    bend = jnp.tanh(0.7978845608028654 * (gate + cube * gate))
+    half = 0.5 * (1.0 + bend)
+    act = gate * half
+    slope = half + (0.5 * 0.7978845608028654) * gate * (1.0 - bend * bend) * (1.0 + 3.0 * cube)
+    inner = (act * up).astype(low)
+    out_ref[...] += mm(inner, down_ref[...])
+    grad_inner = mm_nt(seed, down_ref[...])
+    grad_gate = (grad_inner * up * slope).astype(low)
+    grad_up = (grad_inner * act).astype(low)
+    back_ref[...] += mm_nt(grad_gate, gate_ref[...]) + mm_nt(grad_up, up_ref[...])
+    rows = wide_leave_ref.shape[2]
+    for number, grad in enumerate((grad_gate, grad_up)):
+        leave, stay = part_rows(mm(normed_t_ref[...], grad), core, rows)
+        wide_leave_ref[number] = leave.astype(low)
+        wide_stay_ref[number] = stay.astype(low)
+    leave, stay = part_rows(mm_tn(inner, seed), core, sub)
+    down_leave_ref[...] = leave.astype(low)
+    down_stay_ref[...] = stay.astype(low)
+
+    @pl.when(step == pl.num_programs(0) - 1)
+    def _():
+        block_ref[...] = out_ref[...].astype(low)
+        back = back_ref[...]
+        scale = unit_ref[:, :1]
+        unit = after_ref[...] * scale
+        gained = back * gain_ref[...]
+        mean = jnp.mean(gained * unit, axis=1, keepdims=True)
+        grad_ref[...] = seed_ref[...].astype(f32) + scale * (gained - unit * mean)
+        gain_grad_ref[...] = jnp.sum(back * unit, axis=0, keepdims=True)
+
+
+def feed_forward(core, after_attn, gain, seed, gate, up, down, rows, sub):
+    tokens, width = after_attn.shape
+    ff = gate.shape[1]
+    step = 512
+    chips = width // (2 * rows)
+    f32, low = (jnp.float32, jnp.bfloat16)
+    full = pl.BlockSpec((tokens, width), lambda i, _: (0, 0))
+    line = pl.BlockSpec((1, width), lambda i, _: (0, 0))
+    columns = pl.BlockSpec((width, step), lambda i, _: (0, i))
+    wide = pl.BlockSpec((2, chips, rows, step), lambda i, _: (0, 0, 0, i))
+    tall = pl.BlockSpec((step // (2 * sub), sub, width), lambda i, _: (i, 0, 0))
+    return pl.pallas_call(
+        functools.partial(ffn_kernel, sub),
+        name="feed_forward",
+        cost_estimate=pl.CostEstimate(
+            flops=ff * (12 << 20), bytes_accessed=1 << 20, transcendentals=0
+        ),
+        grid_spec=pltpu.PrefetchScalarGridSpec(
+            num_scalar_prefetch=1,
+            grid=(ff // step,),
+            in_specs=[
+                full,
+                line,
+                full,
+                columns,
+                columns,
+                pl.BlockSpec((step, width), lambda i, _: (i, 0)),
+            ],
+            out_specs=[full, full, line, wide, wide, tall, tall],
+            scratch_shapes=[
+                pltpu.VMEM((tokens, LANES), f32),
+                pltpu.VMEM((tokens, width), low),
+                pltpu.VMEM((width, tokens), low),
+                pltpu.VMEM((tokens, width), f32),
+                pltpu.VMEM((tokens, width), f32),
+            ],
+        ),
+        out_shape=[
+            jax.ShapeDtypeStruct((tokens, width), low),
+            jax.ShapeDtypeStruct((tokens, width), f32),
+            jax.ShapeDtypeStruct((1, width), f32),
+            jax.ShapeDtypeStruct((2, chips, rows, ff), low),
+            jax.ShapeDtypeStruct((2, chips, rows, ff), low),
+            jax.ShapeDtypeStruct((ff // (2 * sub), sub, width), low),
+            jax.ShapeDtypeStruct((ff // (2 * sub), sub, width), low),
+        ],
+        compiler_params=pltpu.CompilerParams(vmem_limit_bytes=58 << 20),
+    )(core, after_attn, gain, seed, gate, up, down)
+
+
+def square_gradient_kernel(
+    core_ref,
+    normed_ref,
+    att_ref,
+    dq_ref,
+    dk_ref,
+    dv_ref,
+    do_ref,
+    qk_leave_ref,
+    qk_stay_ref,
+    vo_leave_ref,
+    vo_stay_ref,
+    normed_t_ref,
+):
+    core = core_ref[0]
+    tokens = att_ref.shape[1]
+
+    @pl.when(pl.program_id(0) == 0)
+    def _():
+        normed_t_ref[...] = jnp.transpose(normed_ref[...])
+
+    normed_t = normed_t_ref[...]
+    own = normed_t_ref[:, pl.ds(pl.multiple_of(core * tokens, tokens), tokens)]
+    grads = (
+        (qk_leave_ref, qk_stay_ref, 0, mm_nt(own, dq_ref[...])),
+        (qk_leave_ref, qk_stay_ref, 1, mm(normed_t, dk_ref[...])),
+        (vo_leave_ref, vo_stay_ref, 0, mm(normed_t, dv_ref[...])),
+        (vo_leave_ref, vo_stay_ref, 1, mm(att_ref[...], do_ref[...])),
+    )
+    for leave_ref, stay_ref, number, grad in grads:
+        leave, stay = part_rows(grad, core, leave_ref.shape[2])
+        leave_ref[number] = leave.astype(jnp.bfloat16)
+        stay_ref[number] = stay.astype(jnp.bfloat16)
+
+
+def square_gradients(core, normed_all, attended_t, grad_q_t, grad_k, grad_v, grad_out, rows):
+    keys, width = normed_all.shape
+    tokens = attended_t.shape[1]
+    step = 256
+    chips = width // (2 * rows)
+    low = jnp.bfloat16
+    block = pl.BlockSpec((2, chips, rows, step), lambda i, _: (0, 0, 0, i))
+    shape = jax.ShapeDtypeStruct((2, chips, rows, width), low)
+    return pl.pallas_call(
+        square_gradient_kernel,
+        name="square_gradients",
+        cost_estimate=pl.CostEstimate(
+            flops=8 << 30, bytes_accessed=1 << 20, transcendentals=0
+        ),
+        grid_spec=pltpu.PrefetchScalarGridSpec(
+            num_scalar_prefetch=1,
+            grid=(width // step,),
+            in_specs=[
+                pl.BlockSpec((keys, width), lambda i, _: (0, 0)),
+                pl.BlockSpec((width, tokens), lambda i, _: (0, 0)),
+                pl.BlockSpec((step, tokens), lambda i, _: (i, 0)),
+                pl.BlockSpec((keys, step), lambda i, _: (0, i)),
+                pl.BlockSpec((keys, step), lambda i, _: (0, i)),
+                pl.BlockSpec((tokens, step), lambda i, _: (0, i)),
+            ],
+            out_specs=[block] * 4,
+            scratch_shapes=[pltpu.VMEM((width, keys), low)],
+        ),
+        out_shape=[shape] * 4,
+        compiler_params=pltpu.CompilerParams(vmem_limit_bytes=48 << 20),
+    )(core, normed_all, attended_t, grad_q_t, grad_k, grad_v, grad_out)
 
 
 def shards(
@@ -850,152 +1237,258 @@
     local_tokens = count * piece_tokens
     key_count = 2 * local_tokens
     low, f32 = (jnp.bfloat16, jnp.float32)
-    order_a, order_b = stage_orders()
+    phases_a, phases_b = stage_phases()
+    along, across_a, across_b = (phases_a[:2], phases_a[2:], phases_b[2:])
     rows = w_query.shape[0]
     vec_rows = KERNEL + 3
-
+    half = 2 * model_width
+    ff = w_gate.shape[1]
+    chain = Chain()
+
+    groups = exchange_groups()
+    pieces = embeddings.reshape(count, local_bytes, model_width)
+    piece_lengths = lengths.reshape(count)
+    square, wide = pack_weights(w_query, w_key, w_value, w_out, w_gate, w_up)
     vectors = jnp.concatenate(
         [conv_weight, scorer[None], gain_attn[None], gain_ffn[None]], axis=0
     )
-    vectors = gather_all(vectors, order_a)
-    vectors = jnp.swapaxes(vectors, 0, 1).reshape(vec_rows, model_width).astype(f32)
+    vectors = exchange(vectors, groups[0])
+    square = Gathering(chain, square, along)
+    bytes_before, bytes_after = neighbour_edges(pieces, 2 * EDGE)
+    for group in groups[1:]:
+        vectors = chain.note(jnp.concatenate(chain.after(*vectors), axis=1))
+        vectors = exchange(vectors, group)
+        if group is groups[1]:
+            square.finish()
+            wide = Gathering(chain, chain.after(wide), along)
+    vectors = chain.note(jnp.concatenate(chain.after(*vectors), axis=1))
+    steps = [step for group in groups for step in group]
+    source = jnp.arange(model_width, dtype=jnp.int32)
+    partner = device ^ sum(
+        ((source // rows >> number) & 1) * (1 << bit if axis == "seq" else seq_count << bit)
+        for number, (axis, bit) in enumerate(steps)
+    )
+    target = partner * rows + source % rows
+    place = target[:, None] == jnp.arange(model_width, dtype=jnp.int32)[None, :]
+    vectors = chain.note(mm(vectors, place.astype(low)))
     gain_one, gain_two = (vectors[KERNEL + 1], vectors[KERNEL + 2])
-
-    pieces = embeddings.reshape(count, local_bytes, model_width)
-    piece_lengths = lengths.reshape(count)
-    bytes_before, bytes_after = neighbour_edges(pieces, 2 * EDGE)
     token_start = seq_index * piece_tokens
     info = jnp.concatenate([token_start.reshape(1).astype(jnp.int32), piece_lengths])
-    both_lengths = swap_bit(piece_lengths, "dp", 0)
-    both_lengths = jnp.where(
-        core == seq_index // count, piece_lengths, both_lengths
-    )
-    seq_length = lax.dynamic_index_in_dim(both_lengths, seq_index % count, 0, keepdims=False)
-
-    sent = pool_forward(info, bytes_before, pieces, bytes_after, vectors)
-    arrived = to_chips(sent).reshape(count, piece_tokens + 2 * EDGE, model_width)
-    normed_low = arrived[:, :piece_tokens].reshape(local_tokens, model_width)
+    square.finish()
+    first = Gathering(chain, square.whole[..., :half], across_a, square.held)
+    second = Gathering(chain, square.whole[..., half:], across_b, square.held)
+    sent = chain.note(
+        pool_forward(info, bytes_before, chain.after(pieces), bytes_after, vectors)
+    )
+    arrived = to_chips(sent)
+    other_lengths = swap_bit(chain.after(piece_lengths), "dp", 0)
+    chain_lengths = jnp.where(core == seq_index // count, piece_lengths, other_lengths)
+    seq_length = lax.dynamic_index_in_dim(chain_lengths, seq_index % count, 0, keepdims=False)
+    first_tile = core * (local_tokens // TILE)
+    first_ref = first_tile.astype(jnp.int32).reshape(1)
+    wide.finish()
+    first.finish()
+    second.finish()
+    seq_length, rel_late = chain.after(seq_length, rel_bias)
+    key_aug, block_rows, far = attn_tables(
+        first_tile, local_tokens, key_count, seq_length, rel_late
+    )
+    bias = chain.note(near_bias(rel_late.T))
+    wide.finish()
+    gate_full = Gathering(chain, wide.whole[..., :ff], across_a, wide.held)
+    up_full = Gathering(chain, wide.whole[..., ff:], across_b, wide.held)
+    arrived = in_token_order(chain.after(*arrived))
+    normed_low = chain.note(arrived[:, :piece_tokens].reshape(local_tokens, model_width))
+    normed_other = swap_bit(normed_low, "dp", 0)
+    tall = Gathering(chain, chain.after(w_down), phases_b)
     scale = arrived[:, piece_tokens : piece_tokens + 2, :piece_tokens].astype(f32)
     scale = jnp.sum(scale, axis=1).reshape(local_tokens, 1)
     unit = normed_low.astype(f32) / gain_one
     hidden_in = unit / scale
-    seed_low = to_chips(cotangent.reshape(count, piece_tokens, model_width))
-    seed_grad = seed_low.astype(f32)
-
-    first = gather_all(jnp.concatenate([w_query, w_key], axis=1), order_a)
-    second = gather_all(jnp.concatenate([w_value, w_out], axis=1), order_b)
-    gate_full = gather_all(w_gate, order_a).reshape(model_width, -1)
-    up_full = gather_all(w_up, order_b).reshape(model_width, -1)
-    down_full = gather_all(w_down, order_a).reshape(-1, model_width)
-    first = first.reshape(model_width, 2 * model_width)
-    second = second.reshape(model_width, 2 * model_width)
+    first.finish()
+    second.finish()
+    tall.finish()
+    normed_other = chain.after(normed_other)
+    normed_all = chain.note(
+        jnp.concatenate(
+            [
+                jnp.where(core == 0, normed_low, normed_other),
+                jnp.where(core == 0, normed_other, normed_low),
+            ],
+            axis=0,
+        )
+    )
+    first = first.finish().reshape(model_width, half)
+    second = second.finish().reshape(model_width, half)
     query_full, key_full = (first[:, :model_width], first[:, model_width:])
     value_full, out_full = (second[:, :model_width], second[:, model_width:])
-
-    normed_other = swap_bit(normed_low, "dp", 0)
-    normed_all = jnp.concatenate(
-        [
-            jnp.where(core == 0, normed_low, normed_other),
-            jnp.where(core == 0, normed_other, normed_low),
-        ],
-        axis=0,
-    )
-
-    first_tile = core * (local_tokens // TILE)
-    key_aug, block_rows, far, bias = attn_tables(
-        first_tile, local_tokens, key_count, seq_length, rel_bias
-    )
-    first_ref = first_tile.astype(jnp.int32).reshape(1)
 
     def project_t(weight, tokens):
         return lax.dot_general(
             weight, tokens, (((0,), (1,)), ((), ())), preferred_element_type=f32
         ).astype(low)
 
-    q_t = project_t(query_full, normed_low)
-    k_t = project_t(key_full, normed_all)
+    tall.finish()
+    q_t = project_t(query_full, chain.after(normed_low))
     v_t = project_t(value_full, normed_all)
-    keys_all = mm(normed_all, key_full).astype(low)
-    values_all = mm(normed_all, value_full).astype(low)
-    attended_t, lse = attn_forward(first_ref, q_t, keys_all, key_aug, v_t, far, bias)
-    after_attn = hidden_in + mm_tn(attended_t, out_full)
-    normed_ffn, ffn_pull = jax.vjp(rms_scale, after_attn, gain_two)
-    normed_ffn_low = normed_ffn.astype(low)
-    gate_value = mm(normed_ffn_low, gate_full)
-    up_value = mm(normed_ffn_low, up_full)
-    inner_act, gelu_pull = jax.vjp(gelu_gate, gate_value, up_value)
-    inner_low = inner_act.astype(low)
-    block_out = (after_attn + mm(inner_low, down_full)).astype(low)
-    blocks_out = from_chips(block_out, count).reshape(
-        num_micro, num_seqs, piece_tokens, model_width
-    )
-
-    down_grad = mm_tn(inner_low, seed_low).astype(low)
-    down_grad = scatter_sum(down_grad.reshape(-1, w_down.shape[0], model_width), order_b)
-    grad_inner = mm_nt(seed_low, down_full)
-    grad_gate, grad_up = gelu_pull(grad_inner)
-    grad_gate_low = grad_gate.astype(low)
-    grad_up_low = grad_up.astype(low)
-    gate_grad = mm_tn(normed_ffn_low, grad_gate_low).astype(low)
-    gate_grad = scatter_sum(gate_grad.reshape(-1, rows, w_gate.shape[1]), order_a)
-    up_grad = mm_tn(normed_ffn_low, grad_up_low).astype(low)
-    up_grad = scatter_sum(up_grad.reshape(-1, rows, w_up.shape[1]), order_b)
-    grad_normed_ffn = mm_nt(grad_gate_low, gate_full) + mm_nt(grad_up_low, up_full)
-    grad_after, gain_ffn_grad = ffn_pull(grad_normed_ffn)
-    grad_after = seed_grad + grad_after
+    keys_all = chain.note(mm(normed_all, key_full).astype(low))
+    gate_full.finish()
+    up_full.finish()
+    tall.finish()
+    seed_pieces = cotangent.reshape(count, piece_tokens, model_width)
+    pairs = model_width // TILE
+    fwd_out = ()
+    for part in range(2):
+        fwd_out = attn_forward(
+            first_ref,
+            chain.after(q_t),
+            keys_all,
+            key_aug,
+            v_t,
+            far,
+            bias,
+            (part * pairs // 2, (part + 1) * pairs // 2),
+            tuple(fwd_out),
+        )
+        chain.note(fwd_out[0])
+        if part == 0:
+            seed_arrived = to_chips(chain.after(seed_pieces))
+    attended_t, lse = fwd_out
+    gate_full.finish()
+    up_full.finish()
+    after_attn = chain.note(hidden_in + mm_tn(chain.after(attended_t), out_full))
+    tall.finish()
+    k_t = chain.note(project_t(key_full, chain.after(normed_all)))
+    values_all = chain.note(mm(chain.after(normed_all), value_full).astype(low))
+    gate_full = gate_full.finish().reshape(model_width, ff)
+    up_full = up_full.finish().reshape(model_width, ff)
+    seed_low = in_token_order(chain.after(*seed_arrived)).reshape(local_tokens, model_width)
+    chain.note(seed_low)
+    down_full = tall.finish().reshape(ff, model_width)
+
+    core_ref = core.astype(jnp.int32).reshape(1)
+    block_out, grad_after, gain_ffn_grad, wide_leave, wide_stay, down_leave, down_stay = (
+        feed_forward(
+            core_ref,
+            chain.after(after_attn),
+            gain_two[None],
+            seed_low,
+            gate_full,
+            up_full,
+            down_full,
+            rows * seq_count,
+            w_down.shape[0] * seq_count,
+        )
+    )
+    chain.note(block_out)
+    down_sum = Reduction(chain, down_leave[None], down_stay[None], w_down.shape[0], phases_b)
+    wide_sum = Reduction(chain, wide_leave, wide_stay, rows, phases_a)
+    blocks_arrived = from_chips(block_out, count)
     grad_after_low = grad_after.astype(low)
-    out_grad = mm(attended_t, grad_after_low).astype(low)
-    out_grad = scatter_sum(out_grad.reshape(-1, rows, model_width), order_a)
-    grad_attended_t = mm_nt(out_full, grad_after_low).astype(low)
-    grad_queries_t, key_terms, value_terms, near, sums = attn_backward(
-        first_ref,
-        q_t,
-        grad_attended_t,
-        attended_t,
-        lse,
-        keys_all,
-        values_all,
-        k_t,
-        key_aug,
-        block_rows,
-        far,
-        bias,
-    )
-    shared = mm_nt(key_terms, key_full) + mm_nt(value_terms, value_full)
-    shared = shared.reshape(2, local_tokens, model_width)
+    grad_attended_t = chain.note(mm_nt(out_full, chain.after(grad_after_low)).astype(low))
+    down_sum.finish()
+    wide_sum.finish()
+    bwd_out = ()
+    for part in range(2):
+        bwd_out = attn_backward(
+            first_ref,
+            q_t,
+            chain.after(grad_attended_t),
+            attended_t,
+            lse,
+            keys_all,
+            values_all,
+            k_t,
+            key_aug,
+            block_rows,
+            far,
+            bias,
+            (part * pairs // 2, (part + 1) * pairs // 2),
+            tuple(bwd_out),
+        )
+        chain.note(bwd_out[0])
+        if part == 0:
+            down_sum.finish()
+            blocks_arrived = chain.after(*blocks_arrived)
+            chain.note(blocks_arrived[0])
+            blocks_out = in_piece_order(blocks_arrived)
+    grad_queries_t, key_terms, value_terms, near, sums = bwd_out
+    shared = mm_nt(chain.after(key_terms), key_full) + mm_nt(value_terms, value_full)
+    shared = chain.note(shared.reshape(2, local_tokens, model_width))
     leaving = lax.dynamic_index_in_dim(shared, 1 - core, 0, keepdims=False).astype(low)
     staying = lax.dynamic_index_in_dim(shared, core, 0, keepdims=False)
+    arrived = swap_bit(leaving, "dp", 0)
+    down_sum.finish()
+    wide_sum.finish()
+    arrived = chain.after(arrived)
     grad_normed = lax.dot_general(
         grad_queries_t, query_full, (((0,), (1,)), ((), ())), preferred_element_type=f32
-    ) + staying + swap_bit(leaving, "dp", 0).astype(f32)
-    query_grad = lax.dot_general(
-        normed_low, grad_queries_t, (((0,), (1,)), ((), ())), preferred_element_type=f32
-    ).astype(low)
-    query_grad = scatter_sum(query_grad.reshape(-1, rows, model_width), order_b)
-    key_grad = mm_tn(normed_all, key_terms).astype(low)
-    key_grad = scatter_sum(key_grad.reshape(-1, rows, model_width), order_a)
-    value_grad = mm_tn(normed_all, value_terms).astype(low)
-    value_grad = scatter_sum(value_grad.reshape(-1, rows, model_width), order_b)
+    ) + (staying + arrived.astype(f32))
     gained = grad_normed * gain_one
-    gain_attn_grad = jnp.sum(grad_normed * unit, axis=0)
     grad_hidden = grad_after + scale * (
         gained - unit * jnp.mean(gained * unit, axis=-1, keepdims=True)
     )
-    grad_pieces = from_chips(grad_hidden.astype(low), count)
+    arrived = from_chips(chain.note(grad_hidden.astype(low)), count)
+    first_leave, first_stay, second_leave, second_stay = square_gradients(
+        core_ref,
+        normed_all,
+        attended_t,
+        grad_queries_t,
+        chain.after(key_terms),
+        value_terms,
+        grad_after_low,
+        rows * seq_count,
+    )
+    chain.note(first_leave)
+    second_sum = Reduction(chain, second_leave, second_stay, rows, phases_b)
+    first_sum = Reduction(chain, first_leave, first_stay, rows, phases_a)
+    second_sum.finish()
+    first_sum.finish()
+    down_sum.finish()
+    bias_terms = chain.note(bias_gradient(first_ref, chain.after(near), sums))
+    gain_attn_grad = chain.note(jnp.sum(chain.after(grad_normed) * unit, axis=0))
+    grad_pieces = chain.note(in_piece_order(chain.after(*arrived)))
     grad_before, grad_after_edge = neighbour_edges(grad_pieces, EDGE)
+    wide_sum.finish()
+    down_grad = down_sum.finish()[0]
+    second_sum.finish()
+    first_sum.finish()
     embed_grad, pool_small = pool_backward(
-        info, bytes_before, pieces, bytes_after, grad_before, grad_pieces, grad_after_edge, vectors
-    )
+        info,
+        bytes_before,
+        pieces,
+        bytes_after,
+        grad_before,
+        chain.after(grad_pieces),
+        grad_after_edge,
+        vectors,
+    )
+    chain.note(pool_small)
     embed_out = embed_grad.reshape(num_micro, num_seqs, local_bytes, model_width)
     pool_small = jnp.sum(pool_small, axis=0)[: KERNEL + 1]
-    bias_terms = bias_gradient(first_tile, near, sums)
     bias_row = jnp.pad(bias_terms.reshape(-1), (0, model_width - bias_terms.size))
     small = jnp.concatenate(
-        [pool_small, gain_attn_grad[None], gain_ffn_grad[None], bias_row[None]],
+        [pool_small, gain_attn_grad[None], gain_ffn_grad, bias_row[None]],
         axis=0,
     )
-    small = sum_all(small, order_a)
-    bias_total = small[vec_rows, : bias_terms.size].reshape(bias_terms.shape)
+    small = exchange(chain.note(small), groups[0])
+    second_sum.finish()
+    first_sum.finish()
+    wide_sum.finish()
+    for group in groups[1:]:
+        small = exchange(chain.note(tree_sum(chain.after(*small))), group)
+        if group is groups[1]:
+            second_sum.finish()
+            first_sum.finish()
+    wide_grad = wide_sum.finish()
+    small = chain.note(tree_sum(chain.after(*small)))
+    gate_grad, up_grad = (wide_grad[0], wide_grad[1])
+    blocks_out = blocks_out.reshape(num_micro, num_seqs, piece_tokens, model_width)
+    second_grad = second_sum.finish()
+    first_grad = first_sum.finish()
+    query_grad, key_grad = (first_grad[0], first_grad[1])
+    value_grad, out_grad = (second_grad[0], second_grad[1])
+    bias_total = small[vec_rows, : bias_terms.size].reshape(bias_terms.shape).T
     own = lax.dynamic_slice_in_dim(small[:vec_rows], device * rows, rows, axis=1)
     return (
         blocks_out,

time: 517 us -> 358 us (0.69)
  waiting for transfers between devices: 188 us -> 47.8 us
  Pallas kernels: 65.1 us -> 109 us
  matrix products: 63.1 us -> 19.5 us
  local copies, waits for them, and re-layouts: 44 us -> 21.5 us
  other arithmetic: 47.6 us -> 54.4 us
    ppermute x73 -> x44, waiting for transfers between devices: 188 us -> 39.4 us  [swap_bit(): return lax.ppermute(x, axis, [(i, i ^ 1 << bit) for i in range(size)])]
    pallas_call x4 -> x11, Pallas kernels: 65.1 us -> 109 us  [the longest x2 25.2 us: attn_backward(): pl.pallas_call(functools.partial(attn_backward_kernel, len(earlier)), nam...]
    ppermute x73 -> x44, starting transfers between devices: 78.1 us -> 57.1 us  [swap_bit(): return lax.ppermute(x, axis, [(i, i ^ 1 << bit) for i in range(size)])]
    ppermute x0 -> x14, starting transfers between devices: none -> 17.2 us  [exchange(): lax.ppermute(x, axis, pairs)]
    dot_general x6 -> x1, matrix products: 16.7 us -> 1.95 us  [mm_tn(): lax.dot_general(a, b, (((0,), (0,)), ((), ())), preferred_element_type=jn...]
    convert_element_type x31 -> x18, other arithmetic: 9.79 us -> 24.4 us  [the longest x16 21.4 us: finish(): (x.astype(f32) + y.astype(f32)).astype(jnp.bfloat16)]
    dynamic_slice x12 -> x1, local copies, waits for them, and re-layouts: 13 us -> 0.59 us  [shards(): lax.dynamic_index_in_dim(chain_lengths, seq_index % count, 0, keepdims=Fa...]
    dot_general x3 -> x0, matrix products: 11.4 us -> none  [the longest x1 5.92 us: bias_gradient(): close = jnp.einsum('hdji,djib->bh', near, near_onehot(), precision=highest)]
  transfers between devices with their start and end apart: 85 -> 70, of which waited for: 45 -> 19; matrix products, arithmetic and copies ran while one was open for 20% -> 24% of each run, Pallas kernels for 8% -> 22%
where the time goes in v2:
time: 358 us; the launch traced here: 353 us
  Pallas kernels  109 us (30%)
  starting transfers between devices  99.1 us (28%)
  other arithmetic  54.4 us (15%)
  waiting for transfers between devices  47.8 us (13%)
  local copies, waits for them, and re-layouts  21.5 us (6%)
  matrix products  19.5 us (5%)
    ppermute x44, starting transfers between devices, swap_bit(): return lax.ppermute(x, axis, [(i, i ^ 1 << bit) for i in range(size)])  57.1 us
    ppermute x44, waiting for transfers between devices, swap_bit(): return lax.ppermute(x, axis, [(i, i ^ 1 << bit) for i in range(size)])  39.4 us
    pallas_call x2, Pallas kernels, attn_backward(): pl.pallas_call(functools.partial(attn_backward_kernel, len(earlier)), nam...  25.2 us
    pallas_call x1, Pallas kernels, feed_forward(): pl.pallas_call(functools.partial(ffn_kernel, sub), name='feed_forward', c...  23 us
    convert_element_type x16, other arithmetic, finish(): (x.astype(f32) + y.astype(f32)).astype(jnp.bfloat16)  21.4 us
    pallas_call x1, Pallas kernels, pool_backward(): pl.pallas_call(pool_backward_kernel, name='pool_backward', cost_estimate=...  19.9 us
    ppermute x14, starting transfers between devices, exchange(): lax.ppermute(x, axis, pairs)  17.2 us
    pallas_call x2, Pallas kernels, attn_forward(): pl.pallas_call(functools.partial(attn_forward_kernel, len(earlier)), name...  15.5 us
  transfers between devices with their start and end apart: 70, of which 19 were waited for; matrix products, arithmetic and copies ran while one was open for 24% of the time, Pallas kernels for 22%

profile of v2, /device:TPU:0, one launch (start us, length us, event | category | flops | bytes accessed | tf_op | source)
XLA Modules:
  0.0 353.3 jit_solution(9933820782779293706)
XLA Ops:
  3.8 3.6 %collective-permute-start.1 = (bf16[24,3072]{1,0:T(8,128)(2,1)}, bf16[24,3072]{1,0:T(8,128)(2,1)S(1)}, u32[]{:S(2)}, u32[]{:S(2)}) collective-permute-start(bf16[24,3072]{1,0:T(8,128)(2,1)} %get-tuple-element.177), channel_id=1, source_target_pairs={{0,2},{1,3},{2,0},{3,1},{4,6},{5,7},{6,4},{7,5},{8,10},{9,11},{10,... | collective-permute-start | bytes 442376 | tf_op jit(solution)/shard_map/ppermute | solution.py:458
  8.2 3.5 collective-permute-start
  34.6 7.9 %pool_forward.1 = bf16[2,272,768]{2,1,0:T(8,128)(2,1)S(1)} custom-call(s32[3]{0:T(128)S(1)} %pad_add_fusion.info_ref, bf16[2,16,768]{2,1,0:T(8,128)(2,1)S(1)} %collective-permute-done.before_ref, bf16[2,512,768]{2,1,0:T(8,128)(2,1)S(1)} %bitcast.261, bf16[2,16,768]{2,1,0:T(8,128)(2,1)S(1)} %collective-permute-done.10.after_ref, f32[8,768]{1,0:T(8,128)S(1)} %fusion.vec_ref), custom_call_target="tpu_custom_call" | custom-call | flops 8589934592 | bytes 1048576 | tf_op jit(solution)/shard_map/pool_forward/pallas_call | solution.py:236
  52.8 10.2 %collective-permute-start.20 = (bf16[512,768]{1,0:T(8,128)(2,1)S(1)}, bf16[512,768]{1,0:T(8,128)(2,1)S(1)}, u32[]{:S(2)}, u32[]{:S(2)}) collective-permute-start(bf16[512,768]{1,0:T(8,128)(2,1)S(1)} %bitcast.262), channel_id=1, source_target_pairs={{0,4},{4,0},{8,12},{12,8},{16,20},{20,16},{24,28},{28,24},{1,5},{5... | collective-permute-start | bytes 2359304 | tf_op jit(solution)/shard_map/ppermute | solution.py:458
  63.1 5.0 %collective-permute-start.21 = (bf16[64,768]{1,0:T(8,128)(2,1)}, bf16[64,768]{1,0:T(8,128)(2,1)}, u32[]{:S(2)}, u32[]{:S(2)}) collective-permute-start(bf16[64,768]{1,0:T(8,128)(2,1)} %param.29), channel_id=1, source_target_pairs={{0,2},{1,3},{2,0},{3,1},{4,6},{5,7},{6,4},{7,5},{8,10},{9,11},{10,... | collective-permute-start | bytes 294920 | tf_op jit(solution)/shard_map/ppermute | solution.py:458
  76.4 8.0 %collective-permute-done.18 = bf16[2,2,2,24,1536]{4,3,1,2,0:T(8,128)(2,1)} collective-permute-done((bf16[2,2,2,24,1536]{4,3,1,2,0:T(8,128)(2,1)S(1)}, bf16[2,2,2,24,1536]{4,3,1,2,0:T(8,128)(2,1)}, u32[]{:S(2)}, u32[]{:S(2)}) %collective-permute-start.18) | collective-permute-done | bytes 589856 | tf_op jit(solution)/shard_map/ppermute | solution.py:458
  101.6 6.9 %collective-permute-done.25 = bf16[2,2,64,768]{3,2,0,1:T(8,128)(2,1)S(1)} collective-permute-done((bf16[2,2,64,768]{3,2,0,1:T(8,128)(2,1)S(1)}, bf16[2,2,64,768]{3,2,0,1:T(8,128)(2,1)S(1)}, u32[]{:S(2)}, u32[]{:S(2)}) %collective-permute-start.25) | collective-permute-done | bytes 393248 | tf_op jit(solution)/shard_map/ppermute | solution.py:458
  109.2 7.8 %attn_forward.2 = (bf16[768,512]{1,0:T(8,128)(2,1)S(1)}, f32[6,2,512]{2,1,0:T(2,128)S(1)}) custom-call(s32[1]{0:T(128)} %bitcast.26.first_ref, bf16[768,512]{1,0:T(8,128)(2,1)S(1)} %convolution_convert_fusion.5.q_ref, bf16[1024,768]{1,0:T(8,128)(2,1)S(1)} %convolution_convert_fusion.3.k_ref, bf16[1024,128]{1,0:T(8,128)(2,1)S(1)} %select_convert_fusion.ka_ref, ...), custom_call_target="tpu_custom_call" | custom-call | flops 8053063680 | bytes 1048576 | tf_op jit(solution)/shard_map/attn_forward/pallas_call | solution.py:724
  120.1 7.7 %attn_forward.3 = (bf16[768,512]{1,0:T(8,128)(2,1)S(1)}, f32[6,2,512]{2,1,0:T(2,128)S(1)}) custom-call(s32[1]{0:T(128)} %bitcast.26.first_ref, bf16[768,512]{1,0:T(8,128)(2,1)S(1)} %convolution_convert_fusion.5.q_ref, bf16[1024,768]{1,0:T(8,128)(2,1)S(1)} %convolution_convert_fusion.3.k_ref, ...), custom_call_target="tpu_custom_call", output_to_operand_aliasing={{0}: (7, {}), {1}: (8, {})} | custom-call | flops 8053063680 | bytes 1048576 | tf_op jit(solution)/shard_map/attn_forward/pallas_call | solution.py:724
  150.4 23.0 %feed_forward.1 = (bf16[512,768]{1,0:T(8,128)(2,1)}, f32[512,768]{1,0:T(8,128)}, f32[1,768]{1,0:T(1,128)}, bf16[2,4,96,2048]{3,2,1,0:T(8,128)(2,1)}, bf16[2,4,96...) custom-call(s32[1]{0:T(128)} %bitcast.core_ref, f32[512,768]{1,0:T(8,128)} %fusion.1.after_ref, ...), custom_call_target="tpu_custom_call" | custom-call | flops 25769803776 | bytes 1048576 | tf_op jit(solution)/shard_map/feed_forward/pallas_call | solution.py:1105
  177.0 4.5 %collective-permute-start.36 = (bf16[256,768]{1,0:T(8,128)(2,1)}, bf16[256,768]{1,0:T(8,128)(2,1)}, u32[]{:S(2)}, u32[]{:S(2)}) collective-permute-start(bf16[256,768]{1,0:T(8,128)(2,1)} %get-tuple-element.427), channel_id=1, source_target_pairs={{0,0},{1,1},{4,2},{5,3},{2,4},{3,5},{6,6},{7,7},{8,8},{9,9},{12,10... | collective-permute-start | bytes 1179656 | tf_op jit(solution)/shard_map/ppermute | solution.py:627
  186.2 4.4 %fusion.3 = (bf16[2,2,2,2,24,2048]{5,4,0,2,3,1:T(8,128)(2,1)S(1)}, bf16[2,2,2,2,24,2048]{5,4,0,2,3,1:T(8,128)(2,1)}) fusion(s32[]{:T(128)S(6)} %select_n.651, s32[]{:T(128)S(6)} %select_n.643, bf16[2,2,2,2,2,24,2048]{6,5,4,3,2,1,0:T(8,128)(2,1)S(1)} %bitcast.272, bf16[2,2,2,2,2,24,2048]{6,5,4,3,2,1,0:T(8,128)(2,1)} %bitcast.78), kind=kLoop, calls=%fused_computation.18 | loop fusion | flops 6291456 | bytes 9437192 | tf_op jit(solution)/shard_map/convert_element_type | solution.py:538
  192.1 12.6 %attn_backward.2 = (bf16[768,512]{1,0:T(8,128)(2,1)}, bf16[1024,768]{1,0:T(8,128)(2,1)}, bf16[1024,768]{1,0:T(8,128)(2,1)}, f32[12,3,128,128]{3,2,1,0:T(8,128)}, f32[6,2,16,512]{3,2,1,0:T(8,128)}) custom-call(s32[1]{0:T(128)} %bitcast.26.first_ref, bf16[768,512]{1,0:T(8,128)(2,1)} %copy-done.9, bf16[768,512]{1,0:T(8,128)(2,1)} %convolution_convert_fusion.4.do_ref, ...), custom_call_target="tpu_custom_call" | custom-call | flops 14495514624 | bytes 1048576 | tf_op jit(solution)/shard_map/attn_backward/pallas_call | solution.py:846
  205.7 12.6 %attn_backward.3 = (bf16[768,512]{1,0:T(8,128)(2,1)}, bf16[1024,768]{1,0:T(8,128)(2,1)}, bf16[1024,768]{1,0:T(8,128)(2,1)}, f32[12,3,128,128]{3,2,1,0:T(8,128)}, f32[6,2,16,512]{3,2,1,0:T(8,128)}) custom-call(s32[1]{0:T(128)} %bitcast.26.first_ref, ...), custom_call_target="tpu_custom_call", output_to_operand_aliasing={{0}: (12, {}), {1}: (13, {}), {2}: (14, {}), {3}: (15, {}),... | custom-call | flops 14495514624 | bytes 1048576 | tf_op jit(solution)/shard_map/attn_backward/pallas_call | solution.py:846
  228.0 9.2 %collective-permute-done.43 = bf16[1,2,2,64,768]{4,3,1,2,0:T(8,128)(2,1)} collective-permute-done((bf16[1,2,2,64,768]{4,3,1,2,0:T(8,128)(2,1)}, bf16[1,2,2,64,768]{4,3,1,2,0:T(8,128)(2,1)}, u32[]{:S(2)}, u32[]{:S(2)}) %collective-permute-start.43) | collective-permute-done | bytes 393248 | tf_op jit(solution)/shard_map/ppermute | solution.py:458
  238.3 3.3 fusion.23
  245.7 7.9 %square_gradients.1 = (bf16[2,4,96,768]{3,2,1,0:T(8,128)(2,1)S(1)}, bf16[2,4,96,768]{3,2,1,0:T(8,128)(2,1)S(1)}, bf16[2,4,96,768]{3,2,1,0:T(8,128)(2,1)}, bf16[2,4,96,768]{3,2,1,0:T(8,128)(2,1)}) custom-call(s32[1]{0:T(128)} %bitcast.core_ref, bf16[1024,768]{1,0:T(8,128)(2,1)} %copy-done.30, bf16[768,512]{1,0:T(8,128)(2,1)S(1)} %copy-done.12, ...), custom_call_target="tpu_custom_call" | custom-call | flops 8589934592 | bytes 1048576 | tf_op jit(solution)/shard_map/square_gradients/pallas_call | solution.py:1187
  258.0 4.5 %collective-permute-start.44 = (bf16[256,768]{1,0:T(8,128)(2,1)}, bf16[256,768]{1,0:T(8,128)(2,1)}, u32[]{:S(2)}, u32[]{:S(2)}) collective-permute-start(bf16[256,768]{1,0:T(8,128)(2,1)} %get-tuple-element.423), channel_id=1, source_target_pairs={{0,0},{1,1},{4,2},{5,3},{2,4},{3,5},{6,6},{7,7},{8,8},{9,9},{12,10... | collective-permute-start | bytes 1179656 | tf_op jit(solution)/shard_map/ppermute | solution.py:627
  270.6 4.6 %bias_gradient.1 = f32[12,32]{1,0:T(8,128)} custom-call(s32[1]{0:T(128)} %bitcast.26.first_ref, f32[12,3,128,128]{3,2,1,0:T(8,128)} %get-tuple-element.293.near_ref, f32[6,2,16,512]{3,2,1,0:T(8,128)} %get-tuple-element.294.sums_ref), custom_call_target="tpu_custom_call" | custom-call | flops 4294967296 | bytes 1048576 | tf_op jit(solution)/shard_map/bias_gradient/pallas_call | solution.py:997
  281.2 4.1 %collective-permute-start.49 = (bf16[2,8,768]{2,1,0:T(8,128)(2,1)}, bf16[2,8,768]{2,1,0:T(8,128)(2,1)}, u32[]{:S(2)}, u32[]{:S(2)}) collective-permute-start(bf16[2,8,768]{2,1,0:T(8,128)(2,1)} %get-tuple-element.417), channel_id=1, source_target_pairs={{0,1},{1,2},{2,3},{4,5},{5,6},{6,7},{8,9},{9,10},{10,11},{12,13},{... | collective-permute-start | bytes 73736 | tf_op jit(solution)/shard_map/ppermute | solution.py:25
  289.9 7.3 %collective-permute-start.56 = (bf16[2,2,24,2048]{3,2,0,1:T(8,128)(2,1)}, bf16[2,2,24,2048]{3,2,0,1:T(8,128)(2,1)}, u32[]{:S(2)}, u32[]{:S(2)}) collective-permute-start(bf16[2,2,24,2048]{3,2,0,1:T(8,128)(2,1)} %get-tuple-element.389), channel_id=1, source_target_pairs={{0,1},{1,0},{2,3},{3,2},{4,5},{5,4},{6,7},{7,6},{8,9},{9,8},{10,11... | collective-permute-start | bytes 1179656 | tf_op jit(solution)/shard_map/ppermute | solution.py:458
  302.9 19.9 %pool_backward.1 = (f32[2,512,768]{2,1,0:T(8,128)}, f32[2,8,768]{2,1,0:T(8,128)}) custom-call(s32[3]{0:T(128)} %copy-done.6, bf16[2,16,768]{2,1,0:T(8,128)(2,1)} %copy-done.4, bf16[2,512,768]{2,1,0:T(8,128)(2,1)} %bitcast.260, bf16[2,16,768]{2,1,0:T(8,128)(2,1)} %copy-done.5, bf16[2,8,768]{2,1,0:T(8,128)(2,1)} %collective-permute-done.49.grad_before_ref, ...), custom_call_target="tpu_custom_call" | custom-call | flops 21474836480 | bytes 1048576 | tf_op jit(solution)/shard_map/pool_backward/pallas_call | solution.py:396
  334.5 3.4 collective-permute-start.65
  340.0 7.1 %collective-permute-done.67 = bf16[2,24,2048]{2,1,0:T(8,128)(2,1)S(1)} collective-permute-done((bf16[2,24,2048]{2,1,0:T(8,128)(2,1)S(1)}, bf16[2,24,2048]{2,1,0:T(8,128)(2,1)S(1)}, u32[]{:S(2)}, u32[]{:S(2)}) %collective-permute-start.67) | collective-permute-done | bytes 196640 | tf_op jit(solution)/shard_map/ppermute | solution.py:458
  (366 shorter events, 162.4 us)
Async XLA Ops:
  8.2 26.4 %collective-permute-start = (bf16[2,16,768]{2,1,0:T(8,128)(2,1)S(1)}, bf16[2,16,768]{2,1,0:T(8,128)(2,1)S(1)}, u32[]{:S(2)}, u32[]{:S(2)}) collective-permute-start(bf16[2,16,768]{2,1,0:T(8,128)(2,1)S(1)} %get-tuple-element.401), channel_id=1, source_target_pairs={{0,1},{1,2},{2,3},{4,5},{5,6},{6,7},{8,9},{9,10},{10,11},{12,13},{... | collective-permute-start | bytes 147464 | tf_op jit(solution)/shard_map/ppermute | solution.py:25
  11.7 22.9 %collective-permute-start.10 = (bf16[2,16,768]{2,1,0:T(8,128)(2,1)S(1)}, bf16[2,16,768]{2,1,0:T(8,128)(2,1)S(1)}, u32[]{:S(2)}, u32[]{:S(2)}) collective-permute-start(bf16[2,16,768]{2,1,0:T(8,128)(2,1)S(1)} %get-tuple-element.400), channel_id=1, source_target_pairs={{1,0},{2,1},{3,2},{5,4},{6,5},{7,6},{9,8},{10,9},{11,10},{13,12},{... | collective-permute-start | bytes 147464 | tf_op jit(solution)/shard_map/ppermute | solution.py:26
  48.6 20.1 %collective-permute-start.17 = (bf16[2,2,24,1536]{3,2,0,1:T(8,128)(2,1)S(1)}, bf16[2,2,24,1536]{3,2,0,1:T(8,128)(2,1)S(1)}, u32[]{:S(2)}, u32[]{:S(2)}) collective-permute-start(bf16[2,2,24,1536]{3,2,0,1:T(8,128)(2,1)S(1)} %get-tuple-element.195), channel_id=1, source_target_pairs={{0,16},{4,20},{8,24},{12,28},{16,0},{20,4},{24,8},{28,12},{1,17},{... | collective-permute-start | bytes 884744 | tf_op jit(solution)/shard_map/ppermute | solution.py:458
  49.2 24.0 %collective-permute-start.14 = (bf16[2,24,4096]{2,1,0:T(8,128)(2,1)S(1)}, bf16[2,24,4096]{2,1,0:T(8,128)(2,1)S(1)}, u32[]{:S(2)}, u32[]{:S(2)}) collective-permute-start(bf16[2,24,4096]{2,1,0:T(8,128)(2,1)S(1)} %pad_maximum_fusion.20), channel_id=1, source_target_pairs={{0,1},{1,0},{2,3},{3,2},{4,5},{5,4},{6,7},{7,6},{8,9},{9,8},{10,11... | collective-permute-start | bytes 1179656 | tf_op jit(solution)/shard_map/ppermute | solution.py:458
  49.9 19.5 %collective-permute-start.16 = (bf16[2,2,24,1536]{3,2,0,1:T(8,128)(2,1)S(1)}, bf16[2,2,24,1536]{3,2,0,1:T(8,128)(2,1)S(1)}, u32[]{:S(2)}, u32[]{:S(2)}) collective-permute-start(bf16[2,2,24,1536]{3,2,0,1:T(8,128)(2,1)S(1)} %get-tuple-element.197), channel_id=1, source_target_pairs={{0,8},{4,12},{8,0},{12,4},{16,24},{20,28},{24,16},{28,20},{1,9},{5... | collective-permute-start | bytes 884744 | tf_op jit(solution)/shard_map/ppermute | solution.py:458
  52.8 36.2 %collective-permute-start.20 = (bf16[512,768]{1,0:T(8,128)(2,1)S(1)}, bf16[512,768]{1,0:T(8,128)(2,1)S(1)}, u32[]{:S(2)}, u32[]{:S(2)}) collective-permute-start(bf16[512,768]{1,0:T(8,128)(2,1)S(1)} %bitcast.262), channel_id=1, source_target_pairs={{0,4},{4,0},{8,12},{12,8},{16,20},{20,16},{24,28},{28,24},{1,5},{5... | collective-permute-start | bytes 2359304 | tf_op jit(solution)/shard_map/ppermute | solution.py:458
  63.1 24.4 %collective-permute-start.21 = (bf16[64,768]{1,0:T(8,128)(2,1)}, bf16[64,768]{1,0:T(8,128)(2,1)}, u32[]{:S(2)}, u32[]{:S(2)}) collective-permute-start(bf16[64,768]{1,0:T(8,128)(2,1)} %param.29), channel_id=1, source_target_pairs={{0,2},{1,3},{2,0},{3,1},{4,6},{5,7},{6,4},{7,5},{8,10},{9,11},{10,... | collective-permute-start | bytes 294920 | tf_op jit(solution)/shard_map/ppermute | solution.py:458
  73.4 19.7 %collective-permute-start.27 = (bf16[2,2,24,2048]{3,2,0,1:T(8,128)(2,1)S(1)}, bf16[2,2,24,2048]{3,2,0,1:T(8,128)(2,1)S(1)}, u32[]{:S(2)}, u32[]{:S(2)}) collective-permute-start(bf16[2,2,24,2048]{3,2,0,1:T(8,128)(2,1)S(1)} %get-tuple-element.219), channel_id=1, source_target_pairs={{0,16},{4,20},{8,24},{12,28},{16,0},{20,4},{24,8},{28,12},{1,17},{... | collective-permute-start | bytes 1179656 | tf_op jit(solution)/shard_map/ppermute | solution.py:458
  98.0 29.8 %collective-permute-start.29 = (bf16[2,2,2,24,2048]{4,3,1,2,0:T(8,128)(2,1)S(1)}, bf16[2,2,2,24,2048]{4,3,1,2,0:T(8,128)(2,1)}, u32[]{:S(2)}, u32[]{:S(2)}) collective-permute-start(bf16[2,2,2,24,2048]{4,3,1,2,0:T(8,128)(2,1)S(1)} %pad_maximum_fusion.13), channel_id=1, source_target_pairs={{0,8},{4,12},{8,0},{12,4},{16,24},{20,28},{24,16},{28,20},{1,9},{5... | collective-permute-start | bytes 2359304 | tf_op jit(solution)/shard_map/ppermute | solution.py:458
  99.6 30.6 %collective-permute-start.28 = (bf16[2,2,2,24,2048]{4,3,1,2,0:T(8,128)(2,1)S(1)}, bf16[2,2,2,24,2048]{4,3,1,2,0:T(8,128)(2,1)}, u32[]{:S(2)}, u32[]{:S(2)}) collective-permute-start(bf16[2,2,2,24,2048]{4,3,1,2,0:T(8,128)(2,1)S(1)} %pad_maximum_fusion.14), channel_id=1, source_target_pairs={{0,16},{4,20},{8,24},{12,28},{16,0},{20,4},{24,8},{28,12},{1,17},{... | collective-permute-start | bytes 2359304 | tf_op jit(solution)/shard_map/ppermute | solution.py:458
  108.7 26.0 %collective-permute-start.30 = (bf16[2,2,2,64,768]{4,3,1,2,0:T(8,128)(2,1)S(1)}, bf16[2,2,2,64,768]{4,3,1,2,0:T(8,128)(2,1)}, u32[]{:S(2)}, u32[]{:S(2)}) collective-permute-start(bf16[2,2,2,64,768]{4,3,1,2,0:T(8,128)(2,1)S(1)} %pad_maximum_fusion.15), channel_id=1, source_target_pairs={{0,16},{4,20},{8,24},{12,28},{16,0},{20,4},{24,8},{28,12},{1,17},{... | collective-permute-start | bytes 2359304 | tf_op jit(solution)/shard_map/ppermute | solution.py:458
  117.9 28.7 %collective-permute-start.32 = (bf16[256,768]{1,0:T(8,128)(2,1)}, bf16[256,768]{1,0:T(8,128)(2,1)S(1)}, u32[]{:S(2)}, u32[]{:S(2)}) collective-permute-start(bf16[256,768]{1,0:T(8,128)(2,1)} %get-tuple-element.431), channel_id=1, source_target_pairs={{0,0},{1,1},{2,4},{3,5},{4,2},{5,3},{6,6},{7,7},{8,8},{9,9},{10,12... | collective-permute-start | bytes 1179656 | tf_op jit(solution)/shard_map/ppermute | solution.py:603
  119.7 26.9 %collective-permute-start.33 = (bf16[256,768]{1,0:T(8,128)(2,1)S(1)}, bf16[256,768]{1,0:T(8,128)(2,1)S(1)}, u32[]{:S(2)}, u32[]{:S(2)}) collective-permute-start(bf16[256,768]{1,0:T(8,128)(2,1)S(1)} %get-tuple-element.430), channel_id=1, source_target_pairs={{0,1},{1,0},{2,5},{3,4},{4,3},{5,2},{6,7},{7,6},{8,9},{9,8},{10,13... | collective-permute-start | bytes 1179656 | tf_op jit(solution)/shard_map/ppermute | solution.py:603
  177.0 28.7 %collective-permute-start.36 = (bf16[256,768]{1,0:T(8,128)(2,1)}, bf16[256,768]{1,0:T(8,128)(2,1)}, u32[]{:S(2)}, u32[]{:S(2)}) collective-permute-start(bf16[256,768]{1,0:T(8,128)(2,1)} %get-tuple-element.427), channel_id=1, source_target_pairs={{0,0},{1,1},{4,2},{5,3},{2,4},{3,5},{6,6},{7,7},{8,8},{9,9},{12,10... | collective-permute-start | bytes 1179656 | tf_op jit(solution)/shard_map/ppermute | solution.py:627
  181.5 24.2 %collective-permute-start.37 = (bf16[256,768]{1,0:T(8,128)(2,1)S(1)}, bf16[256,768]{1,0:T(8,128)(2,1)}, u32[]{:S(2)}, u32[]{:S(2)}) collective-permute-start(bf16[256,768]{1,0:T(8,128)(2,1)S(1)} %get-tuple-element.426), channel_id=1, source_target_pairs={{1,0},{0,1},{5,2},{4,3},{3,4},{2,5},{7,6},{6,7},{9,8},{8,9},{13,10... | collective-permute-start | bytes 1179656 | tf_op jit(solution)/shard_map/ppermute | solution.py:627
  184.6 20.1 %collective-permute-start.39 = (bf16[1,2,2,2,64,768]{5,4,2,3,1,0:T(8,128)(2,1)S(1)}, bf16[1,2,2,2,64,768]{5,4,2,3,1,0:T(8,128)(2,1)S(1)}, u32[]{:S(2)}, u32[]{:S(2)}) collective-permute-start(bf16[1,2,2,2,64,768]{5,4,2,3,1,0:T(8,128)(2,1)S(1)} %get-tuple-element.373), channel_id=1, source_target_pairs={{0,16},{4,20},{8,24},{12,28},{16,0},{20,4},{24,8},{28,12},{1,17},{... | collective-permute-start | bytes 2359304 | tf_op jit(solution)/shard_map/ppermute | solution.py:458
  190.6 47.7 %collective-permute-start.42 = (bf16[2,2,2,2,24,2048]{5,4,0,2,3,1:T(8,128)(2,1)}, bf16[2,2,2,2,24,2048]{5,4,0,2,3,1:T(8,128)(2,1)}, u32[]{:S(2)}, u32[]{:S(2)}) collective-permute-start(bf16[2,2,2,2,24,2048]{5,4,0,2,3,1:T(8,128)(2,1)} %get-tuple-element.369), channel_id=1, source_target_pairs={{0,8},{4,12},{8,0},{12,4},{16,24},{20,28},{24,16},{28,20},{1,9},{5... | collective-permute-start | bytes 4718600 | tf_op jit(solution)/shard_map/ppermute | solution.py:458
  255.0 26.3 %collective-permute-start.53 = (bf16[2,2,2,24,2048]{4,3,0,1,2:T(8,128)(2,1)}, bf16[2,2,2,24,2048]{4,3,0,1,2:T(8,128)(2,1)}, u32[]{:S(2)}, u32[]{:S(2)}) collective-permute-start(bf16[2,2,2,24,2048]{4,3,0,1,2:T(8,128)(2,1)} %get-tuple-element.371), channel_id=1, source_target_pairs={{0,16},{4,20},{8,24},{12,28},{16,0},{20,4},{24,8},{28,12},{1,17},{... | collective-permute-start | bytes 2359304 | tf_op jit(solution)/shard_map/ppermute | solution.py:458
  266.7 32.1 %collective-permute-start.51 = (bf16[2,2,2,2,24,768]{5,4,0,2,3,1:T(8,128)(2,1)}, bf16[2,2,2,2,24,768]{5,4,0,2,3,1:T(8,128)(2,1)}, u32[]{:S(2)}, u32[]{:S(2)}) collective-permute-start(bf16[2,2,2,2,24,768]{5,4,0,2,3,1:T(8,128)(2,1)} %get-tuple-element.381), channel_id=1, source_target_pairs={{0,16},{4,20},{8,24},{12,28},{16,0},{20,4},{24,8},{28,12},{1,17},{... | collective-permute-start | bytes 1769480 | tf_op jit(solution)/shard_map/ppermute | solution.py:458
  276.2 25.9 %collective-permute-start.50 = (bf16[2,2,2,2,24,768]{5,4,0,2,3,1:T(8,128)(2,1)S(1)}, bf16[2,2,2,2,24,768]{5,4,0,2,3,1:T(8,128)(2,1)S(1)}, u32[]{:S(2)}, u32[]{:S(2)}) collective-permute-start(bf16[2,2,2,2,24,768]{5,4,0,2,3,1:T(8,128)(2,1)S(1)} %copy-done.35), channel_id=1, source_target_pairs={{0,8},{4,12},{8,0},{12,4},{16,24},{20,28},{24,16},{28,20},{1,9},{5... | collective-permute-start | bytes 1769480 | tf_op jit(solution)/shard_map/ppermute | solution.py:458
  281.2 21.7 %collective-permute-start.49 = (bf16[2,8,768]{2,1,0:T(8,128)(2,1)}, bf16[2,8,768]{2,1,0:T(8,128)(2,1)}, u32[]{:S(2)}, u32[]{:S(2)}) collective-permute-start(bf16[2,8,768]{2,1,0:T(8,128)(2,1)} %get-tuple-element.417), channel_id=1, source_target_pairs={{0,1},{1,2},{2,3},{4,5},{5,6},{6,7},{8,9},{9,10},{10,11},{12,13},{... | collective-permute-start | bytes 73736 | tf_op jit(solution)/shard_map/ppermute | solution.py:25
  289.9 36.2 %collective-permute-start.56 = (bf16[2,2,24,2048]{3,2,0,1:T(8,128)(2,1)}, bf16[2,2,24,2048]{3,2,0,1:T(8,128)(2,1)}, u32[]{:S(2)}, u32[]{:S(2)}) collective-permute-start(bf16[2,2,24,2048]{3,2,0,1:T(8,128)(2,1)} %get-tuple-element.389), channel_id=1, source_target_pairs={{0,1},{1,0},{2,3},{3,2},{4,5},{5,4},{6,7},{7,6},{8,9},{9,8},{10,11... | collective-permute-start | bytes 1179656 | tf_op jit(solution)/shard_map/ppermute | solution.py:458
  300.7 23.1 %collective-permute-start.58 = (bf16[2,2,2,24,768]{4,3,0,1,2:T(8,128)(2,1)}, bf16[2,2,2,24,768]{4,3,0,1,2:T(8,128)(2,1)S(1)}, u32[]{:S(2)}, u32[]{:S(2)}) collective-permute-start(bf16[2,2,2,24,768]{4,3,0,1,2:T(8,128)(2,1)} %get-tuple-element.403), channel_id=1, source_target_pairs={{0,8},{4,12},{8,0},{12,4},{16,24},{20,28},{24,16},{28,20},{1,9},{5... | collective-permute-start | bytes 884744 | tf_op jit(solution)/shard_map/ppermute | solution.py:458
  302.3 21.6 %collective-permute-start.57 = (bf16[2,2,2,24,768]{4,3,0,1,2:T(8,128)(2,1)S(1)}, bf16[2,2,2,24,768]{4,3,0,1,2:T(8,128)(2,1)S(1)}, u32[]{:S(2)}, u32[]{:S(2)}) collective-permute-start(bf16[2,2,2,24,768]{4,3,0,1,2:T(8,128)(2,1)S(1)} %get-tuple-element.405), channel_id=1, source_target_pairs={{0,16},{4,20},{8,24},{12,28},{16,0},{20,4},{24,8},{28,12},{1,17},{... | collective-permute-start | bytes 884744 | tf_op jit(solution)/shard_map/ppermute | solution.py:458
  (96 other events, 1113.3 us)
